TPU v7x, 256 devices: a whole 4x4x8 slice. The times are simulated.
256 devices in a mesh: row: 16 (over z, core), col: 16 (over x, y).
Axes of the slice: x: 4, y: 4, z: 8, core: 2. Of those that a mesh axis runs over, the one named last changes fastest.
Arguments:
- tile_values: float32 [12288, 32, 1024], P(('row', 'col')), may hold values from -6 to 6
- tile_count: int32 [256], P(('row', 'col')), may hold values from 1 to 48, as said below
- mode1_column: int32 [12288, 1], P(('row', 'col')), may hold values from 0 to 15; in each aligned block of 48 rows (0 to 47, 48 to 95, ...) at most 4 rows name the same one
- mode1_offset: int32 [12288], P(('row', 'col')), may hold values from 0 to 15
- mode2_row: int32 [12288, 1], P(('row', 'col')), may hold values from 0 to 15; in each aligned block of 48 rows (0 to 47, 48 to 95, ...) at most 4 rows name the same one
- mode2_offset: int32 [12288], P(('row', 'col')), may hold values from 0 to 7
- mode3_offset: int32 [12288], P(('row', 'col')), may hold values from 0 to 15
- mode2_factor: float32 [65536, 256], P(('row', 'col'))
- mode3_factor: float32 [8192, 256], P('col')
Outputs:
- updated: float32 [131072, 256], P(('row', 'col'))
Inputs may be any that keep to these rules, and one draw needn't show every extreme that they name: Device d's live tiles fill its first tile_count[d] slots; other slots are ignored. Some device holds 48 live tiles. `mode1_column`: at most 4 slots of one device name the same value, and some device reaches it. `mode2_row`: at most 4 slots of one device name the same value, and some device reaches it.
All inputs are finite; a program needn't handle non-finite values.
Results may differ from a plain program's by a relative error of at most 0.0003.
Values sent between devices are 32-bit elements; how exact they have to be, the bound alone decides.
No kernel may reach another device: no remote copies, remote signals or barrier semaphores. Data moves between devices by JAX's collectives and lax.ppermute only.
A program may use at most 128 MiB of HBM per device.

v0:
```python
import jax
import jax.numpy as jnp
from jax import lax
from jax.sharding import PartitionSpec as P

IB_DEV = 16


HIGHEST_PRECISION = lax.Precision.HIGHEST


def product_of(left_matrix, right_matrix):
    return lax.dot_general(
        left_matrix,
        right_matrix,
        (((0,), (0,)), ((), ())),
        precision=HIGHEST_PRECISION,
        preferred_element_type=jnp.float32,
    )


def local(
    tile_values,
    tile_count,
    mode1_column,
    mode1_offset,
    mode2_row,
    mode2_offset,
    mode3_offset,
    mode2_factor,
    mode3_factor,
):
    slot_count = tile_values.shape[0]
    tile_edge = tile_values.shape[1]
    rank_width = mode2_factor.shape[1]
    rows_held = mode2_factor.shape[0]
    col_index = lax.axis_index("col")
    live_count = tile_count[0]
    slot_index = jnp.arange(slot_count, dtype=jnp.int32)
    is_live = slot_index < live_count
    tile_lines = jnp.arange(tile_edge, dtype=jnp.int32)
    owner_row = jnp.where(is_live, mode2_row[:, 0], -1)
    owner_col = jnp.where(is_live, mode1_column[:, 0], -1)
    own_second = product_of(mode2_factor, mode2_factor)
    own_third = product_of(mode3_factor, mode3_factor)
    sum_second = lax.psum(own_second, ("row", "col"))
    sum_third = lax.psum(own_third, "col")
    normal_matrix = sum_second * sum_third
    wanted = (owner_row * rows_held + mode2_offset * tile_edge)[:, None] + tile_lines[None, :]
    shard_piece = lax.all_gather(mode2_factor, "row", axis=0, tiled=True)
    piece_length = shard_piece.shape[0]
    inside = (wanted >= 0) & (wanted < piece_length)
    taken = jnp.take(shard_piece, jnp.clip(wanted, 0, piece_length - 1).reshape(-1), axis=0)
    taken = taken.reshape(slot_count, tile_edge, rank_width)
    picked = jnp.where(inside[:, :, None], taken, 0.0)
    third_index = (mode3_offset * tile_edge)[:, None] + tile_lines[None, :]
    mode3_rows = jnp.take(mode3_factor, third_index.reshape(-1), axis=0).reshape(
        slot_count, tile_edge, rank_width
    )
    group_size = min(8, slot_count)
    group_total = (live_count + group_size - 1) // group_size

    def contract(group_at, partials):
        start_slot = jnp.minimum(group_at * group_size, slot_count - group_size).astype(jnp.int32)
        second_part = lax.dynamic_slice_in_dim(picked, start_slot, group_size, 0)
        third_part = lax.dynamic_slice_in_dim(mode3_rows, start_slot, group_size, 0)
        values_part = lax.dynamic_slice_in_dim(tile_values, start_slot, group_size, 0)
        khatri = (second_part[:, :, None, :] * third_part[:, None, :, :]).reshape(
            group_size, tile_edge * tile_edge, rank_width
        )
        product_rows = jnp.einsum("gie,ger->gir", values_part, khatri, precision=HIGHEST_PRECISION)
        return lax.dynamic_update_slice_in_dim(partials, product_rows, start_slot, 0)

    partials = lax.fori_loop(
        0, group_total, contract, jnp.zeros((slot_count, tile_edge, rank_width), jnp.float32)
    )
    sent_targets = jnp.where(is_live, owner_col * IB_DEV + mode1_offset, -1).astype(jnp.float32)
    own_blocks = (col_index * IB_DEV + jnp.arange(IB_DEV, dtype=jnp.int32)).astype(jnp.float32)
    gathered_rows = lax.all_gather(partials, "col", axis=0, tiled=True)
    gathered_targets = lax.all_gather(sent_targets, "col", axis=0, tiled=True)
    selector = (gathered_targets[:, None] == own_blocks[None, :]).astype(jnp.float32)
    mttkrp = jnp.einsum("pb,pir->bir", selector, gathered_rows, precision=HIGHEST_PRECISION)
    cholesky_factor = jnp.linalg.cholesky(normal_matrix)
    mttkrp_rows = mttkrp.reshape(IB_DEV * tile_edge, rank_width)
    return jax.scipy.linalg.cho_solve((cholesky_factor, True), mttkrp_rows.T).T


def solution(mesh):
    placed = (
        P(("row", "col"), None, None),
        P(("row", "col")),
        P(("row", "col"), None),
        P(("row", "col")),
        P(("row", "col"), None),
        P(("row", "col")),
        P(("row", "col")),
        P(("row", "col"), None),
        P("col", None),
    )
    return jax.shard_map(
        local, mesh=mesh, in_specs=placed, out_specs=P(("row", "col"), None), check_vma=False
    )
```

profile of v0, /device:TPU:32, one launch (start us, length us, event | category | flops | bytes accessed | tf_op | source)
XLA Modules:
  0.0 550.5 jit_solution(1135849408825072373)
XLA Ops:
  7.4 0.7 all-gather.3.cloned.1.call-update
  8.2 2.3 fusion.31
  10.6 1.7 fusion.32
  13.7 3.7 gather_fusion.1
  17.4 1.5 broadcast_select_fusion
  18.8 35.9 %all-gather.3.cloned.1.call-done = f32[4096,256]{1,0:T(8,128)} async-done(((f32[256,256]{1,0:T(8,128)}), f32[4096,256]{1,0:T(8,128)}) %all-gather.3.cloned.1.call-update) | async-done | bytes 4194320 | tf_op jit(solution)/shard_map/all_gather | solution.py:50
  54.7 5.9 %gather_fusion = f32[1536,256]{1,0:T(8,128)S(1)} fusion(f32[4096,256]{1,0:T(8,128)} %all-gather.3.cloned.1.call-done, s32[2048]{0:T(1024)S(1)} %pad_clamp_fusion.1), kind=kCustom, calls=%fused_computation | custom fusion | bytes 3151872 | tf_op jit(solution)/shard_map/jit(_take)/gather | solution.py:53
  60.6 1.5 select_select_fusion
  62.3 53.0 %while.11 = (s32[]{:T(128)}, f32[48,32,256]{2,0,1:T(8,128)S(1)}, s32[]{:T(128)}, f32[48,32,1024]{2,1,0:T(8,128)}, f32[48,32,256]{2,1,0:T(8,128)}, /*index=5*/f32...) while((s32[]{:T(128)}, f32[48,32,256]{2,0,1:T(8,128)S(1)}, ...), condition=%wide.region_7.8_spmd, body=%wide.region_6.7_spmd.sunk | while | flops 807403520 | bytes 20709556 | solution.py:74
  62.3 1.1 constant_dynamic-slice_fusion.5
  63.4 1.2 broadcast_multiply_fusion.3
  64.5 6.1 %fusion.52 = f32[8,32,256]{2,1,0:T(8,128)S(1)} fusion(f32[8,1024,256]{2,1,0:T(8,128)S(1)} %bitcast.78, f32[48,32,1024]{2,1,0:T(8,128)} %get-tuple-element.177, s32[]{:T(128)S(6)} %select_n.118), kind=kOutput, calls=%fused_computation.3.clone.1 | convolution fusion | flops 805306368 | bytes 9699332 | tf_op jit(solution)/shard_map/while/body/gie,ger->gir/dot_general | solution.py:71
  71.1 1.1 constant_dynamic-slice_fusion.5
  72.2 1.2 broadcast_multiply_fusion.3
  73.4 6.1 %fusion.52 = f32[8,32,256]{2,1,0:T(8,128)S(1)} fusion(f32[8,1024,256]{2,1,0:T(8,128)S(1)} %bitcast.78, f32[48,32,1024]{2,1,0:T(8,128)} %get-tuple-element.177, s32[]{:T(128)S(6)} %select_n.118), kind=kOutput, calls=%fused_computation.3.clone.1 | convolution fusion | flops 805306368 | bytes 9699332 | tf_op jit(solution)/shard_map/while/body/gie,ger->gir/dot_general | solution.py:71
  80.0 1.1 constant_dynamic-slice_fusion.5
  81.0 1.2 broadcast_multiply_fusion.3
  82.2 6.1 %fusion.52 = f32[8,32,256]{2,1,0:T(8,128)S(1)} fusion(f32[8,1024,256]{2,1,0:T(8,128)S(1)} %bitcast.78, f32[48,32,1024]{2,1,0:T(8,128)} %get-tuple-element.177, s32[]{:T(128)S(6)} %select_n.118), kind=kOutput, calls=%fused_computation.3.clone.1 | convolution fusion | flops 805306368 | bytes 9699332 | tf_op jit(solution)/shard_map/while/body/gie,ger->gir/dot_general | solution.py:71
  88.8 1.1 constant_dynamic-slice_fusion.5
  89.9 1.2 broadcast_multiply_fusion.3
  91.0 6.1 %fusion.52 = f32[8,32,256]{2,1,0:T(8,128)S(1)} fusion(f32[8,1024,256]{2,1,0:T(8,128)S(1)} %bitcast.78, f32[48,32,1024]{2,1,0:T(8,128)} %get-tuple-element.177, s32[]{:T(128)S(6)} %select_n.118), kind=kOutput, calls=%fused_computation.3.clone.1 | convolution fusion | flops 805306368 | bytes 9699332 | tf_op jit(solution)/shard_map/while/body/gie,ger->gir/dot_general | solution.py:71
  97.6 1.1 constant_dynamic-slice_fusion.5
  98.7 1.2 broadcast_multiply_fusion.3
  99.9 6.1 %fusion.52 = f32[8,32,256]{2,1,0:T(8,128)S(1)} fusion(f32[8,1024,256]{2,1,0:T(8,128)S(1)} %bitcast.78, f32[48,32,1024]{2,1,0:T(8,128)} %get-tuple-element.177, s32[]{:T(128)S(6)} %select_n.118), kind=kOutput, calls=%fused_computation.3.clone.1 | convolution fusion | flops 805306368 | bytes 9699332 | tf_op jit(solution)/shard_map/while/body/gie,ger->gir/dot_general | solution.py:71
  106.5 1.1 constant_dynamic-slice_fusion.5
  107.5 1.2 broadcast_multiply_fusion.3
  108.7 6.1 %fusion.52 = f32[8,32,256]{2,1,0:T(8,128)S(1)} fusion(f32[8,1024,256]{2,1,0:T(8,128)S(1)} %bitcast.78, f32[48,32,1024]{2,1,0:T(8,128)} %get-tuple-element.177, s32[]{:T(128)S(6)} %select_n.118), kind=kOutput, calls=%fused_computation.3.clone.1 | convolution fusion | flops 805306368 | bytes 9699332 | tf_op jit(solution)/shard_map/while/body/gie,ger->gir/dot_general | solution.py:71
  115.3 1.2 copy-done.1
  116.5 0.6 dynamic-slice.3
  117.8 40.4 %all-reduce.1 = f32[768]{0:T(1024)S(1)} all-reduce(f32[768]{0:T(1024)S(1)} %convert_dynamic-update-slice_fusion), channel_id=1, replica_groups=mesh['row'=16,'col'=16] {'col'}, use_global_device_ids=true, to_apply=%add.1 | all-reduce | flops 768 | bytes 6144
  158.2 109.1 %all-reduce.5.cloned.1.call-done = f32[256,256]{0,1:T(8,128)} async-done(((f32[256,256]{0,1:T(8,128)}), f32[256,256]{0,1:T(8,128)}) %all-reduce.5.cloned.1.call-update) | async-done | bytes 262160 | tf_op jit(solution)/shard_map/psum | solution.py:46
  267.4 98.0 %all-reduce.7.cloned.1.call-done = f32[256,256]{0,1:T(8,128)} async-done(((f32[256,256]{0,1:T(8,128)}), f32[256,256]{0,1:T(8,128)}) %all-reduce.7.cloned.1.call-update) | async-done | bytes 262160 | tf_op jit(solution)/shard_map/psum | solution.py:47
  365.3 1.1 mul.44
  366.6 11.7 %cholesky.50 = f32[128,128]{1,0:T(8,128)S(1)} custom-call(f32[128,128]{1,0:T(8,128)S(1)} %cholesky.118), custom_call_target="Cholesky" | custom-call | tf_op jit(solution)/shard_map/jit(cholesky)/cholesky | solution.py:83
  378.4 9.8 %custom-call.18 = f32[1,128,128]{1,2,0:T(8,128)S(1)} custom-call(f32[1,128,128]{2,1,0:T(8,128)S(1)} %get-tuple-element.74), custom_call_target="InvertDiagBlocksLowerTriangular" | custom-call | tf_op jit(solution)/shard_map/jit(cholesky)/cholesky | solution.py:83
  388.7 11.7 %cholesky.105 = f32[128,128]{1,0:T(8,128)S(1)} custom-call(f32[128,128]{1,0:T(8,128)S(1)} %convolution_subtract_fusion.2), custom_call_target="Cholesky" | custom-call | tf_op jit(solution)/shard_map/jit(cholesky)/cholesky | solution.py:83
  400.4 0.7 compare_reduce_fusion
  402.6 4.3 while.12
  402.8 0.6 fusion.53
  403.4 1.4 bitcast_dynamic-update-slice_fusion.2
  404.8 0.6 fusion.53
  405.4 1.4 bitcast_dynamic-update-slice_fusion.2
  406.9 19.7 %custom-call.19 = f32[2,128,128]{1,2,0:T(8,128)S(1)} custom-call(f32[2,128,128]{2,1,0:T(8,128)S(1)} %get-tuple-element.46), custom_call_target="InvertDiagBlocksLowerTriangular" | custom-call | tf_op jit(solution)/shard_map/jit(_cho_solve)/triangular_solve | solution.py:85
  426.6 100.0 %all-gather.5.cloned.1.call-done = f32[768,32,256]{2,0,1:T(8,128)} async-done(((f32[48,32,256]{2,0,1:T(8,128)}), f32[768,32,256]{2,0,1:T(8,128)}) %all-gather.5.cloned.1.call-update) | async-done | bytes 25165840 | tf_op jit(solution)/shard_map/all_gather | solution.py:79
  526.6 12.3 %fusion.14 = f32[16,32,256]{2,0,1:T(8,128)S(1)} fusion(f32[768,32,256]{2,0,1:T(8,128)} %all-gather.5.cloned.1.call-done, f32[768]{0:T(1024)S(1)} %all-reduce.1, f32[16]{0:T(128)S(1)} %add_convert_fusion), kind=kOutput, calls=%fused_computation.39 | convolution fusion | flops 1207971840 | bytes 25693248 | tf_op jit(solution)/shard_map/pb,pir->bir/dot_general | solution.py:82
  539.6 0.6 convolution_subtract_fusion.1
  541.0 0.4 convolution_subtract_fusion
  541.9 1.0 copy.20
  (70 shorter events, 6.5 us)
Async XLA Ops:
  7.4 3.2 copy-start
  7.4 5.7 %copy-start.4 = (s32[48,1]{0,1:T(1,128)S(1)}, s32[48,1]{0,1:T(1,128)}, u32[]{:S(2)}) copy-start(s32[48,1]{0,1:T(1,128)} %param.15) | copy-start | bytes 580
  7.4 5.7 %copy-start.5 = (s32[48]{0:T(128)S(1)}, s32[48]{0:T(128)}, u32[]{:S(2)}) copy-start(s32[48]{0:T(128)} %param.16) | copy-start | bytes 580
  7.4 5.9 %copy-start.6 = (s32[48]{0:T(128)S(1)}, s32[48]{0:T(128)}, u32[]{:S(2)}) copy-start(s32[48]{0:T(128)} %param.17) | copy-start | bytes 580
  7.4 47.4 %all-gather.3.cloned.1.call-start = ((), (), s32[]{:S(2)}) async-start(), calls=%async_computation.2 | async-start | bytes 4456448 | tf_op jit(solution)/shard_map/all_gather | solution.py:50
  8.1 259.2 %all-reduce.5.cloned.1.call-start = ((), (), s32[]{:S(2)}) async-start(), calls=%async_computation | async-start | bytes 524288 | tf_op jit(solution)/shard_map/psum | solution.py:46
  10.5 354.8 %all-reduce.7.cloned.1.call-start = ((), (), s32[]{:S(2)}) async-start(), calls=%async_computation.1 | async-start | bytes 524288 | tf_op jit(solution)/shard_map/psum | solution.py:47
  12.3 514.2 %all-gather.5.cloned.1.call-start = ((), (), s32[]{:S(2)}) async-start(), calls=%async_computation.3 | async-start | bytes 26738688 | tf_op jit(solution)/shard_map/all_gather | solution.py:79
  115.2 1.2 copy-start.1
  115.2 1.3 copy-start.7
  115.3 2.4 copy-start.2
  115.3 2.4 copy-start.3
Sparse Core Ops, SparseCore 0:
  10.2 44.5 all-gather.2
Sparse Core Ops, SparseCore 1:
  14.0 253.3 all-reduce.4
  270.4 94.9 all-reduce.6
  367.9 158.6 all-gather.4
where the time goes:
time: 552 us; the launch traced here: 550 us
  waiting for transfers between devices  344 us (62%)
  other arithmetic  65.2 us (12%)
  matrix products  56.1 us (10%)
  blocking collectives  40.4 us (7%)
  local copies, waits for them, and re-layouts  26.3 us (5%)
  between operations  18 us (3%)
    psum x1, waiting for transfers between devices, local(): sum_second = lax.psum(own_second, ('row', 'col'))  109 us
    all_gather x1, waiting for transfers between devices, local(): gathered_rows = lax.all_gather(partials, 'col', axis=0, tiled=True)  100 us
    psum x1, waiting for transfers between devices, local(): sum_third = lax.psum(own_third, 'col')  98 us
    unnamed x1, blocking collectives  40.4 us
    dot_general x6, matrix products, contract(): jnp.einsum('gie,ger->gir', values_part, khatri, precision=HIGHEST_PRECISION)  36.6 us
    all_gather x1, waiting for transfers between devices, local(): shard_piece = lax.all_gather(mode2_factor, 'row', axis=0, tiled=True)  35.9 us
    another operation x6, other arithmetic, local(): cholesky_factor = jnp.linalg.cholesky(normal_matrix)  34 us
    another operation x3, other arithmetic, local(): return jax.scipy.linalg.cho_solve((cholesky_factor, True), mttkrp_rows.T).T  19.7 us
  transfers between devices with their start and end apart: 4, of which 4 were waited for; matrix products, arithmetic and copies ran while one was open for 24% of the time, Pallas kernels for 0%

commit v1 on v0

v1 whole, which is shorter than its diff:
```python
import jax
import jax.numpy as jnp
from jax import lax
from jax.experimental import pallas as pl
from jax.experimental.pallas import tpu as pltpu
from jax.sharding import PartitionSpec as P

IB_DEV = 16
JB_DEV = 8
SLOTS = 4
PAIR = 2

HIGHEST = lax.Precision.HIGHEST


def gram_of(matrix):
    return lax.dot_general(
        matrix, matrix, (((0,), (0,)), ((), ())), precision=HIGHEST, preferred_element_type=jnp.float32
    )


def split(value):
    high = value.astype(jnp.bfloat16)
    low = (value - high.astype(jnp.float32)).astype(jnp.bfloat16)
    return high, low


def dot32(left, right):
    return jnp.dot(left, right, preferred_element_type=jnp.float32)


def contract_kernel(
    table_ref, count_ref, tile_hbm, second_hbm, third_ref, out_ref, tile_buf, second_buf, tile_sem, second_sem
):
    count = count_ref[0]
    pairs = (count + PAIR - 1) // PAIR
    tile_edge = third_ref.shape[1]
    depth = tile_buf.shape[2]
    chunk = min(256, depth)
    per_chunk = chunk // tile_edge

    def tile_copy(pair):
        return pltpu.make_async_copy(
            tile_hbm.at[pl.ds(pair * PAIR, PAIR)], tile_buf.at[pl.ds(pair * PAIR, PAIR)], tile_sem.at[pair]
        )

    def second_copy(slot):
        return pltpu.make_async_copy(
            second_hbm.at[table_ref[0, slot]], second_buf.at[slot], second_sem.at[slot]
        )

    def start(pair, carry):
        tile_copy(pair).start()
        for at in range(PAIR):
            second_copy(pair * PAIR + at).start()
        return carry

    lax.fori_loop(0, pairs, start, 0)
    out_ref[...] = jnp.zeros_like(out_ref)

    def contract(pair, carry):
        tile_copy(pair).wait()
        for at in range(PAIR):
            second_copy(pair * PAIR + at).wait()
        for at in range(PAIR):
            slot = pair * PAIR + at
            second = second_buf[slot]
            third = third_ref[table_ref[1, slot]]
            high, low = split(tile_buf[slot])
            both = jnp.concatenate([high, low], axis=0)
            total = jnp.zeros((2 * tile_edge, third.shape[1]), jnp.float32)
            total_low = jnp.zeros((tile_edge, third.shape[1]), jnp.float32)
            for q in range(depth // chunk):
                rows = second[q * per_chunk : (q + 1) * per_chunk]
                khatri = (rows[:, None, :] * third[None, :, :]).reshape(chunk, third.shape[1])
                khatri_high, khatri_low = split(khatri)
                total = total + dot32(both[:, q * chunk : (q + 1) * chunk], khatri_high)
                total_low = total_low + dot32(high[:, q * chunk : (q + 1) * chunk], khatri_low)
            result = total[:tile_edge] + (total[tile_edge:] + total_low)

            @pl.when(slot < count)
            def _():
                out_ref[table_ref[2, slot]] = result

        return carry

    lax.fori_loop(0, pairs, contract, 0)


def contract_tiles(table, count, tile_values, second_blocks, third_blocks, out_slots):
    slot_count, tile_edge, depth = tile_values.shape
    rank_width = third_blocks.shape[2]
    smem = pl.BlockSpec(memory_space=pltpu.SMEM)
    vmem = pl.BlockSpec(memory_space=pltpu.VMEM)
    hbm = pl.BlockSpec(memory_space=pl.ANY)
    return pl.pallas_call(
        contract_kernel,
        out_shape=jax.ShapeDtypeStruct((out_slots, tile_edge, rank_width), jnp.float32),
        in_specs=[smem, smem, hbm, hbm, vmem],
        out_specs=vmem,
        scratch_shapes=[
            pltpu.VMEM((slot_count, tile_edge, depth), jnp.float32),
            pltpu.VMEM((slot_count, tile_edge, rank_width), jnp.float32),
            pltpu.SemaphoreType.DMA((slot_count // PAIR,)),
            pltpu.SemaphoreType.DMA((slot_count,)),
        ],
        compiler_params=pltpu.CompilerParams(vmem_limit_bytes=28 * 1024 * 1024),
        cost_estimate=pl.CostEstimate(
            flops=6 * slot_count * tile_edge * depth * rank_width, bytes_accessed=10_000_000, transcendentals=0
        ),
        name="contract",
    )(table, count, tile_values, second_blocks, third_blocks)


def combine_kernel(target_ref, received_ref, inverse_ref, out_ref, total_ref):
    tile_edge = received_ref.shape[1]
    total_ref[...] = jnp.zeros_like(total_ref)

    def add(slot, carry):
        target = target_ref[slot]

        @pl.when(target >= 0)
        def _():
            rows = pl.ds(pl.multiple_of(target * tile_edge, tile_edge), tile_edge)
            total_ref[rows, :] += received_ref[slot]

        return carry

    lax.fori_loop(0, received_ref.shape[0], add, 0)
    out_ref[...] = jnp.dot(
        total_ref[...], inverse_ref[...], precision=HIGHEST, preferred_element_type=jnp.float32
    )


def combine(targets, received, inverse):
    tile_edge, rank_width = received.shape[1:]
    vmem = pl.BlockSpec(memory_space=pltpu.VMEM)
    return pl.pallas_call(
        combine_kernel,
        out_shape=jax.ShapeDtypeStruct((IB_DEV * tile_edge, rank_width), jnp.float32),
        in_specs=[pl.BlockSpec(memory_space=pltpu.SMEM), vmem, vmem],
        out_specs=vmem,
        scratch_shapes=[pltpu.VMEM((IB_DEV * tile_edge, rank_width), jnp.float32)],
        compiler_params=pltpu.CompilerParams(vmem_limit_bytes=16 * 1024 * 1024),
        name="combine",
    )(targets, received, inverse)


def local(
    tile_values,
    tile_count,
    mode1_column,
    mode1_offset,
    mode2_row,
    mode2_offset,
    mode3_offset,
    mode2_factor,
    mode3_factor,
):
    slot_count, tile_edge, _ = tile_values.shape
    rank_width = mode2_factor.shape[1]
    row_index = lax.axis_index("row")
    col_index = lax.axis_index("col")
    n_row = lax.axis_size("row")
    n_col = lax.axis_size("col")
    part = rank_width // n_row

    with jax.named_scope("gather_second"):
        gathered = lax.all_gather(mode2_factor, "row", axis=0, tiled=True)

    with jax.named_scope("tables"):
        slot_index = jnp.arange(slot_count, dtype=jnp.int32)
        is_live = slot_index < tile_count[0]
        chosen = (mode1_column[:, 0][None, :] == jnp.arange(n_col, dtype=jnp.int32)[:, None]) & is_live[None, :]
        chosen = chosen.astype(jnp.float32)
        earlier = (slot_index[:, None] < slot_index[None, :]).astype(jnp.float32)
        rank = jnp.dot(chosen, earlier)
        own_rank = jnp.sum(chosen * rank, axis=0).astype(jnp.int32)
        out_slot = jnp.clip(mode1_column[:, 0], 0, n_col - 1) * SLOTS + own_rank
        table = jnp.stack(
            [
                jnp.clip(mode2_row[:, 0] * JB_DEV + mode2_offset, 0, gathered.shape[0] // tile_edge - 1),
                jnp.clip(mode3_offset, 0, mode3_factor.shape[0] // tile_edge - 1),
                out_slot,
            ]
        ).astype(jnp.int32)
        place = jnp.arange(SLOTS, dtype=jnp.float32)
        taken = chosen[:, None, :] * (rank[:, None, :] == place[None, :, None])
        targets = jnp.sum(taken * (mode1_offset + 1).astype(jnp.float32), axis=2) - 1.0
        target_rows = jnp.zeros((8, rank_width), jnp.float32).at[0, : n_col * SLOTS].set(targets.reshape(-1))

    with jax.named_scope("normal"):
        own_second = gram_of(mode2_factor)
        own_third = gram_of(mode3_factor)
        exchanged = lax.all_to_all(own_second.reshape(n_row, part, rank_width), "row", 0, 0)
        second_part = jnp.sum(exchanged, axis=0)
        third_part = lax.dynamic_slice_in_dim(own_third, row_index * part, part, 0)
        sent = jnp.concatenate([second_part, third_part, target_rows], axis=0)
        spread = lax.all_gather(sent, "col", axis=0)
        both = jnp.sum(spread[:, : 2 * part], axis=0)
        normal_part = both[:part] * both[part:]
        normal_matrix = lax.all_gather(normal_part, "row", axis=0, tiled=True)
        received_targets = lax.dynamic_slice_in_dim(spread[:, 2 * part], col_index * SLOTS, SLOTS, 1)
        received_targets = received_targets.astype(jnp.int32).reshape(-1)

    with jax.named_scope("contract"):
        partials = contract_tiles(
            table,
            tile_count,
            tile_values,
            gathered.reshape(-1, tile_edge, rank_width),
            mode3_factor.reshape(-1, tile_edge, rank_width),
            n_col * SLOTS,
        )
    with jax.named_scope("exchange"):
        received = lax.all_to_all(
            partials.reshape(n_col, SLOTS * tile_edge, rank_width), "col", 0, 0
        ).reshape(n_col * SLOTS, tile_edge, rank_width)

    with jax.named_scope("inverse"):
        factor = jnp.linalg.cholesky(normal_matrix)
        inverse = jax.scipy.linalg.cho_solve((factor, True), jnp.eye(rank_width, dtype=jnp.float32))

    with jax.named_scope("combine"):
        return combine(received_targets, received, inverse)


def solution(mesh):
    placed = (
        P(("row", "col"), None, None),
        P(("row", "col")),
        P(("row", "col"), None),
        P(("row", "col")),
        P(("row", "col"), None),
        P(("row", "col")),
        P(("row", "col")),
        P(("row", "col"), None),
        P("col", None),
    )
    return jax.shard_map(
        local, mesh=mesh, in_specs=placed, out_specs=P(("row", "col"), None), check_vma=False
    )
```

time: 552 us -> 182 us (0.33)
  waiting for transfers between devices: 344 us -> 8.84 us
  matrix products: 56.1 us -> 7.62 us
  Pallas kernels: 0 us -> 22.3 us
  starting transfers between devices: 0.16 us -> 18.3 us
  local copies, waits for them, and re-layouts: 26.3 us -> 10.8 us
  other arithmetic: 65.2 us -> 56.7 us
    psum x2 -> x0, waiting for transfers between devices: 207 us -> none  [the longest x1 109 us: local(): sum_second = lax.psum(own_second, ('row', 'col'))]
    all_gather x2 -> x1, waiting for transfers between devices: 136 us -> 0.02 us  [local(): gathered = lax.all_gather(mode2_factor, 'row', axis=0, tiled=True)]
    dot_general x9 -> x3, matrix products: 53 us -> 5.49 us  [the longest x2 4.62 us: gram_of(): lax.dot_general(matrix, matrix, (((0,), (0,)), ((), ())), precision=HIGHE...]
    all_gather x0 -> x2, blocking collectives: none -> 41.3 us  [the longest x1 24.8 us: local(): spread = lax.all_gather(sent, 'col', axis=0)]
    unnamed x1 -> x0, blocking collectives: 40.4 us -> none
    pallas_call x0 -> x2, Pallas kernels: none -> 22.3 us  [the longest x1 19.4 us: contract_tiles(): pl.pallas_call(contract_kernel, out_shape=jax.ShapeDtypeStruct((out_slots...]
    all_to_all x0 -> x2, starting transfers between devices: none -> 18.3 us  [the longest x1 9.68 us: local(): lax.all_to_all(partials.reshape(n_col, SLOTS * tile_edge, rank_width), 'c...]
    gather x2 -> x0, local copies, waits for them, and re-layouts: 9.53 us -> none  [the longest x1 5.86 us: local(): jnp.take(shard_piece, jnp.clip(wanted, 0, piece_length - 1).reshape(-1),...]
  transfers between devices with their start and end apart: 4 -> 3, of which waited for: 4 -> 2; matrix products, arithmetic and copies ran while one was open for 24% -> 38% of each run, Pallas kernels for 0% -> 0%
where the time goes in v1:
time: 182 us; the launch traced here: 181 us
  other arithmetic  56.7 us (31%)
  blocking collectives  41.3 us (23%)
  Pallas kernels  22.3 us (12%)
  starting transfers between devices  18.3 us (10%)
  between operations  15.6 us (9%)
  local copies, waits for them, and re-layouts  10.8 us (6%)
  waiting for transfers between devices  8.84 us (5%)
  matrix products  7.62 us (4%)
    another operation x6, other arithmetic, local(): factor = jnp.linalg.cholesky(normal_matrix)  34 us
    all_gather x1, blocking collectives, local(): spread = lax.all_gather(sent, 'col', axis=0)  24.8 us
    another operation x4, other arithmetic, local(): jax.scipy.linalg.cho_solve((factor, True), jnp.eye(rank_width, dtype=jnp....  19.7 us
    pallas_call x1, Pallas kernels, contract_tiles(): pl.pallas_call(contract_kernel, out_shape=jax.ShapeDtypeStruct((out_slots...  19.4 us
    all_gather x1, blocking collectives, local(): normal_matrix = lax.all_gather(normal_part, 'row', axis=0, tiled=True)  16.4 us
    all_to_all x1, starting transfers between devices, local(): lax.all_to_all(partials.reshape(n_col, SLOTS * tile_edge, rank_width), 'c...  9.68 us
    all_to_all x1, starting transfers between devices, local(): lax.all_to_all(own_second.reshape(n_row, part, rank_width), 'row', 0, 0)  8.59 us
    unnamed x8, local copies, waits for them, and re-layouts  6.32 us
  transfers between devices with their start and end apart: 3, of which 2 were waited for; matrix products, arithmetic and copies ran while one was open for 38% of the time, Pallas kernels for 0%

profile of v1, /device:TPU:32, one launch (start us, length us, event | category | flops | bytes accessed | tf_op | source)
XLA Modules:
  0.0 181.5 jit_solution(10166284817587803548)
XLA Ops:
  6.5 0.0 all-gather.3.cloned.1.call-start
  6.5 0.7 all-gather.3.cloned.1.call-update
  7.3 2.4 %fusion.20 = f32[256,256]{1,0:T(8,128)} fusion(f32[256,256]{1,0:T(8,128)} %param.18), kind=kOutput, calls=%fused_computation.59 | convolution fusion | flops 201326592 | bytes 524288 | tf_op jit(solution)/shard_map/normal/dot_general | solution.py:17
  9.6 8.6 %all-to-all-start = ((f32[16,16,256]{2,1,0:T(8,128)}), f32[16,16,256]{2,1,0:T(8,128)S(1)}, u32[]{:S(2)}, u32[]{:S(2)}) async-start(f32[16,16,256]{2,1,0:T(8,128)} %bitcast), calls=%async_computation | async-start | bytes 524288 | tf_op jit(solution)/shard_map/normal/all_to_all | solution.py:195
  18.9 0.9 select_reduce_fusion.2
  19.8 0.7 bitcast_add_fusion.1
  20.4 0.7 fusion.18
  21.1 0.7 add_convert_fusion
  21.8 0.7 fusion.13
  22.4 0.1 multiply_reduce_fusion
  22.6 0.1 copy.16
  22.6 0.1 sub.7
  22.7 2.2 %fusion.21 = f32[256,256]{1,0:T(8,128)S(1)} fusion(f32[512,256]{1,0:T(8,128)} %param.19), kind=kOutput, calls=%fused_computation.60 | convolution fusion | flops 402653184 | bytes 786432 | tf_op jit(solution)/shard_map/normal/dot_general | solution.py:17
  25.0 2.8 %all-to-all-done = f32[16,16,256]{2,1,0:T(8,128)S(1)} async-done(((f32[16,16,256]{2,1,0:T(8,128)}), f32[16,16,256]{2,1,0:T(8,128)S(1)}, u32[]{:S(2)}, u32[]{:S(2)}) %all-to-all-start) | async-done | bytes 262176 | tf_op jit(solution)/shard_map/normal/all_to_all | solution.py:195
  27.9 24.8 %all-gather = f32[640,256]{1,0:T(8,128)S(1)} all-gather(f32[40,256]{1,0:T(8,128)S(1)} %select_maximum_fusion), channel_id=2, replica_groups=mesh['row'=16,'col'=16] {'col'}, dimensions={0}, use_global_device_ids=true | all-gather | bytes 696320 | tf_op jit(solution)/shard_map/normal/all_gather | solution.py:199
  52.8 0.1 constant_dynamic-slice_fusion.1
  52.8 0.1 convert_element_type.36.target_ref
  53.0 16.4 %all_gather.15 = f32[256,256]{1,0:T(8,128)S(1)} all-gather(f32[16,256]{1,0:T(8,128)S(1)} %slice_multiply_fusion), channel_id=1, replica_groups=mesh['row'=16,'col'=16] {'row'}, dimensions={0}, use_global_device_ids=true | all-gather | bytes 278528 | tf_op jit(solution)/shard_map/normal/all_gather | solution.py:202
  69.4 0.1 copy.18
  69.6 11.7 %cholesky.50 = f32[128,128]{1,0:T(8,128)S(1)} custom-call(f32[128,128]{1,0:T(8,128)S(1)} %cholesky.118), custom_call_target="Cholesky" | custom-call | tf_op jit(solution)/shard_map/inverse/jit(cholesky)/cholesky | solution.py:221
  81.4 9.8 %custom-call.18 = f32[1,128,128]{1,2,0:T(8,128)S(1)} custom-call(f32[1,128,128]{2,1,0:T(8,128)S(1)} %get-tuple-element.38), custom_call_target="InvertDiagBlocksLowerTriangular" | custom-call | tf_op jit(solution)/shard_map/inverse/jit(cholesky)/cholesky | solution.py:221
  91.2 0.2 constant_dynamic-update-slice_fusion
  91.4 0.3 convolution_subtract_fusion.2
  91.7 11.7 %cholesky.105 = f32[128,128]{1,0:T(8,128)S(1)} custom-call(f32[128,128]{1,0:T(8,128)S(1)} %convolution_subtract_fusion.2), custom_call_target="Cholesky" | custom-call | tf_op jit(solution)/shard_map/inverse/jit(cholesky)/cholesky | solution.py:221
  103.4 0.7 compare_reduce_fusion
  105.5 0.0 all-gather.3.cloned.1.call-done
  105.6 0.0 copy-done.2
  105.6 0.0 copy-start.1
  105.6 2.8 %copy-done.1 = f32[48,32,1024]{2,1,0:T(8,128)S(1)} copy-done((f32[48,32,1024]{2,1,0:T(8,128)S(1)}, f32[48,32,1024]{2,1,0:T(8,128)}, u32[]{:S(2)}) %copy-start.1) | copy-done | bytes 6291480
  108.4 2.2 %copy-done.3 = f32[4096,256]{1,0:T(8,128)S(1)} copy-done((f32[4096,256]{1,0:T(8,128)S(1)}, f32[4096,256]{1,0:T(8,128)}, u32[]{:S(2)}) %copy-start.3) | copy-done | bytes 4194328
  110.5 19.4 %contract.1 = f32[64,32,256]{2,1,0:T(8,128)S(1)} custom-call(s32[3,48]{1,0:T(4,128)S(1)} %pad_add_fusion.table_ref, s32[1]{0:T(128)} %copy.31.count_ref, f32[48,32,1024]{2,1,0:T(8,128)S(1)} %copy-done.1, f32[128,32,256]{2,1,0:T(8,128)S(1)} %bitcast.69, f32[16,32,256]{2,1,0:T(8,128)S(1)} %bitcast.68), custom_call_target="tpu_custom_call" | custom-call | flops 2415919104 | bytes 10000000 | tf_op jit(solution)/shard_map/contract/contract/pallas_call | solution.py:96
  129.9 1.3 copy-done
  131.3 9.7 %all-to-all-start.1 = ((f32[16,128,256]{2,1,0:T(8,128)}), f32[16,128,256]{2,1,0:T(8,128)S(1)}, u32[]{:S(2)}, u32[]{:S(2)}) async-start(f32[16,128,256]{2,1,0:T(8,128)} %bitcast.67), calls=%async_computation.1 | async-start | bytes 4194304 | tf_op jit(solution)/shard_map/exchange/all_to_all | solution.py:216
  141.0 0.1 triangular_solve.72
  141.0 3.9 %while.2 = (s32[]{:T(128)}, f32[256,256]{1,0:T(8,128)S(1)}, s32[2,2]{1,0:T(2,128)S(1)}, f32[2,128,128]{2,1,0:T(8,128)S(1)}, s32[]{:T(128)}) while((s32[]{:T(128)}, f32[256,256]{1,0:T(8,128)S(1)}, s32[2,2]{1,0:T(2,128)S(1)}, f32[2,128,128]{2,1,0:T(8,128)S(1)}, s32[]{:T(128)}) %tuple.29), condition=%wide.while_cond.1, body=%wide.while_body.1.sunk | while | flops 2 | bytes 131189 | solution.py:222
  141.1 0.6 fusion.34
  141.6 1.4 bitcast_dynamic-update-slice_fusion.2
  143.0 0.6 fusion.34
  143.6 1.4 bitcast_dynamic-update-slice_fusion.2
  145.0 19.7 %custom-call.19 = f32[2,128,128]{1,2,0:T(8,128)S(1)} custom-call(f32[2,128,128]{2,1,0:T(8,128)S(1)} %get-tuple-element.24), custom_call_target="InvertDiagBlocksLowerTriangular" | custom-call | tf_op jit(solution)/shard_map/inverse/jit(_cho_solve)/triangular_solve | solution.py:222
  164.7 0.3 fusion.1
  164.9 0.3 convolution_subtract_fusion.1
  165.2 0.3 fusion.8
  165.5 0.3 fusion.7
  165.8 0.3 convolution_subtract_fusion
  166.1 0.3 fusion.6
  166.4 5.3 %all-to-all-done.1 = f32[16,128,256]{2,1,0:T(8,128)S(1)} async-done(((f32[16,128,256]{2,1,0:T(8,128)}), f32[16,128,256]{2,1,0:T(8,128)S(1)}, u32[]{:S(2)}, u32[]{:S(2)}) %all-to-all-start.1) | async-done | bytes 2097184 | tf_op jit(solution)/shard_map/exchange/all_to_all | solution.py:216
  171.7 2.9 %combine.1 = f32[512,256]{1,0:T(8,128)} custom-call(s32[64]{0:T(128)S(1)} %convert_element_type.36.target_ref, f32[64,32,256]{2,1,0:T(8,128)S(1)} %bitcast.66, f32[256,256]{1,0:T(8,128)S(1)} %pad_maximum_fusion.inverse_ref), custom_call_target="tpu_custom_call" | custom-call | tf_op jit(solution)/shard_map/combine/combine/pallas_call | solution.py:138
  (25 shorter events, 0.4 us)
Async XLA Ops:
  6.5 99.0 %copy-start.2 = (f32[512,256]{1,0:T(8,128)S(1)}, f32[512,256]{1,0:T(8,128)}, u32[]{:S(2)}) copy-start(f32[512,256]{1,0:T(8,128)} %param.19) | copy-start | bytes 1572868
  6.5 99.0 %all-gather.3.cloned.1.call-start = ((), (), s32[]{:S(2)}) async-start(), calls=%async_computation.2 | async-start | bytes 4456448 | tf_op jit(solution)/shard_map/gather_second/all_gather | solution.py:169
  9.6 18.2 %all-to-all-start = ((f32[16,16,256]{2,1,0:T(8,128)}), f32[16,16,256]{2,1,0:T(8,128)S(1)}, u32[]{:S(2)}, u32[]{:S(2)}) async-start(f32[16,16,256]{2,1,0:T(8,128)} %bitcast), calls=%async_computation | async-start | bytes 524288 | tf_op jit(solution)/shard_map/normal/all_to_all | solution.py:195
  105.6 2.8 %copy-start.1 = (f32[48,32,1024]{2,1,0:T(8,128)S(1)}, f32[48,32,1024]{2,1,0:T(8,128)}, u32[]{:S(2)}) copy-start(f32[48,32,1024]{2,1,0:T(8,128)} %tile_hbm.1) | copy-start | bytes 18874372
  108.4 2.2 %copy-start.3 = (f32[4096,256]{1,0:T(8,128)S(1)}, f32[4096,256]{1,0:T(8,128)}, u32[]{:S(2)}) copy-start(f32[4096,256]{1,0:T(8,128)} %all-gather.3.cloned.1.call-done) | copy-start | bytes 12582916
  129.9 1.4 copy-start
  131.3 40.4 %all-to-all-start.1 = ((f32[16,128,256]{2,1,0:T(8,128)}), f32[16,128,256]{2,1,0:T(8,128)S(1)}, u32[]{:S(2)}, u32[]{:S(2)}) async-start(f32[16,128,256]{2,1,0:T(8,128)} %bitcast.67), calls=%async_computation.1 | async-start | bytes 4194304 | tf_op jit(solution)/shard_map/exchange/all_to_all | solution.py:216
Sparse Core Ops, SparseCore 0:
  9.2 45.8 all-gather.2

commit v2 on v1

--- a/solution.py
+++ b/solution.py
@@ -1,3 +1,5 @@
+import functools
+
 import jax
 import jax.numpy as jnp
 from jax import lax
@@ -30,7 +32,18 @@
 
 
 def contract_kernel(
-    table_ref, count_ref, tile_hbm, second_hbm, third_ref, out_ref, tile_buf, second_buf, tile_sem, second_sem
+    table_ref,
+    count_ref,
+    tile_hbm,
+    second_hbm,
+    third_ref,
+    out_hbm,
+    tile_buf,
+    second_buf,
+    result_buf,
+    tile_sem,
+    second_sem,
+    result_sem,
 ):
     count = count_ref[0]
     pairs = (count + PAIR - 1) // PAIR
@@ -49,6 +62,9 @@
             second_hbm.at[table_ref[0, slot]], second_buf.at[slot], second_sem.at[slot]
         )
 
+    def result_copy(slot):
+        return pltpu.make_async_copy(result_buf.at[slot], out_hbm.at[table_ref[2, slot]], result_sem.at[slot])
+
     def start(pair, carry):
         tile_copy(pair).start()
         for at in range(PAIR):
@@ -56,7 +72,6 @@
         return carry
 
     lax.fori_loop(0, pairs, start, 0)
-    out_ref[...] = jnp.zeros_like(out_ref)
 
     def contract(pair, carry):
         tile_copy(pair).wait()
@@ -76,15 +91,21 @@
                 khatri_high, khatri_low = split(khatri)
                 total = total + dot32(both[:, q * chunk : (q + 1) * chunk], khatri_high)
                 total_low = total_low + dot32(high[:, q * chunk : (q + 1) * chunk], khatri_low)
-            result = total[:tile_edge] + (total[tile_edge:] + total_low)
+            result_buf[slot] = total[:tile_edge] + (total[tile_edge:] + total_low)
 
             @pl.when(slot < count)
             def _():
-                out_ref[table_ref[2, slot]] = result
+                result_copy(slot).start()
 
         return carry
 
     lax.fori_loop(0, pairs, contract, 0)
+
+    def finish(slot, carry):
+        result_copy(slot).wait()
+        return carry
+
+    lax.fori_loop(0, count, finish, 0)
 
 
 def contract_tiles(table, count, tile_values, second_blocks, third_blocks, out_slots):
@@ -92,19 +113,21 @@
     rank_width = third_blocks.shape[2]
     smem = pl.BlockSpec(memory_space=pltpu.SMEM)
     vmem = pl.BlockSpec(memory_space=pltpu.VMEM)
-    hbm = pl.BlockSpec(memory_space=pl.ANY)
+    hbm = pl.BlockSpec(memory_space=pltpu.HBM)
     return pl.pallas_call(
         contract_kernel,
         out_shape=jax.ShapeDtypeStruct((out_slots, tile_edge, rank_width), jnp.float32),
         in_specs=[smem, smem, hbm, hbm, vmem],
-        out_specs=vmem,
+        out_specs=hbm,
         scratch_shapes=[
             pltpu.VMEM((slot_count, tile_edge, depth), jnp.float32),
             pltpu.VMEM((slot_count, tile_edge, rank_width), jnp.float32),
+            pltpu.VMEM((slot_count, tile_edge, rank_width), jnp.float32),
             pltpu.SemaphoreType.DMA((slot_count // PAIR,)),
             pltpu.SemaphoreType.DMA((slot_count,)),
+            pltpu.SemaphoreType.DMA((slot_count,)),
         ],
-        compiler_params=pltpu.CompilerParams(vmem_limit_bytes=28 * 1024 * 1024),
+        compiler_params=pltpu.CompilerParams(vmem_limit_bytes=60 * 1024 * 1024),
         cost_estimate=pl.CostEstimate(
             flops=6 * slot_count * tile_edge * depth * rank_width, bytes_accessed=10_000_000, transcendentals=0
         ),
@@ -144,6 +167,95 @@
         compiler_params=pltpu.CompilerParams(vmem_limit_bytes=16 * 1024 * 1024),
         name="combine",
     )(targets, received, inverse)
+
+
+def invert_four(s):
+    det = s[0][0] * s[1][1] - s[0][1] * s[0][1]
+    over = 1.0 / det
+    a00, a01, a11 = s[1][1] * over, -s[0][1] * over, s[0][0] * over
+    y00 = a00 * s[0][2] + a01 * s[1][2]
+    y01 = a00 * s[0][3] + a01 * s[1][3]
+    y10 = a01 * s[0][2] + a11 * s[1][2]
+    y11 = a01 * s[0][3] + a11 * s[1][3]
+    c00 = s[2][2] - (s[0][2] * y00 + s[1][2] * y10)
+    c01 = s[2][3] - (s[0][2] * y01 + s[1][2] * y11)
+    c11 = s[3][3] - (s[0][3] * y01 + s[1][3] * y11)
+    over = 1.0 / (c00 * c11 - c01 * c01)
+    d00, d01, d11 = c11 * over, -c01 * over, c00 * over
+    e00 = -(y00 * d00 + y01 * d01)
+    e01 = -(y00 * d01 + y01 * d11)
+    e10 = -(y10 * d00 + y11 * d01)
+    e11 = -(y10 * d01 + y11 * d11)
+    b00 = a00 - (e00 * y00 + e01 * y01)
+    b01 = a01 - (e00 * y10 + e01 * y11)
+    b11 = a11 - (e10 * y10 + e11 * y11)
+    return [[b00, b01, e00, e01], [b01, b11, e10, e11], [e00, e10, d00, d01], [e01, e11, d01, d11]]
+
+def invert_block(groups):
+    width = groups[0].shape[1]
+    full = (8, width)
+    lane = lax.broadcasted_iota(jnp.int32, full, 1)
+    sub = lax.broadcasted_iota(jnp.int32, full, 0)
+    for first in range(0, width, 4):
+        at, off = first // 8, first % 8
+        cols = [[jnp.broadcast_to(g[:, first + j : first + j + 1], full) for j in range(4)] for g in groups]
+        s = [[jnp.broadcast_to(cols[at][j][off + i : off + i + 1], full) if i <= j else None for j in range(4)] for i in range(4)]
+        rows = [jnp.broadcast_to(groups[at][off + i : off + i + 1], full) for i in range(4)]
+        d = invert_four(s)
+        new_rows = []
+        for i in range(4):
+            w = d[i][0] * rows[0] + d[i][1] * rows[1] + d[i][2] * rows[2] + d[i][3] * rows[3]
+            for j in range(4):
+                w = jnp.where(lane == first + j, d[i][j], w)
+            new_rows.append(w)
+        in_pivot = (lane >= first) & (lane < first + 4)
+        out = []
+        for k, g in enumerate(groups):
+            v = jnp.where(in_pivot, 0.0, g)
+            v = v - ((cols[k][0] * new_rows[0] + cols[k][1] * new_rows[1]) + (cols[k][2] * new_rows[2] + cols[k][3] * new_rows[3]))
+            if k == at:
+                for i in range(4):
+                    v = jnp.where(sub == off + i, new_rows[i], v)
+            out.append(v)
+        groups = out
+    return groups
+
+def invert_kernel(block, normal_ref, out_ref, work_ref):
+    n = normal_ref.shape[0]
+    normal = normal_ref[...]
+    on_diagonal = lax.broadcasted_iota(jnp.int32, (n, n), 0) == lax.broadcasted_iota(jnp.int32, (n, n), 1)
+    diagonal = jnp.where(on_diagonal, normal, 0.0)
+    scale_row = lax.rsqrt(jnp.sum(diagonal, axis=0, keepdims=True))
+    scale_col = lax.rsqrt(jnp.sum(diagonal, axis=1, keepdims=True))
+    work_ref[...] = normal * scale_col * scale_row
+    for first in range(0, n, block):
+        last = first + block
+        groups = [work_ref[r : r + 8, first:last] for r in range(first, last, 8)]
+        inner = jnp.concatenate(invert_block(groups), axis=0)
+        rows = jnp.dot(inner, work_ref[first:last, :], precision=HIGHEST, preferred_element_type=jnp.float32)
+        pieces = [rows[:, :first]] if first else []
+        pieces.append(inner)
+        if last < n:
+            pieces.append(rows[:, last:])
+        rows = jnp.concatenate(pieces, axis=1)
+        change = jnp.dot(work_ref[:, first:last], rows, precision=HIGHEST, preferred_element_type=jnp.float32)
+        lane = lax.broadcasted_iota(jnp.int32, (n, n), 1)
+        work_ref[...] = jnp.where((lane >= first) & (lane < last), 0.0, work_ref[...]) - change
+        work_ref[first:last, :] = rows
+    out_ref[...] = work_ref[...] * scale_col * scale_row
+
+def invert(normal, block=64):
+    n = normal.shape[0]
+    vmem = pl.BlockSpec(memory_space=pltpu.VMEM)
+    return pl.pallas_call(
+        functools.partial(invert_kernel, block),
+        out_shape=jax.ShapeDtypeStruct((n, n), jnp.float32),
+        in_specs=[vmem], out_specs=vmem,
+        scratch_shapes=[pltpu.VMEM((n, n), jnp.float32)],
+        compiler_params=pltpu.CompilerParams(vmem_limit_bytes=16 * 1024 * 1024),
+        cost_estimate=pl.CostEstimate(flops=12 * n * n * n, bytes_accessed=8 * n * n, transcendentals=0),
+        name="invert",
+    )(normal)
 
 
 def local(
@@ -196,10 +308,12 @@
         second_part = jnp.sum(exchanged, axis=0)
         third_part = lax.dynamic_slice_in_dim(own_third, row_index * part, part, 0)
         sent = jnp.concatenate([second_part, third_part, target_rows], axis=0)
-        spread = lax.all_gather(sent, "col", axis=0)
+        spread = lax.all_to_all(jnp.broadcast_to(sent[None], (n_col,) + sent.shape), "col", 0, 0)
         both = jnp.sum(spread[:, : 2 * part], axis=0)
         normal_part = both[:part] * both[part:]
-        normal_matrix = lax.all_gather(normal_part, "row", axis=0, tiled=True)
+        normal_matrix = lax.all_to_all(
+            jnp.broadcast_to(normal_part[None], (n_row, part, rank_width)), "row", 0, 0
+        ).reshape(rank_width, rank_width)
         received_targets = lax.dynamic_slice_in_dim(spread[:, 2 * part], col_index * SLOTS, SLOTS, 1)
         received_targets = received_targets.astype(jnp.int32).reshape(-1)
 
@@ -218,8 +332,7 @@
         ).reshape(n_col * SLOTS, tile_edge, rank_width)
 
     with jax.named_scope("inverse"):
-        factor = jnp.linalg.cholesky(normal_matrix)
-        inverse = jax.scipy.linalg.cho_solve((factor, True), jnp.eye(rank_width, dtype=jnp.float32))
+        inverse = invert(normal_matrix)
 
     with jax.named_scope("combine"):
         return combine(received_targets, received, inverse)

time: 182 us -> 119 us (0.65)
  other arithmetic: 56.7 us -> 2.19 us
  blocking collectives: 41.3 us -> 0 us
  waiting for transfers between devices: 8.84 us -> 30.9 us
  starting transfers between devices: 18.3 us -> 29.5 us
  Pallas kernels: 22.3 us -> 32.8 us
  local copies, waits for them, and re-layouts: 10.8 us -> 1.92 us
  matrix products: 7.62 us -> 5.49 us
    another operation x10 -> x0, other arithmetic: 53.8 us -> none  [the longest x6 34 us: local(): factor = jnp.linalg.cholesky(normal_matrix)]
    all_gather x2 -> x0, blocking collectives: 41.3 us -> none  [the longest x1 24.8 us: local(): spread = lax.all_gather(sent, 'col', axis=0)]
    pallas_call x0 -> x1, Pallas kernels: none -> 16 us  [invert(): pl.pallas_call(functools.partial(invert_kernel, block), out_shape=jax.Sha...]
    all_to_all x0 -> x2, waiting for transfers between devices: none -> 13.4 us  [the longest x1 13.4 us: local(): lax.all_to_all(jnp.broadcast_to(sent[None], (n_col,) + sent.shape), 'col'...]
    all_to_all x0 -> x2, starting transfers between devices: none -> 13 us  [the longest x1 7.05 us: local(): lax.all_to_all(jnp.broadcast_to(sent[None], (n_col,) + sent.shape), 'col'...]
    all_to_all x1, waiting for transfers between devices: 5.29 us -> 12.5 us  [local(): lax.all_to_all(partials.reshape(n_col, SLOTS * tile_edge, rank_width), 'c...]
    unnamed x8, local copies, waits for them, and re-layouts: 6.32 us -> 0.01 us
    pallas_call x1, Pallas kernels: 19.4 us -> 13.8 us  [contract_tiles(): pl.pallas_call(contract_kernel, out_shape=jax.ShapeDtypeStruct((out_slots...]
  transfers between devices with their start and end apart: 3 -> 5, of which waited for: 2 -> 3; matrix products, arithmetic and copies ran while one was open for 38% -> 8% of each run, Pallas kernels for 0% -> 25%
where the time goes in v2:
time: 119 us; the launch traced here: 117 us
  Pallas kernels  32.8 us (28%)
  waiting for transfers between devices  30.9 us (26%)
  starting transfers between devices  29.5 us (25%)
  between operations  14.2 us (12%)
  matrix products  5.49 us (5%)
  other arithmetic  2.19 us (2%)
  local copies, waits for them, and re-layouts  1.92 us (2%)
    pallas_call x1, Pallas kernels, invert(): pl.pallas_call(functools.partial(invert_kernel, block), out_shape=jax.Sha...  16 us
    pallas_call x1, Pallas kernels, contract_tiles(): pl.pallas_call(contract_kernel, out_shape=jax.ShapeDtypeStruct((out_slots...  13.8 us
    all_to_all x1, waiting for transfers between devices, local(): lax.all_to_all(jnp.broadcast_to(sent[None], (n_col,) + sent.shape), 'col'...  13.4 us
    all_to_all x1, waiting for transfers between devices, local(): lax.all_to_all(partials.reshape(n_col, SLOTS * tile_edge, rank_width), 'c...  12.5 us
    all_to_all x1, starting transfers between devices, local(): lax.all_to_all(own_second.reshape(n_row, part, rank_width), 'row', 0, 0)  8.59 us
    all_to_all x1, starting transfers between devices, local(): lax.all_to_all(partials.reshape(n_col, SLOTS * tile_edge, rank_width), 'c...  7.89 us
    all_to_all x1, starting transfers between devices, local(): lax.all_to_all(jnp.broadcast_to(sent[None], (n_col,) + sent.shape), 'col'...  7.05 us
    all_to_all x1, starting transfers between devices, local(): lax.all_to_all(jnp.broadcast_to(normal_part[None], (n_row, part, rank_wid...  5.99 us
  transfers between devices with their start and end apart: 5, of which 3 were waited for; matrix products, arithmetic and copies ran while one was open for 8% of the time, Pallas kernels for 25%

profile of v2, /device:TPU:32, one launch (start us, length us, event | category | flops | bytes accessed | tf_op | source)
XLA Modules:
  0.0 117.0 jit_solution(3231959215475655629)
XLA Ops:
  6.5 0.0 copy-start.3
  6.5 0.0 copy-start.2
  6.5 0.0 copy-start
  6.5 0.0 copy-start.1
  6.5 0.0 all-gather.2.cloned.1.call-start
  6.6 0.7 all-gather.2.cloned.1.call-update
  7.3 2.4 %fusion.8 = f32[256,256]{1,0:T(8,128)} fusion(f32[256,256]{1,0:T(8,128)} %param.18), kind=kOutput, calls=%fused_computation.25 | convolution fusion | flops 201326592 | bytes 524288 | tf_op jit(solution)/shard_map/normal/dot_general | solution.py:19
  9.6 8.6 %all-to-all-start = ((f32[16,16,256]{2,1,0:T(8,128)}), f32[16,16,256]{2,1,0:T(8,128)S(1)}, u32[]{:S(2)}, u32[]{:S(2)}) async-start(f32[16,16,256]{2,1,0:T(8,128)} %bitcast), calls=%async_computation | async-start | bytes 524288 | tf_op jit(solution)/shard_map/normal/all_to_all | solution.py:307
  18.9 0.7 add_convert_fusion
  19.6 0.7 fusion.2
  20.2 0.9 select_reduce_fusion
  21.1 0.1 multiply_reduce_fusion
  21.2 0.1 copy.10
  21.3 0.1 sub.7
  21.4 2.2 %fusion.9 = f32[256,256]{1,0:T(8,128)S(1)} fusion(f32[512,256]{1,0:T(8,128)} %param.19), kind=kOutput, calls=%fused_computation.26 | convolution fusion | flops 402653184 | bytes 786432 | tf_op jit(solution)/shard_map/normal/dot_general | solution.py:19
  23.6 4.2 %all-to-all-done = f32[16,16,256]{2,1,0:T(8,128)S(1)} async-done(((f32[16,16,256]{2,1,0:T(8,128)}), f32[16,16,256]{2,1,0:T(8,128)S(1)}, u32[]{:S(2)}, u32[]{:S(2)}) %all-to-all-start) | async-done | bytes 262176 | tf_op jit(solution)/shard_map/normal/all_to_all | solution.py:307
  27.9 0.9 broadcast_in_dim.4
  28.8 7.0 %all-to-all-start.1 = ((f32[16,40,256]{2,1,0:T(8,128)}), f32[16,40,256]{2,1,0:T(8,128)S(1)}, u32[]{:S(2)}, u32[]{:S(2)}) async-start(f32[16,40,256]{2,1,0:T(8,128)} %broadcast_in_dim.4), calls=%async_computation.1 | async-start | bytes 1310720 | tf_op jit(solution)/shard_map/normal/all_to_all | solution.py:311
  35.9 0.0 copy-done.2
  35.9 0.0 copy-done
  35.9 0.0 copy-done.1
  35.9 13.4 %all-to-all-done.1 = f32[16,40,256]{2,1,0:T(8,128)S(1)} async-done(((f32[16,40,256]{2,1,0:T(8,128)}), f32[16,40,256]{2,1,0:T(8,128)S(1)}, u32[]{:S(2)}, u32[]{:S(2)}) %all-to-all-start.1) | async-done | bytes 655392 | tf_op jit(solution)/shard_map/normal/all_to_all | solution.py:311
  49.4 0.7 broadcast_in_dim.5
  50.1 6.0 %all-to-all-start.3 = ((f32[16,16,256]{2,1,0:T(8,128)}), f32[16,16,256]{2,1,0:T(8,128)S(1)}, u32[]{:S(2)}, u32[]{:S(2)}) async-start(f32[16,16,256]{2,1,0:T(8,128)} %broadcast_in_dim.5), calls=%async_computation.3 | async-start | bytes 524288 | tf_op jit(solution)/shard_map/normal/all_to_all | solution.py:314
  56.1 0.0 copy-done.3
  56.1 0.6 pad_add_fusion.table_ref
  56.7 0.0 all-gather.2.cloned.1.call-done
  56.7 13.8 %contract.1 = f32[64,32,256]{2,1,0:T(8,128)} custom-call(s32[3,48]{1,0:T(4,128)} %pad_add_fusion.table_ref, s32[1]{0:T(128)} %copy.11.count_ref, f32[48,32,1024]{2,1,0:T(8,128)} %tile_hbm.1, f32[128,32,256]{2,1,0:T(8,128)} %bitcast.31, f32[16,32,256]{2,1,0:T(8,128)} %bitcast.30), custom_call_target="tpu_custom_call" | custom-call | flops 2415919104 | bytes 10000000 | tf_op jit(solution)/shard_map/contract/contract/pallas_call | solution.py:117
  70.5 0.0 all-to-all-done.3
  70.5 7.9 %all-to-all-start.2 = ((f32[16,128,256]{2,1,0:T(8,128)}), f32[16,128,256]{2,1,0:T(8,128)S(1)}, u32[]{:S(2)}, u32[]{:S(2)}) async-start(f32[16,128,256]{2,1,0:T(8,128)} %bitcast.29), calls=%async_computation.2 | async-start | bytes 4194304 | tf_op jit(solution)/shard_map/exchange/all_to_all | solution.py:330
  78.4 0.1 convert_reduce_fusion
  78.5 0.1 convert_element_type.35.target_ref
  78.6 16.0 %invert.1.inverse_ref = f32[256,256]{1,0:T(8,128)S(1)} custom-call(f32[256,256]{1,0:T(8,128)S(1)} %bitcast.28), custom_call_target="tpu_custom_call" | custom-call | flops 201326592 | bytes 524288 | tf_op jit(solution)/shard_map/inverse/invert/pallas_call | solution.py:250
  94.7 12.5 %all-to-all-done.2 = f32[16,128,256]{2,1,0:T(8,128)S(1)} async-done(((f32[16,128,256]{2,1,0:T(8,128)}), f32[16,128,256]{2,1,0:T(8,128)S(1)}, u32[]{:S(2)}, u32[]{:S(2)}) %all-to-all-start.2) | async-done | bytes 2097184 | tf_op jit(solution)/shard_map/exchange/all_to_all | solution.py:330
  107.2 3.0 %combine.1 = f32[512,256]{1,0:T(8,128)} custom-call(s32[64]{0:T(128)S(1)} %convert_element_type.35.target_ref, f32[64,32,256]{2,1,0:T(8,128)S(1)} %bitcast.27, f32[256,256]{1,0:T(8,128)S(1)} %invert.1.inverse_ref), custom_call_target="tpu_custom_call" | custom-call | tf_op jit(solution)/shard_map/combine/combine/pallas_call | solution.py:161
  (10 shorter events, 0.1 us)
Async XLA Ops:
  6.5 49.6 %copy-start.3 = (s32[48,1]{0,1:T(1,128)S(1)}, s32[48,1]{0,1:T(1,128)}, u32[]{:S(2)}) copy-start(s32[48,1]{0,1:T(1,128)} %param.13) | copy-start | bytes 580
  6.5 29.3 %copy-start.2 = (s32[48]{0:T(128)S(1)}, s32[48]{0:T(128)}, u32[]{:S(2)}) copy-start(s32[48]{0:T(128)} %param.17) | copy-start | bytes 580
  6.5 29.3 %copy-start = (s32[48]{0:T(128)S(1)}, s32[48]{0:T(128)}, u32[]{:S(2)}) copy-start(s32[48]{0:T(128)} %param.16) | copy-start | bytes 580
  6.5 29.3 %copy-start.1 = (s32[48,1]{0,1:T(1,128)S(1)}, s32[48,1]{0,1:T(1,128)}, u32[]{:S(2)}) copy-start(s32[48,1]{0,1:T(1,128)} %param.15) | copy-start | bytes 580
  6.5 50.2 %all-gather.2.cloned.1.call-start = ((), (), s32[]{:S(2)}) async-start(), calls=%async_computation.4 | async-start | bytes 4456448 | tf_op jit(solution)/shard_map/gather_second/all_gather | solution.py:281
  9.6 18.2 %all-to-all-start = ((f32[16,16,256]{2,1,0:T(8,128)}), f32[16,16,256]{2,1,0:T(8,128)S(1)}, u32[]{:S(2)}, u32[]{:S(2)}) async-start(f32[16,16,256]{2,1,0:T(8,128)} %bitcast), calls=%async_computation | async-start | bytes 524288 | tf_op jit(solution)/shard_map/normal/all_to_all | solution.py:307
  28.8 20.5 %all-to-all-start.1 = ((f32[16,40,256]{2,1,0:T(8,128)}), f32[16,40,256]{2,1,0:T(8,128)S(1)}, u32[]{:S(2)}, u32[]{:S(2)}) async-start(f32[16,40,256]{2,1,0:T(8,128)} %broadcast_in_dim.4), calls=%async_computation.1 | async-start | bytes 1310720 | tf_op jit(solution)/shard_map/normal/all_to_all | solution.py:311
  50.1 20.4 %all-to-all-start.3 = ((f32[16,16,256]{2,1,0:T(8,128)}), f32[16,16,256]{2,1,0:T(8,128)S(1)}, u32[]{:S(2)}, u32[]{:S(2)}) async-start(f32[16,16,256]{2,1,0:T(8,128)} %broadcast_in_dim.5), calls=%async_computation.3 | async-start | bytes 524288 | tf_op jit(solution)/shard_map/normal/all_to_all | solution.py:314
  70.5 36.7 %all-to-all-start.2 = ((f32[16,128,256]{2,1,0:T(8,128)}), f32[16,128,256]{2,1,0:T(8,128)S(1)}, u32[]{:S(2)}, u32[]{:S(2)}) async-start(f32[16,128,256]{2,1,0:T(8,128)} %bitcast.29), calls=%async_computation.2 | async-start | bytes 4194304 | tf_op jit(solution)/shard_map/exchange/all_to_all | solution.py:330
Sparse Core Ops, SparseCore 0:
  9.2 45.8 all-gather.1

commit v3 on v2

--- a/solution.py
+++ b/solution.py
@@ -31,58 +31,55 @@
     return jnp.dot(left, right, preferred_element_type=jnp.float32)
 
 
-def contract_kernel(
-    table_ref,
-    count_ref,
-    tile_hbm,
-    second_hbm,
-    third_ref,
-    out_hbm,
-    tile_buf,
-    second_buf,
-    result_buf,
-    tile_sem,
-    second_sem,
-    result_sem,
-):
-    count = count_ref[0]
-    pairs = (count + PAIR - 1) // PAIR
+def contract_kernel(table_ref, bound_ref, tile_hbm, own_hbm, other_hbm, third_ref, *rest):
+    out_hbm, tile_buf, second_buf, result_buf, tile_sem, second_sem, result_sem = rest[-7:]
+    low, high = bound_ref[0], bound_ref[1]
+    pairs = (high - low + PAIR - 1) // PAIR
     tile_edge = third_ref.shape[1]
     depth = tile_buf.shape[2]
     chunk = min(256, depth)
     per_chunk = chunk // tile_edge
 
-    def tile_copy(pair):
-        return pltpu.make_async_copy(
-            tile_hbm.at[pl.ds(pair * PAIR, PAIR)], tile_buf.at[pl.ds(pair * PAIR, PAIR)], tile_sem.at[pair]
-        )
-
-    def second_copy(slot):
-        return pltpu.make_async_copy(
-            second_hbm.at[table_ref[0, slot]], second_buf.at[slot], second_sem.at[slot]
-        )
-
-    def result_copy(slot):
-        return pltpu.make_async_copy(result_buf.at[slot], out_hbm.at[table_ref[2, slot]], result_sem.at[slot])
-
-    def start(pair, carry):
-        tile_copy(pair).start()
-        for at in range(PAIR):
-            second_copy(pair * PAIR + at).start()
+    def tile_copy(at):
+        return pltpu.make_async_copy(tile_hbm.at[table_ref[0, at]], tile_buf.at[at], tile_sem.at[at])
+
+    def second_copy(source, at):
+        return pltpu.make_async_copy(source.at[table_ref[1, at]], second_buf.at[at], second_sem.at[at])
+
+    def result_copy(at):
+        return pltpu.make_async_copy(result_buf.at[at], out_hbm.at[table_ref[3, at]], result_sem.at[at])
+
+    def start(at, carry):
+        tile_copy(at).start()
+        other = table_ref[4, at]
+
+        @pl.when(other == 0)
+        def _():
+            second_copy(own_hbm, at).start()
+
+        @pl.when(other != 0)
+        def _():
+            second_copy(other_hbm, at).start()
+
         return carry
 
-    lax.fori_loop(0, pairs, start, 0)
+    lax.fori_loop(low, high, start, 0)
 
     def contract(pair, carry):
-        tile_copy(pair).wait()
-        for at in range(PAIR):
-            second_copy(pair * PAIR + at).wait()
-        for at in range(PAIR):
-            slot = pair * PAIR + at
-            second = second_buf[slot]
-            third = third_ref[table_ref[1, slot]]
-            high, low = split(tile_buf[slot])
-            both = jnp.concatenate([high, low], axis=0)
+        first = low + pair * PAIR
+        for u in range(PAIR):
+
+            @pl.when(first + u < high)
+            def _():
+                tile_copy(first + u).wait()
+                second_copy(own_hbm, first + u).wait()
+
+        for u in range(PAIR):
+            at = jnp.minimum(first + u, high - 1)
+            second = second_buf[at]
+            third = third_ref[table_ref[2, at]]
+            high_part, low_part = split(tile_buf[at])
+            both = jnp.concatenate([high_part, low_part], axis=0)
             total = jnp.zeros((2 * tile_edge, third.shape[1]), jnp.float32)
             total_low = jnp.zeros((tile_edge, third.shape[1]), jnp.float32)
             for q in range(depth // chunk):
@@ -90,49 +87,52 @@
                 khatri = (rows[:, None, :] * third[None, :, :]).reshape(chunk, third.shape[1])
                 khatri_high, khatri_low = split(khatri)
                 total = total + dot32(both[:, q * chunk : (q + 1) * chunk], khatri_high)
-                total_low = total_low + dot32(high[:, q * chunk : (q + 1) * chunk], khatri_low)
-            result_buf[slot] = total[:tile_edge] + (total[tile_edge:] + total_low)
-
-            @pl.when(slot < count)
+                total_low = total_low + dot32(high_part[:, q * chunk : (q + 1) * chunk], khatri_low)
+            result = total[:tile_edge] + (total[tile_edge:] + total_low)
+
+            @pl.when(first + u < high)
             def _():
-                result_copy(slot).start()
+                result_buf[first + u] = result
+                result_copy(first + u).start()
 
         return carry
 
     lax.fori_loop(0, pairs, contract, 0)
 
-    def finish(slot, carry):
-        result_copy(slot).wait()
+    def finish(at, carry):
+        result_copy(at).wait()
         return carry
 
-    lax.fori_loop(0, count, finish, 0)
-
-
-def contract_tiles(table, count, tile_values, second_blocks, third_blocks, out_slots):
+    lax.fori_loop(low, high, finish, 0)
+
+
+def contract_tiles(table, bounds, tile_values, own_blocks, other_blocks, third_blocks, out_slots, earlier=()):
     slot_count, tile_edge, depth = tile_values.shape
     rank_width = third_blocks.shape[2]
     smem = pl.BlockSpec(memory_space=pltpu.SMEM)
     vmem = pl.BlockSpec(memory_space=pltpu.VMEM)
     hbm = pl.BlockSpec(memory_space=pltpu.HBM)
+    block = (slot_count, tile_edge, rank_width)
     return pl.pallas_call(
         contract_kernel,
         out_shape=jax.ShapeDtypeStruct((out_slots, tile_edge, rank_width), jnp.float32),
-        in_specs=[smem, smem, hbm, hbm, vmem],
+        in_specs=[smem, smem, hbm, hbm, hbm, vmem] + [hbm] * len(earlier),
         out_specs=hbm,
         scratch_shapes=[
             pltpu.VMEM((slot_count, tile_edge, depth), jnp.float32),
-            pltpu.VMEM((slot_count, tile_edge, rank_width), jnp.float32),
-            pltpu.VMEM((slot_count, tile_edge, rank_width), jnp.float32),
-            pltpu.SemaphoreType.DMA((slot_count // PAIR,)),
+            pltpu.VMEM(block, jnp.float32),
+            pltpu.VMEM(block, jnp.float32),
+            pltpu.SemaphoreType.DMA((slot_count,)),
             pltpu.SemaphoreType.DMA((slot_count,)),
             pltpu.SemaphoreType.DMA((slot_count,)),
         ],
+        input_output_aliases={6: 0} if earlier else {},
         compiler_params=pltpu.CompilerParams(vmem_limit_bytes=60 * 1024 * 1024),
         cost_estimate=pl.CostEstimate(
-            flops=6 * slot_count * tile_edge * depth * rank_width, bytes_accessed=10_000_000, transcendentals=0
+            flops=3 * slot_count * tile_edge * depth * rank_width, bytes_accessed=5_000_000, transcendentals=0
         ),
         name="contract",
-    )(table, count, tile_values, second_blocks, third_blocks)
+    )(table, bounds, tile_values, own_blocks, other_blocks, third_blocks, *earlier)
 
 
 def combine_kernel(target_ref, received_ref, inverse_ref, out_ref, total_ref):
@@ -277,34 +277,72 @@
     n_col = lax.axis_size("col")
     part = rank_width // n_row
 
+    with jax.named_scope("normal"):
+        own_second = gram_of(mode2_factor)
+        exchanged = lax.all_to_all(own_second.reshape(n_row, part, rank_width), "row", 0, 0)
+
     with jax.named_scope("gather_second"):
-        gathered = lax.all_gather(mode2_factor, "row", axis=0, tiled=True)
+        n_z = n_row // 2
+
+        def moved(shift):
+            pairs = [(i, 2 * ((i // 2 + shift) % n_z) + i % 2) for i in range(n_row)]
+            return lax.ppermute(mode2_factor, "row", pairs)
+
+        near = [1, n_z - 1, 2, n_z - 2]
+        far = [3, n_z - 3, 4]
+        twin = [(i, i ^ 1) for i in range(n_row)]
+        near_own = jnp.concatenate([mode2_factor] + [moved(shift) for shift in near], axis=0)
+        far_own = jnp.concatenate([moved(shift) for shift in far], axis=0)
+        near_other = lax.ppermute(near_own, "row", twin)
+        far_other = lax.ppermute(far_own, "row", twin)
 
     with jax.named_scope("tables"):
         slot_index = jnp.arange(slot_count, dtype=jnp.int32)
-        is_live = slot_index < tile_count[0]
+        live_count = tile_count[0]
+        is_live = slot_index < live_count
         chosen = (mode1_column[:, 0][None, :] == jnp.arange(n_col, dtype=jnp.int32)[:, None]) & is_live[None, :]
         chosen = chosen.astype(jnp.float32)
         earlier = (slot_index[:, None] < slot_index[None, :]).astype(jnp.float32)
         rank = jnp.dot(chosen, earlier)
         own_rank = jnp.sum(chosen * rank, axis=0).astype(jnp.int32)
         out_slot = jnp.clip(mode1_column[:, 0], 0, n_col - 1) * SLOTS + own_rank
+        source = jnp.clip(mode2_row[:, 0], 0, n_row - 1)
+        shift = (row_index // 2 - source // 2 + n_z) % n_z
+        place_of = [0] * n_z
+        for at, each in enumerate([0] + near):
+            place_of[each] = at
+        for at, each in enumerate(far):
+            place_of[each] = at
+        place = sum(jnp.where(shift == each, place_of[each], 0) for each in range(n_z))
+        is_far = (shift > 2) & (shift < n_z - 2)
+        is_other = (source % 2 != row_index % 2).astype(jnp.int32)
+        group = jnp.where(is_live, is_far.astype(jnp.int32), 2)
+        before = (group[:, None] < group[None, :]) | (
+            (group[:, None] == group[None, :]) & (slot_index[:, None] < slot_index[None, :])
+        )
+        position = jnp.sum(before.astype(jnp.int32), axis=0)
         table = jnp.stack(
             [
-                jnp.clip(mode2_row[:, 0] * JB_DEV + mode2_offset, 0, gathered.shape[0] // tile_edge - 1),
+                slot_index,
+                place * JB_DEV + jnp.clip(mode2_offset, 0, JB_DEV - 1),
                 jnp.clip(mode3_offset, 0, mode3_factor.shape[0] // tile_edge - 1),
                 out_slot,
+                is_other,
             ]
+        )
+        table = jnp.sum(
+            jnp.where(position[None, :, None] == slot_index[None, None, :], table[:, :, None], 0), axis=1
         ).astype(jnp.int32)
-        place = jnp.arange(SLOTS, dtype=jnp.float32)
-        taken = chosen[:, None, :] * (rank[:, None, :] == place[None, :, None])
+        near_count = jnp.sum((group == 0).astype(jnp.int32))
+        near_bounds = jnp.stack([jnp.int32(0), near_count]).astype(jnp.int32)
+        far_bounds = jnp.stack([near_count, live_count]).astype(jnp.int32)
+        slots = jnp.arange(SLOTS, dtype=jnp.float32)
+        taken = chosen[:, None, :] * (rank[:, None, :] == slots[None, :, None])
         targets = jnp.sum(taken * (mode1_offset + 1).astype(jnp.float32), axis=2) - 1.0
         target_rows = jnp.zeros((8, rank_width), jnp.float32).at[0, : n_col * SLOTS].set(targets.reshape(-1))
 
     with jax.named_scope("normal"):
-        own_second = gram_of(mode2_factor)
         own_third = gram_of(mode3_factor)
-        exchanged = lax.all_to_all(own_second.reshape(n_row, part, rank_width), "row", 0, 0)
         second_part = jnp.sum(exchanged, axis=0)
         third_part = lax.dynamic_slice_in_dim(own_third, row_index * part, part, 0)
         sent = jnp.concatenate([second_part, third_part, target_rows], axis=0)
@@ -318,13 +356,17 @@
         received_targets = received_targets.astype(jnp.int32).reshape(-1)
 
     with jax.named_scope("contract"):
+        third_blocks = mode3_factor.reshape(-1, tile_edge, rank_width)
+
+        def blocks(array):
+            return array.reshape(-1, tile_edge, rank_width)
+
+        out_slots = n_col * SLOTS
+        near_done = contract_tiles(
+            table, near_bounds, tile_values, blocks(near_own), blocks(near_other), third_blocks, out_slots
+        )
         partials = contract_tiles(
-            table,
-            tile_count,
-            tile_values,
-            gathered.reshape(-1, tile_edge, rank_width),
-            mode3_factor.reshape(-1, tile_edge, rank_width),
-            n_col * SLOTS,
+            table, far_bounds, tile_values, blocks(far_own), blocks(far_other), third_blocks, out_slots, (near_done,)
         )
     with jax.named_scope("exchange"):
         received = lax.all_to_all(

time: 119 us -> 153 us (1.29)
  starting transfers between devices: 29.5 us -> 48.7 us
  waiting for transfers between devices: 30.9 us -> 46.9 us
  between operations: 14.2 us -> 1.07 us
  Pallas kernels: 32.8 us -> 42.4 us
  other arithmetic: 2.19 us -> 6.17 us
    ppermute x0 -> x9, starting transfers between devices: none -> 20.8 us  [the longest x7 19.3 us: moved(): return lax.ppermute(mode2_factor, 'row', pairs)]
    all_to_all x1, waiting for transfers between devices: 4.23 us -> 21.9 us  [local(): lax.all_to_all(own_second.reshape(n_row, part, rank_width), 'row', 0, 0)]
    pallas_call x1 -> x2, Pallas kernels: 13.8 us -> 23.4 us  [contract_tiles(): pl.pallas_call(contract_kernel, out_shape=jax.ShapeDtypeStruct((out_slots...]
    all_to_all x1, starting transfers between devices: 8.59 us -> 3.43 us  [local(): lax.all_to_all(own_second.reshape(n_row, part, rank_width), 'row', 0, 0)]
    all_to_all x1, starting transfers between devices: 5.99 us -> 10.2 us  [local(): lax.all_to_all(jnp.broadcast_to(normal_part[None], (n_row, part, rank_wid...]
    all_to_all x1, waiting for transfers between devices: 13.4 us -> 10.4 us  [local(): lax.all_to_all(jnp.broadcast_to(sent[None], (n_col,) + sent.shape), 'col'...]
    another operation x2 -> x3, other arithmetic: 0.59 us -> 3.1 us  [the longest x1 1.28 us: local(): far_bounds = jnp.stack([near_count, live_count]).astype(jnp.int32)]
    all_to_all x1, waiting for transfers between devices: 12.5 us -> 14.5 us  [local(): lax.all_to_all(partials.reshape(n_col, SLOTS * tile_edge, rank_width), 'c...]
  transfers between devices with their start and end apart: 5 -> 13, of which waited for: 3 -> 3; matrix products, arithmetic and copies ran while one was open for 8% -> 9% of each run, Pallas kernels for 25% -> 26%
where the time goes in v3:
time: 153 us; the launch traced here: 152 us
  starting transfers between devices  48.7 us (32%)
  waiting for transfers between devices  46.9 us (31%)
  Pallas kernels  42.4 us (28%)
  other arithmetic  6.17 us (4%)
  matrix products  4.12 us (3%)
  local copies, waits for them, and re-layouts  3.08 us (2%)
    pallas_call x2, Pallas kernels, contract_tiles(): pl.pallas_call(contract_kernel, out_shape=jax.ShapeDtypeStruct((out_slots...  23.4 us
    all_to_all x1, waiting for transfers between devices, local(): lax.all_to_all(own_second.reshape(n_row, part, rank_width), 'row', 0, 0)  21.9 us
    ppermute x7, starting transfers between devices, moved(): return lax.ppermute(mode2_factor, 'row', pairs)  19.3 us
    pallas_call x1, Pallas kernels, invert(): pl.pallas_call(functools.partial(invert_kernel, block), out_shape=jax.Sha...  16 us
    all_to_all x1, waiting for transfers between devices, local(): lax.all_to_all(partials.reshape(n_col, SLOTS * tile_edge, rank_width), 'c...  14.5 us
    all_to_all x1, waiting for transfers between devices, local(): lax.all_to_all(jnp.broadcast_to(sent[None], (n_col,) + sent.shape), 'col'...  10.4 us
    all_to_all x1, starting transfers between devices, local(): lax.all_to_all(jnp.broadcast_to(normal_part[None], (n_row, part, rank_wid...  10.2 us
    all_to_all x1, starting transfers between devices, local(): lax.all_to_all(partials.reshape(n_col, SLOTS * tile_edge, rank_width), 'c...  7.26 us
  transfers between devices with their start and end apart: 13, of which 3 were waited for; matrix products, arithmetic and copies ran while one was open for 9% of the time, Pallas kernels for 26%

profile of v3, /device:TPU:32, one launch (start us, length us, event | category | flops | bytes accessed | tf_op | source)
XLA Modules:
  0.0 152.4 jit_solution(2635723044380318843)
XLA Ops:
  0.0 0.0 copy-start
  0.1 2.0 %collective-permute-start.4 = (f32[256,256]{1,0:T(8,128)}, f32[256,256]{1,0:T(8,128)S(1)}, u32[]{:S(2)}, u32[]{:S(2)}) collective-permute-start(f32[256,256]{1,0:T(8,128)} %param.18), channel_id=1, source_target_pairs={{0,32},{16,48},{32,64},{48,80},{64,96},{80,112},{96,128},{112,144}... | collective-permute-start | bytes 786440 | tf_op jit(solution)/shard_map/gather_second/ppermute | solution.py:289
  2.0 0.1 collective-permute-start.5
  2.2 4.4 %collective-permute-start.6 = (f32[256,256]{1,0:T(8,128)}, f32[256,256]{1,0:T(8,128)S(1)}, u32[]{:S(2)}, u32[]{:S(2)}) collective-permute-start(f32[256,256]{1,0:T(8,128)} %param.18), channel_id=1, source_target_pairs={{0,64},{16,80},{32,96},{48,112},{64,128},{80,144},{96,160},{112,17... | collective-permute-start | bytes 786440 | tf_op jit(solution)/shard_map/gather_second/ppermute | solution.py:289
  6.5 1.0 collective-permute-start.7
  7.6 5.8 %collective-permute-start = (f32[256,256]{1,0:T(8,128)}, f32[256,256]{1,0:T(8,128)S(1)}, u32[]{:S(2)}, u32[]{:S(2)}) collective-permute-start(f32[256,256]{1,0:T(8,128)} %param.18), channel_id=1, source_target_pairs={{0,96},{16,112},{32,128},{48,144},{64,160},{80,176},{96,192},{112,... | collective-permute-start | bytes 786440 | tf_op jit(solution)/shard_map/gather_second/ppermute | solution.py:289
  13.3 2.4 %fusion.23 = f32[256,256]{1,0:T(8,128)} fusion(f32[256,256]{1,0:T(8,128)} %param.18), kind=kOutput, calls=%fused_computation.80 | convolution fusion | flops 201326592 | bytes 524288 | tf_op jit(solution)/shard_map/normal/dot_general | solution.py:19
  15.7 3.4 %all-to-all-start = ((f32[16,16,256]{2,1,0:T(8,128)}), f32[16,16,256]{2,1,0:T(8,128)S(1)}, u32[]{:S(2)}, u32[]{:S(2)}) async-start(f32[16,16,256]{2,1,0:T(8,128)} %bitcast), calls=%async_computation | async-start | bytes 524288 | tf_op jit(solution)/shard_map/normal/all_to_all | solution.py:282
  19.8 0.7 select_reduce_fusion.1
  20.6 0.7 fusion.16
  21.3 0.1 convert_reduce_fusion
  21.4 0.1 iota_compare_fusion.2
  21.5 1.0 fusion.24
  22.5 0.1 multiply_reduce_fusion
  22.6 0.5 clamp_bitcast_fusion
  23.2 0.1 copy.11
  23.3 0.1 sub.34
  23.4 3.5 %collective-permute-start.1 = (f32[256,256]{1,0:T(8,128)S(1)}, f32[256,256]{1,0:T(8,128)}, u32[]{:S(2)}, u32[]{:S(2)}) collective-permute-start(f32[256,256]{1,0:T(8,128)S(1)} %copy-done.1), channel_id=1, source_target_pairs={{0,160},{16,176},{32,192},{48,208},{64,224},{80,240},{96,0},{112,1... | collective-permute-start | bytes 786440 | tf_op jit(solution)/shard_map/gather_second/ppermute | solution.py:289
  27.0 0.0 collective-permute-done.5
  27.0 2.4 %collective-permute-start.2 = (f32[256,256]{1,0:T(8,128)S(1)}, f32[256,256]{1,0:T(8,128)S(1)}, u32[]{:S(2)}, u32[]{:S(2)}) collective-permute-start(f32[256,256]{1,0:T(8,128)S(1)} %copy-done.1), channel_id=1, source_target_pairs={{0,128},{16,144},{32,160},{48,176},{64,192},{80,208},{96,224},{112... | collective-permute-start | bytes 786440 | tf_op jit(solution)/shard_map/gather_second/ppermute | solution.py:289
  29.4 0.0 collective-permute-done.6
  29.5 0.0 copy-start.9
  29.5 0.1 collective-permute-start.8
  29.6 21.9 %all-to-all-done = f32[16,16,256]{2,1,0:T(8,128)S(1)} async-done(((f32[16,16,256]{2,1,0:T(8,128)}), f32[16,16,256]{2,1,0:T(8,128)S(1)}, u32[]{:S(2)}, u32[]{:S(2)}) %all-to-all-start) | async-done | bytes 262176 | tf_op jit(solution)/shard_map/normal/all_to_all | solution.py:282
  51.6 0.9 broadcast_in_dim.72
  52.5 7.0 %all-to-all-start.1 = ((f32[16,40,256]{2,1,0:T(8,128)}), f32[16,40,256]{2,1,0:T(8,128)S(1)}, u32[]{:S(2)}, u32[]{:S(2)}) async-start(f32[16,40,256]{2,1,0:T(8,128)} %broadcast_in_dim.72), calls=%async_computation.1 | async-start | bytes 1310720 | tf_op jit(solution)/shard_map/normal/all_to_all | solution.py:349
  59.6 0.6 bitcast_add_fusion
  60.2 0.6 compare_convert_fusion.1
  60.8 0.0 collective-permute-done.1
  60.8 1.0 constant_dynamic-update-slice_fusion.1
  61.8 0.0 collective-permute-done.2
  61.8 1.4 collective-permute-start.3
  63.3 10.4 %all-to-all-done.1 = f32[16,40,256]{2,1,0:T(8,128)S(1)} async-done(((f32[16,40,256]{2,1,0:T(8,128)}), f32[16,40,256]{2,1,0:T(8,128)S(1)}, u32[]{:S(2)}, u32[]{:S(2)}) %all-to-all-start.1) | async-done | bytes 655392 | tf_op jit(solution)/shard_map/normal/all_to_all | solution.py:349
  73.7 0.7 broadcast_in_dim.77
  74.5 10.2 %all-to-all-start.3 = ((f32[16,16,256]{2,1,0:T(8,128)}), f32[16,16,256]{2,1,0:T(8,128)S(1)}, u32[]{:S(2)}, u32[]{:S(2)}) async-start(f32[16,16,256]{2,1,0:T(8,128)} %broadcast_in_dim.77), calls=%async_computation.3 | async-start | bytes 524288 | tf_op jit(solution)/shard_map/normal/all_to_all | solution.py:352
  84.7 1.3 pad_add_fusion.bound_ref
  86.0 1.3 pad_add_fusion.1.bound_ref
  87.3 0.7 select_reduce_fusion.table_ref
  88.0 0.0 collective-permute-done.8
  88.0 13.6 %contract.2.rest_0_ = f32[64,32,256]{2,1,0:T(8,128)} custom-call(s32[5,48]{1,0:T(8,128)} %select_reduce_fusion.table_ref, s32[2]{0:T(128)} %pad_add_fusion.1.bound_ref, f32[48,32,1024]{2,1,0:T(8,128)} %tile_hbm.3, f32[40,32,256]{2,1,0:T(8,128)} %bitcast.47, f32[40,32,256]{2,1,0:T(8,128)} %bitcast.15.other_hbm, f32[16,32,256]{2,1,0:T(8,128)} %bitcast.45), custom_call_target="tpu_custom_call" | custom-call | flops 1207959552 | bytes 5000000 | tf_op jit(solution)/shard_map/contract/contract/pallas_call | solution.py:116
  101.6 0.0 collective-permute-done.3
  101.6 9.8 %contract.3 = f32[64,32,256]{2,1,0:T(8,128)} custom-call(s32[5,48]{1,0:T(8,128)} %select_reduce_fusion.table_ref, s32[2]{0:T(128)} %pad_add_fusion.bound_ref, f32[48,32,1024]{2,1,0:T(8,128)} %tile_hbm.3, f32[24,32,256]{2,1,0:T(8,128)} %bitcast.48, f32[24,32,256]{2,1,0:T(8,128)} %bitcast.12.other_hbm, ...), custom_call_target="tpu_custom_call", output_to_operand_aliasing={{}: (6, {})} | custom-call | flops 1207959552 | bytes 5000000 | tf_op jit(solution)/shard_map/contract/contract/pallas_call | solution.py:116
  111.4 7.3 %all-to-all-start.2 = ((f32[16,128,256]{2,1,0:T(8,128)}), f32[16,128,256]{2,1,0:T(8,128)S(1)}, u32[]{:S(2)}, u32[]{:S(2)}) async-start(f32[16,128,256]{2,1,0:T(8,128)} %bitcast.44), calls=%async_computation.2 | async-start | bytes 4194304 | tf_op jit(solution)/shard_map/exchange/all_to_all | solution.py:372
  118.7 0.1 convert_reduce_fusion.1
  118.8 0.1 convert_element_type.61.target_ref
  118.9 16.0 %invert.1.inverse_ref = f32[256,256]{1,0:T(8,128)S(1)} custom-call(f32[256,256]{1,0:T(8,128)S(1)} %bitcast.43), custom_call_target="tpu_custom_call" | custom-call | flops 201326592 | bytes 524288 | tf_op jit(solution)/shard_map/inverse/invert/pallas_call | solution.py:250
  134.9 14.5 %all-to-all-done.2 = f32[16,128,256]{2,1,0:T(8,128)S(1)} async-done(((f32[16,128,256]{2,1,0:T(8,128)}), f32[16,128,256]{2,1,0:T(8,128)S(1)}, u32[]{:S(2)}, u32[]{:S(2)}) %all-to-all-start.2) | async-done | bytes 2097184 | tf_op jit(solution)/shard_map/exchange/all_to_all | solution.py:372
  149.4 2.9 %combine.1 = f32[512,256]{1,0:T(8,128)} custom-call(s32[64]{0:T(128)S(1)} %convert_element_type.61.target_ref, f32[64,32,256]{2,1,0:T(8,128)S(1)} %bitcast.42, f32[256,256]{1,0:T(8,128)S(1)} %invert.1.inverse_ref), custom_call_target="tpu_custom_call" | custom-call | tf_op jit(solution)/shard_map/combine/combine/pallas_call | solution.py:161
  (50 shorter events, 0.4 us)
Async XLA Ops:
  0.0 23.2 %copy-start.1 = (f32[256,256]{1,0:T(8,128)S(1)}, f32[256,256]{1,0:T(8,128)}, u32[]{:S(2)}) copy-start(f32[256,256]{1,0:T(8,128)} %param.18) | copy-start | bytes 786436
  0.0 19.8 %copy-start.8 = (s32[48,1]{0,1:T(1,128)S(1)}, s32[48,1]{0,1:T(1,128)}, u32[]{:S(2)}) copy-start(s32[48,1]{0,1:T(1,128)} %param.13) | copy-start | bytes 580
  0.0 20.6 %copy-start.4 = (s32[48,1]{0,1:T(1,128)S(1)}, s32[48,1]{0,1:T(1,128)}, u32[]{:S(2)}) copy-start(s32[48,1]{0,1:T(1,128)} %param.15) | copy-start | bytes 580
  0.0 21.5 %copy-start = (f32[512,256]{1,0:T(8,128)S(1)}, f32[512,256]{1,0:T(8,128)}, u32[]{:S(2)}) copy-start(f32[512,256]{1,0:T(8,128)} %param.19) | copy-start | bytes 1572868
  0.0 22.5 %copy-start.12 = (s32[48]{0:T(128)S(1)}, s32[48]{0:T(128)}, u32[]{:S(2)}) copy-start(s32[48]{0:T(128)} %param.14) | copy-start | bytes 580
  0.0 22.6 %copy-start.7 = (s32[48]{0:T(128)S(1)}, s32[48]{0:T(128)}, u32[]{:S(2)}) copy-start(s32[48]{0:T(128)} %param.16) | copy-start | bytes 580
  0.0 22.6 %copy-start.6 = (s32[48]{0:T(128)S(1)}, s32[48]{0:T(128)}, u32[]{:S(2)}) copy-start(s32[48]{0:T(128)} %param.17) | copy-start | bytes 580
  0.1 23.3 %collective-permute-start.4 = (f32[256,256]{1,0:T(8,128)}, f32[256,256]{1,0:T(8,128)S(1)}, u32[]{:S(2)}, u32[]{:S(2)}) collective-permute-start(f32[256,256]{1,0:T(8,128)} %param.18), channel_id=1, source_target_pairs={{0,32},{16,48},{32,64},{48,80},{64,96},{80,112},{96,128},{112,144}... | collective-permute-start | bytes 786440 | tf_op jit(solution)/shard_map/gather_second/ppermute | solution.py:289
  2.0 24.9 %collective-permute-start.5 = (f32[256,256]{1,0:T(8,128)}, f32[256,256]{1,0:T(8,128)S(1)}, u32[]{:S(2)}, u32[]{:S(2)}) collective-permute-start(f32[256,256]{1,0:T(8,128)} %param.18), channel_id=1, source_target_pairs={{0,224},{16,240},{32,0},{48,16},{64,32},{80,48},{96,64},{112,80},{... | collective-permute-start | bytes 786440 | tf_op jit(solution)/shard_map/gather_second/ppermute | solution.py:289
  2.2 27.3 %collective-permute-start.6 = (f32[256,256]{1,0:T(8,128)}, f32[256,256]{1,0:T(8,128)S(1)}, u32[]{:S(2)}, u32[]{:S(2)}) collective-permute-start(f32[256,256]{1,0:T(8,128)} %param.18), channel_id=1, source_target_pairs={{0,64},{16,80},{32,96},{48,112},{64,128},{80,144},{96,160},{112,17... | collective-permute-start | bytes 786440 | tf_op jit(solution)/shard_map/gather_second/ppermute | solution.py:289
  6.5 22.9 %collective-permute-start.7 = (f32[256,256]{1,0:T(8,128)}, f32[256,256]{1,0:T(8,128)S(1)}, u32[]{:S(2)}, u32[]{:S(2)}) collective-permute-start(f32[256,256]{1,0:T(8,128)} %param.18), channel_id=1, source_target_pairs={{0,192},{16,208},{32,224},{48,240},{64,0},{80,16},{96,32},{112,48}... | collective-permute-start | bytes 786440 | tf_op jit(solution)/shard_map/gather_second/ppermute | solution.py:289
  7.6 53.2 %collective-permute-start = (f32[256,256]{1,0:T(8,128)}, f32[256,256]{1,0:T(8,128)S(1)}, u32[]{:S(2)}, u32[]{:S(2)}) collective-permute-start(f32[256,256]{1,0:T(8,128)} %param.18), channel_id=1, source_target_pairs={{0,96},{16,112},{32,128},{48,144},{64,160},{80,176},{96,192},{112,... | collective-permute-start | bytes 786440 | tf_op jit(solution)/shard_map/gather_second/ppermute | solution.py:289
  15.7 35.9 %all-to-all-start = ((f32[16,16,256]{2,1,0:T(8,128)}), f32[16,16,256]{2,1,0:T(8,128)S(1)}, u32[]{:S(2)}, u32[]{:S(2)}) async-start(f32[16,16,256]{2,1,0:T(8,128)} %bitcast), calls=%async_computation | async-start | bytes 524288 | tf_op jit(solution)/shard_map/normal/all_to_all | solution.py:282
  23.4 37.4 %collective-permute-start.1 = (f32[256,256]{1,0:T(8,128)S(1)}, f32[256,256]{1,0:T(8,128)}, u32[]{:S(2)}, u32[]{:S(2)}) collective-permute-start(f32[256,256]{1,0:T(8,128)S(1)} %copy-done.1), channel_id=1, source_target_pairs={{0,160},{16,176},{32,192},{48,208},{64,224},{80,240},{96,0},{112,1... | collective-permute-start | bytes 786440 | tf_op jit(solution)/shard_map/gather_second/ppermute | solution.py:289
  27.0 34.8 %collective-permute-start.2 = (f32[256,256]{1,0:T(8,128)S(1)}, f32[256,256]{1,0:T(8,128)S(1)}, u32[]{:S(2)}, u32[]{:S(2)}) collective-permute-start(f32[256,256]{1,0:T(8,128)S(1)} %copy-done.1), channel_id=1, source_target_pairs={{0,128},{16,144},{32,160},{48,176},{64,192},{80,208},{96,224},{112... | collective-permute-start | bytes 786440 | tf_op jit(solution)/shard_map/gather_second/ppermute | solution.py:289
  29.5 31.3 %copy-start.2 = (f32[1280,256]{1,0:T(8,128)}, f32[1280,256]{1,0:T(8,128)S(1)}, u32[]{:S(2)}) copy-start(f32[1280,256]{1,0:T(8,128)S(1)} %constant_dynamic-update-slice_fusion.3) | copy-start | bytes 3932164
  29.5 30.0 %copy-start.9 = (s32[48,1]{0,1:T(1,128)S(1)}, s32[48,1]{0,1:T(1,128)}, u32[]{:S(2)}) copy-start(s32[48,1]{0,1:T(1,128)} %param.13) | copy-start | bytes 580
  29.5 30.0 %copy-start.13 = (f32[48]{0:T(128)S(1)}, f32[48]{0:T(128)}, u32[]{:S(2)}) copy-start(f32[48]{0:T(128)} %get-tuple-element.20) | copy-start | bytes 580
  29.5 58.4 %collective-permute-start.8 = (f32[1280,256]{1,0:T(8,128)S(1)}, f32[1280,256]{1,0:T(8,128)}, u32[]{:S(2)}, u32[]{:S(2)}) collective-permute-start(f32[1280,256]{1,0:T(8,128)S(1)} %constant_dynamic-update-slice_fusion.3), channel_id=1, source_target_pairs={{0,16},{16,0},{32,48},{48,32},{64,80},{80,64},{96,112},{112,96},{1... | collective-permute-start | bytes 3932168 | tf_op jit(solution)/shard_map/gather_second/ppermute | solution.py:296
  52.5 21.2 %all-to-all-start.1 = ((f32[16,40,256]{2,1,0:T(8,128)}), f32[16,40,256]{2,1,0:T(8,128)S(1)}, u32[]{:S(2)}, u32[]{:S(2)}) async-start(f32[16,40,256]{2,1,0:T(8,128)} %broadcast_in_dim.72), calls=%async_computation.1 | async-start | bytes 1310720 | tf_op jit(solution)/shard_map/normal/all_to_all | solution.py:349
  60.8 25.2 %copy-start.5 = (s32[1,48]{1,0:T(1,128)S(1)}, s32[1,48]{1,0:T(1,128)}, u32[]{:S(2)}) copy-start(s32[1,48]{1,0:T(1,128)} %get-tuple-element.23) | copy-start | bytes 580
  60.8 25.2 %copy-start.10 = (s32[1,48]{1,0:T(1,128)S(1)}, s32[1,48]{1,0:T(1,128)}, u32[]{:S(2)}) copy-start(s32[1,48]{1,0:T(1,128)} %bitcast_add_fusion) | copy-start | bytes 580
  60.8 25.1 %copy-start.11 = (s32[1,48]{1,0:T(1,128)S(1)}, s32[1,48]{1,0:T(1,128)}, u32[]{:S(2)}) copy-start(s32[1,48]{1,0:T(1,128)} %compare_convert_fusion.1) | copy-start | bytes 580
  61.8 39.7 %copy-start.3 = (f32[768,256]{1,0:T(8,128)}, f32[768,256]{1,0:T(8,128)S(1)}, u32[]{:S(2)}) copy-start(f32[768,256]{1,0:T(8,128)S(1)} %constant_dynamic-update-slice_fusion) | copy-start | bytes 2359300
  61.8 39.7 %collective-permute-start.3 = (f32[768,256]{1,0:T(8,128)S(1)}, f32[768,256]{1,0:T(8,128)}, u32[]{:S(2)}, u32[]{:S(2)}) collective-permute-start(f32[768,256]{1,0:T(8,128)S(1)} %constant_dynamic-update-slice_fusion), channel_id=1, source_target_pairs={{0,16},{16,0},{32,48},{48,32},{64,80},{80,64},{96,112},{112,96},{1... | collective-permute-start | bytes 2359304 | tf_op jit(solution)/shard_map/gather_second/ppermute | solution.py:297
  74.5 36.9 %all-to-all-start.3 = ((f32[16,16,256]{2,1,0:T(8,128)}), f32[16,16,256]{2,1,0:T(8,128)S(1)}, u32[]{:S(2)}, u32[]{:S(2)}) async-start(f32[16,16,256]{2,1,0:T(8,128)} %broadcast_in_dim.77), calls=%async_computation.3 | async-start | bytes 524288 | tf_op jit(solution)/shard_map/normal/all_to_all | solution.py:352
  111.4 38.0 %all-to-all-start.2 = ((f32[16,128,256]{2,1,0:T(8,128)}), f32[16,128,256]{2,1,0:T(8,128)S(1)}, u32[]{:S(2)}, u32[]{:S(2)}) async-start(f32[16,128,256]{2,1,0:T(8,128)} %bitcast.44), calls=%async_computation.2 | async-start | bytes 4194304 | tf_op jit(solution)/shard_map/exchange/all_to_all | solution.py:372

commit v4 on v2

--- a/solution.py
+++ b/solution.py
@@ -35,8 +35,11 @@
     table_ref,
     count_ref,
     tile_hbm,
-    second_hbm,
     third_ref,
+    source_0,
+    source_1,
+    source_2,
+    source_3,
     out_hbm,
     tile_buf,
     second_buf,
@@ -57,10 +60,10 @@
             tile_hbm.at[pl.ds(pair * PAIR, PAIR)], tile_buf.at[pl.ds(pair * PAIR, PAIR)], tile_sem.at[pair]
         )
 
-    def second_copy(slot):
-        return pltpu.make_async_copy(
-            second_hbm.at[table_ref[0, slot]], second_buf.at[slot], second_sem.at[slot]
-        )
+    sources = [source_0, source_1, source_2, source_3]
+
+    def second_copy(source, slot):
+        return pltpu.make_async_copy(source.at[table_ref[0, slot]], second_buf.at[slot], second_sem.at[slot])
 
     def result_copy(slot):
         return pltpu.make_async_copy(result_buf.at[slot], out_hbm.at[table_ref[2, slot]], result_sem.at[slot])
@@ -68,7 +71,14 @@
     def start(pair, carry):
         tile_copy(pair).start()
         for at in range(PAIR):
-            second_copy(pair * PAIR + at).start()
+            slot = pair * PAIR + at
+            chosen = table_ref[3, slot]
+            for which, source in enumerate(sources):
+
+                @pl.when(chosen == which)
+                def _():
+                    second_copy(source, slot).start()
+
         return carry
 
     lax.fori_loop(0, pairs, start, 0)
@@ -76,7 +86,7 @@
     def contract(pair, carry):
         tile_copy(pair).wait()
         for at in range(PAIR):
-            second_copy(pair * PAIR + at).wait()
+            second_copy(source_0, pair * PAIR + at).wait()
         for at in range(PAIR):
             slot = pair * PAIR + at
             second = second_buf[slot]
@@ -108,7 +118,7 @@
     lax.fori_loop(0, count, finish, 0)
 
 
-def contract_tiles(table, count, tile_values, second_blocks, third_blocks, out_slots):
+def contract_tiles(table, count, tile_values, third_blocks, sources, out_slots):
     slot_count, tile_edge, depth = tile_values.shape
     rank_width = third_blocks.shape[2]
     smem = pl.BlockSpec(memory_space=pltpu.SMEM)
@@ -117,7 +127,7 @@
     return pl.pallas_call(
         contract_kernel,
         out_shape=jax.ShapeDtypeStruct((out_slots, tile_edge, rank_width), jnp.float32),
-        in_specs=[smem, smem, hbm, hbm, vmem],
+        in_specs=[smem, smem, hbm, vmem] + [hbm] * len(sources),
         out_specs=hbm,
         scratch_shapes=[
             pltpu.VMEM((slot_count, tile_edge, depth), jnp.float32),
@@ -132,7 +142,7 @@
             flops=6 * slot_count * tile_edge * depth * rank_width, bytes_accessed=10_000_000, transcendentals=0
         ),
         name="contract",
-    )(table, count, tile_values, second_blocks, third_blocks)
+    )(table, count, tile_values, third_blocks, *sources)
 
 
 def combine_kernel(target_ref, received_ref, inverse_ref, out_ref, total_ref):
@@ -275,10 +285,22 @@
     col_index = lax.axis_index("col")
     n_row = lax.axis_size("row")
     n_col = lax.axis_size("col")
-    part = rank_width // n_row
+    part = rank_width // n_col
 
     with jax.named_scope("gather_second"):
-        gathered = lax.all_gather(mode2_factor, "row", axis=0, tiled=True)
+        n_z = n_row // 2
+
+        def moved(shift):
+            pairs = [(i, 2 * ((i // 2 + shift) % n_z) + i % 2) for i in range(n_row)]
+            return lax.ppermute(mode2_factor, "row", pairs)
+
+        near = [1, n_z - 1, 2, n_z - 2]
+        far = [3, n_z - 3, 4]
+        twin = [(i, i ^ 1) for i in range(n_row)]
+        near_own = jnp.concatenate([mode2_factor] + [moved(shift) for shift in near], axis=0)
+        far_own = jnp.concatenate([moved(shift) for shift in far], axis=0)
+        near_other = lax.ppermute(near_own, "row", twin)
+        far_other = lax.ppermute(far_own, "row", twin)
 
     with jax.named_scope("tables"):
         slot_index = jnp.arange(slot_count, dtype=jnp.int32)
@@ -289,41 +311,53 @@
         rank = jnp.dot(chosen, earlier)
         own_rank = jnp.sum(chosen * rank, axis=0).astype(jnp.int32)
         out_slot = jnp.clip(mode1_column[:, 0], 0, n_col - 1) * SLOTS + own_rank
+        source = jnp.clip(mode2_row[:, 0], 0, n_row - 1)
+        shift = (row_index // 2 - source // 2 + n_z) % n_z
+        place_of = [0] * n_z
+        for at, each in enumerate([0] + near):
+            place_of[each] = at
+        for at, each in enumerate(far):
+            place_of[each] = at
+        place = sum(jnp.where(shift == each, place_of[each], 0) for each in range(n_z))
+        is_far = ((shift > 2) & (shift < n_z - 2)).astype(jnp.int32)
+        is_other = (source % 2 != row_index % 2).astype(jnp.int32)
         table = jnp.stack(
             [
-                jnp.clip(mode2_row[:, 0] * JB_DEV + mode2_offset, 0, gathered.shape[0] // tile_edge - 1),
+                place * JB_DEV + jnp.clip(mode2_offset, 0, JB_DEV - 1),
                 jnp.clip(mode3_offset, 0, mode3_factor.shape[0] // tile_edge - 1),
                 out_slot,
+                is_far + 2 * is_other,
             ]
         ).astype(jnp.int32)
-        place = jnp.arange(SLOTS, dtype=jnp.float32)
-        taken = chosen[:, None, :] * (rank[:, None, :] == place[None, :, None])
+        slots = jnp.arange(SLOTS, dtype=jnp.float32)
+        taken = chosen[:, None, :] * (rank[:, None, :] == slots[None, :, None])
         targets = jnp.sum(taken * (mode1_offset + 1).astype(jnp.float32), axis=2) - 1.0
         target_rows = jnp.zeros((8, rank_width), jnp.float32).at[0, : n_col * SLOTS].set(targets.reshape(-1))
 
     with jax.named_scope("normal"):
-        own_second = gram_of(mode2_factor)
-        own_third = gram_of(mode3_factor)
-        exchanged = lax.all_to_all(own_second.reshape(n_row, part, rank_width), "row", 0, 0)
-        second_part = jnp.sum(exchanged, axis=0)
-        third_part = lax.dynamic_slice_in_dim(own_third, row_index * part, part, 0)
-        sent = jnp.concatenate([second_part, third_part, target_rows], axis=0)
+        strips = [gram_of(each).reshape(n_col, part, rank_width) for each in (mode2_factor, mode3_factor)]
+        strips = lax.all_to_all(jnp.concatenate(strips, axis=1), "col", 0, 0)
+        strips = jnp.sum(strips, axis=0)
+        second_strips = lax.all_to_all(
+            jnp.broadcast_to(strips[None, :part], (n_row, part, rank_width)), "row", 0, 0
+        )
+        normal_part = jnp.sum(second_strips, axis=0) * strips[part:]
+        sent = jnp.concatenate([normal_part, target_rows], axis=0)
         spread = lax.all_to_all(jnp.broadcast_to(sent[None], (n_col,) + sent.shape), "col", 0, 0)
-        both = jnp.sum(spread[:, : 2 * part], axis=0)
-        normal_part = both[:part] * both[part:]
-        normal_matrix = lax.all_to_all(
-            jnp.broadcast_to(normal_part[None], (n_row, part, rank_width)), "row", 0, 0
-        ).reshape(rank_width, rank_width)
-        received_targets = lax.dynamic_slice_in_dim(spread[:, 2 * part], col_index * SLOTS, SLOTS, 1)
+        normal_matrix = spread[:, :part].reshape(rank_width, rank_width)
+        received_targets = lax.dynamic_slice_in_dim(spread[:, part], col_index * SLOTS, SLOTS, 1)
         received_targets = received_targets.astype(jnp.int32).reshape(-1)
 
     with jax.named_scope("contract"):
+        def blocks(array):
+            return array.reshape(-1, tile_edge, rank_width)
+
         partials = contract_tiles(
             table,
             tile_count,
             tile_values,
-            gathered.reshape(-1, tile_edge, rank_width),
-            mode3_factor.reshape(-1, tile_edge, rank_width),
+            blocks(mode3_factor),
+            [blocks(near_own), blocks(far_own), blocks(near_other), blocks(far_other)],
             n_col * SLOTS,
         )
     with jax.named_scope("exchange"):

time: 119 us -> 128 us (1.076)
  starting transfers between devices: 29.5 us -> 44.3 us
  between operations: 14.2 us -> 1.06 us
  waiting for transfers between devices: 30.9 us -> 40.7 us
  matrix products: 5.49 us -> 2.83 us
  local copies, waits for them, and re-layouts: 1.92 us -> 3.89 us
    ppermute x0 -> x9, waiting for transfers between devices: none -> 22.5 us  [the longest x7 22.5 us: moved(): return lax.ppermute(mode2_factor, 'row', pairs)]
    ppermute x0 -> x9, starting transfers between devices: none -> 17.8 us  [the longest x7 17.6 us: moved(): return lax.ppermute(mode2_factor, 'row', pairs)]
    all_to_all x1, waiting for transfers between devices: 13.4 us -> 0.01 us  [local(): lax.all_to_all(jnp.broadcast_to(sent[None], (n_col,) + sent.shape), 'col'...]
    all_to_all x2, starting transfers between devices: 14.6 us -> 10.6 us  [the longest x1 7.04 us: local(): strips = lax.all_to_all(jnp.concatenate(strips, axis=1), 'col', 0, 0)]
    all_to_all x1, waiting for transfers between devices: 12.5 us -> 14.6 us  [local(): lax.all_to_all(partials.reshape(n_col, SLOTS * tile_edge, rank_width), 'c...]
    dot_general x2, matrix products: 4.62 us -> 2.69 us  [gram_of(): lax.dot_general(matrix, matrix, (((0,), (0,)), ((), ())), precision=HIGHE...]
  transfers between devices with their start and end apart: 5 -> 13, of which waited for: 3 -> 4; matrix products, arithmetic and copies ran while one was open for 8% -> 7% of each run, Pallas kernels for 25% -> 23%
where the time goes in v4:
time: 128 us; the launch traced here: 127 us
  starting transfers between devices  44.3 us (35%)
  waiting for transfers between devices  40.7 us (32%)
  Pallas kernels  32.7 us (26%)
  local copies, waits for them, and re-layouts  3.89 us (3%)
  matrix products  2.83 us (2%)
  other arithmetic  1.76 us (1%)
    ppermute x7, waiting for transfers between devices, moved(): return lax.ppermute(mode2_factor, 'row', pairs)  22.5 us
    ppermute x7, starting transfers between devices, moved(): return lax.ppermute(mode2_factor, 'row', pairs)  17.6 us
    pallas_call x1, Pallas kernels, invert(): pl.pallas_call(functools.partial(invert_kernel, block), out_shape=jax.Sha...  16 us
    all_to_all x1, waiting for transfers between devices, local(): lax.all_to_all(partials.reshape(n_col, SLOTS * tile_edge, rank_width), 'c...  14.6 us
    pallas_call x1, Pallas kernels, contract_tiles(): pl.pallas_call(contract_kernel, out_shape=jax.ShapeDtypeStruct((out_slots...  13.8 us
    all_to_all x1, starting transfers between devices, local(): lax.all_to_all(partials.reshape(n_col, SLOTS * tile_edge, rank_width), 'c...  9.05 us
    all_to_all x1, starting transfers between devices, local(): strips = lax.all_to_all(jnp.concatenate(strips, axis=1), 'col', 0, 0)  7.04 us
    all_to_all x1, starting transfers between devices, local(): lax.all_to_all(jnp.broadcast_to(sent[None], (n_col,) + sent.shape), 'col'...  6.85 us
  transfers between devices with their start and end apart: 13, of which 4 were waited for; matrix products, arithmetic and copies ran while one was open for 7% of the time, Pallas kernels for 23%

profile of v4, /device:TPU:32, one launch (start us, length us, event | category | flops | bytes accessed | tf_op | source)
XLA Modules:
  0.0 127.3 jit_solution(2596366456959415067)
XLA Ops:
  0.0 1.9 %collective-permute-start = (f32[256,256]{1,0:T(8,128)}, f32[256,256]{1,0:T(8,128)}, u32[]{:S(2)}, u32[]{:S(2)}) collective-permute-start(f32[256,256]{1,0:T(8,128)} %param.18), channel_id=1, source_target_pairs={{0,32},{16,48},{32,64},{48,80},{64,96},{80,112},{96,128},{112,144}... | collective-permute-start | bytes 786440 | tf_op jit(solution)/shard_map/gather_second/ppermute | solution.py:295
  1.9 0.1 collective-permute-start.1
  2.0 4.4 %collective-permute-start.2 = (f32[256,256]{1,0:T(8,128)}, f32[256,256]{1,0:T(8,128)S(1)}, u32[]{:S(2)}, u32[]{:S(2)}) collective-permute-start(f32[256,256]{1,0:T(8,128)} %param.18), channel_id=1, source_target_pairs={{0,64},{16,80},{32,96},{48,112},{64,128},{80,144},{96,160},{112,17... | collective-permute-start | bytes 786440 | tf_op jit(solution)/shard_map/gather_second/ppermute | solution.py:295
  6.4 1.0 collective-permute-start.3
  7.4 5.8 %collective-permute-start.4 = (f32[256,256]{1,0:T(8,128)}, f32[256,256]{1,0:T(8,128)S(1)}, u32[]{:S(2)}, u32[]{:S(2)}) collective-permute-start(f32[256,256]{1,0:T(8,128)} %param.18), channel_id=1, source_target_pairs={{0,96},{16,112},{32,128},{48,144},{64,160},{80,176},{96,192},{112,... | collective-permute-start | bytes 786440 | tf_op jit(solution)/shard_map/gather_second/ppermute | solution.py:295
  13.2 1.7 %fusion.17 = f32[256,256]{1,0:T(8,128)S(1)} fusion(f32[256,256]{1,0:T(8,128)} %param.18), kind=kOutput, calls=%fused_computation.65 | convolution fusion | flops 201326592 | bytes 524288 | tf_op jit(solution)/shard_map/normal/dot_general | solution.py:19
  14.9 1.0 fusion.18
  15.9 0.0 copy-start.4
  15.9 0.0 copy-start.8
  15.9 0.0 copy-start.1
  16.0 0.8 pad_maximum_fusion
  16.8 7.0 %all-to-all-start = ((f32[16,32,256]{2,1,0:T(8,128)}), f32[16,32,256]{2,1,0:T(8,128)S(1)}, u32[]{:S(2)}, u32[]{:S(2)}) async-start(f32[16,32,256]{2,1,0:T(8,128)} %pad_maximum_fusion), calls=%async_computation | async-start | bytes 1048576 | tf_op jit(solution)/shard_map/normal/all_to_all | solution.py:339
  24.5 0.1 select_reduce_fusion
  24.7 0.1 multiply_reduce_fusion
  24.8 0.0 collective-permute-done
  24.8 0.1 collective-permute-start.5
  24.9 1.0 constant_dynamic-update-slice_fusion.3
  25.9 0.0 collective-permute-done.1
  25.9 4.3 %collective-permute-start.6 = (f32[256,256]{1,0:T(8,128)S(1)}, f32[256,256]{1,0:T(8,128)}, u32[]{:S(2)}, u32[]{:S(2)}) collective-permute-start(f32[256,256]{1,0:T(8,128)S(1)} %copy-done.1), channel_id=1, source_target_pairs={{0,128},{16,144},{32,160},{48,176},{64,192},{80,208},{96,224},{112... | collective-permute-start | bytes 786440 | tf_op jit(solution)/shard_map/gather_second/ppermute | solution.py:295
  30.3 0.0 collective-permute-done.2
  30.3 0.0 collective-permute-done.3
  30.3 0.1 collective-permute-start.7
  30.5 3.5 %all-to-all-done = f32[16,32,256]{2,1,0:T(8,128)S(1)} async-done(((f32[16,32,256]{2,1,0:T(8,128)}), f32[16,32,256]{2,1,0:T(8,128)S(1)}, u32[]{:S(2)}, u32[]{:S(2)}) %all-to-all-start) | async-done | bytes 524320 | tf_op jit(solution)/shard_map/normal/all_to_all | solution.py:339
  34.0 0.0 copy-start.5
  34.0 0.7 broadcast_in_dim.41
  34.7 3.6 %all-to-all-start.1 = ((f32[16,16,256]{2,1,0:T(8,128)}), f32[16,16,256]{2,1,0:T(8,128)S(1)}, u32[]{:S(2)}, u32[]{:S(2)}) async-start(f32[16,16,256]{2,1,0:T(8,128)} %broadcast_in_dim.41), calls=%async_computation.1 | async-start | bytes 524288 | tf_op jit(solution)/shard_map/normal/all_to_all | solution.py:341
  38.3 11.5 %collective-permute-done.4 = f32[256,256]{1,0:T(8,128)S(1)} collective-permute-done((f32[256,256]{1,0:T(8,128)}, f32[256,256]{1,0:T(8,128)S(1)}, u32[]{:S(2)}, u32[]{:S(2)}) %collective-permute-start.4) | collective-permute-done | bytes 262176 | tf_op jit(solution)/shard_map/gather_second/ppermute | solution.py:295
  49.8 0.0 copy-start.6
  49.8 0.0 copy-start.7
  49.8 11.0 %collective-permute-done.5 = f32[256,256]{1,0:T(8,128)S(1)} collective-permute-done((f32[256,256]{1,0:T(8,128)S(1)}, f32[256,256]{1,0:T(8,128)S(1)}, u32[]{:S(2)}, u32[]{:S(2)}) %collective-permute-start.5) | collective-permute-done | bytes 262176 | tf_op jit(solution)/shard_map/gather_second/ppermute | solution.py:295
  60.9 0.0 collective-permute-done.6
  60.9 1.0 constant_dynamic-update-slice_fusion.5
  61.9 0.1 collective-permute-start.8
  62.0 0.1 copy.12
  62.1 0.1 sub.36
  62.2 0.0 all-to-all-done.1
  62.3 0.8 broadcast_in_dim.42
  63.0 6.8 %all-to-all-start.2 = ((f32[16,24,256]{2,1,0:T(8,128)}), f32[16,24,256]{2,1,0:T(8,128)S(1)}, u32[]{:S(2)}, u32[]{:S(2)}) async-start(f32[16,24,256]{2,1,0:T(8,128)} %broadcast_in_dim.42), calls=%async_computation.2 | async-start | bytes 786432 | tf_op jit(solution)/shard_map/normal/all_to_all | solution.py:346
  69.9 0.6 pad_add_fusion.table_ref
  70.5 0.0 collective-permute-done.8
  70.5 13.8 %contract.1 = f32[64,32,256]{2,1,0:T(8,128)} custom-call(s32[4,48]{1,0:T(4,128)} %pad_add_fusion.table_ref, s32[1]{0:T(128)} %copy.19.count_ref, f32[48,32,1024]{2,1,0:T(8,128)} %tile_hbm.1, f32[16,32,256]{2,1,0:T(8,128)} %bitcast.53, f32[40,32,256]{2,1,0:T(8,128)} %bitcast.54, f32[24,32,256]{2,1,0:T(8,128)} %bitcast.55, f32[40,32,256]{2,1,0:T(8,128)} %bitcast.13.source_2, ...), custom_call_target="tpu_custom_call" | custom-call | flops 2415919104 | bytes 10000000 | tf_op jit(solution)/shard_map/contract/contract/pallas_call | solution.py:127
  84.3 0.0 all-to-all-done.2
  84.3 9.0 %all-to-all-start.3 = ((f32[16,128,256]{2,1,0:T(8,128)}), f32[16,128,256]{2,1,0:T(8,128)S(1)}, u32[]{:S(2)}, u32[]{:S(2)}) async-start(f32[16,128,256]{2,1,0:T(8,128)} %bitcast.52), calls=%async_computation.3 | async-start | bytes 4194304 | tf_op jit(solution)/shard_map/exchange/all_to_all | solution.py:364
  93.4 0.1 convert_reduce_fusion
  93.5 0.1 convert_element_type.46.target_ref
  93.7 16.0 %invert.1.inverse_ref = f32[256,256]{1,0:T(8,128)S(1)} custom-call(f32[256,256]{1,0:T(8,128)S(1)} %bitcast.51), custom_call_target="tpu_custom_call" | custom-call | flops 201326592 | bytes 524288 | tf_op jit(solution)/shard_map/inverse/invert/pallas_call | solution.py:260
  109.7 14.6 %all-to-all-done.3 = f32[16,128,256]{2,1,0:T(8,128)S(1)} async-done(((f32[16,128,256]{2,1,0:T(8,128)}), f32[16,128,256]{2,1,0:T(8,128)S(1)}, u32[]{:S(2)}, u32[]{:S(2)}) %all-to-all-start.3) | async-done | bytes 2097184 | tf_op jit(solution)/shard_map/exchange/all_to_all | solution.py:364
  124.3 2.9 %combine.1 = f32[512,256]{1,0:T(8,128)} custom-call(s32[64]{0:T(128)S(1)} %convert_element_type.46.target_ref, f32[64,32,256]{2,1,0:T(8,128)S(1)} %bitcast.50, f32[256,256]{1,0:T(8,128)S(1)} %invert.1.inverse_ref), custom_call_target="tpu_custom_call" | custom-call | tf_op jit(solution)/shard_map/combine/combine/pallas_call | solution.py:171
  (32 shorter events, 0.3 us)
Async XLA Ops:
  0.0 14.9 %copy-start = (f32[512,256]{1,0:T(8,128)S(1)}, f32[512,256]{1,0:T(8,128)}, u32[]{:S(2)}) copy-start(f32[512,256]{1,0:T(8,128)} %param.19) | copy-start | bytes 1572868
  0.0 24.8 %collective-permute-start = (f32[256,256]{1,0:T(8,128)}, f32[256,256]{1,0:T(8,128)}, u32[]{:S(2)}, u32[]{:S(2)}) collective-permute-start(f32[256,256]{1,0:T(8,128)} %param.18), channel_id=1, source_target_pairs={{0,32},{16,48},{32,64},{48,80},{64,96},{80,112},{96,128},{112,144}... | collective-permute-start | bytes 786440 | tf_op jit(solution)/shard_map/gather_second/ppermute | solution.py:295
  1.9 24.0 %collective-permute-start.1 = (f32[256,256]{1,0:T(8,128)}, f32[256,256]{1,0:T(8,128)S(1)}, u32[]{:S(2)}, u32[]{:S(2)}) collective-permute-start(f32[256,256]{1,0:T(8,128)} %param.18), channel_id=1, source_target_pairs={{0,224},{16,240},{32,0},{48,16},{64,32},{80,48},{96,64},{112,80},{... | collective-permute-start | bytes 786440 | tf_op jit(solution)/shard_map/gather_second/ppermute | solution.py:295
  2.0 28.2 %collective-permute-start.2 = (f32[256,256]{1,0:T(8,128)}, f32[256,256]{1,0:T(8,128)S(1)}, u32[]{:S(2)}, u32[]{:S(2)}) collective-permute-start(f32[256,256]{1,0:T(8,128)} %param.18), channel_id=1, source_target_pairs={{0,64},{16,80},{32,96},{48,112},{64,128},{80,144},{96,160},{112,17... | collective-permute-start | bytes 786440 | tf_op jit(solution)/shard_map/gather_second/ppermute | solution.py:295
  6.4 23.9 %collective-permute-start.3 = (f32[256,256]{1,0:T(8,128)}, f32[256,256]{1,0:T(8,128)S(1)}, u32[]{:S(2)}, u32[]{:S(2)}) collective-permute-start(f32[256,256]{1,0:T(8,128)} %param.18), channel_id=1, source_target_pairs={{0,192},{16,208},{32,224},{48,240},{64,0},{80,16},{96,32},{112,48}... | collective-permute-start | bytes 786440 | tf_op jit(solution)/shard_map/gather_second/ppermute | solution.py:295
  7.4 42.3 %collective-permute-start.4 = (f32[256,256]{1,0:T(8,128)}, f32[256,256]{1,0:T(8,128)S(1)}, u32[]{:S(2)}, u32[]{:S(2)}) collective-permute-start(f32[256,256]{1,0:T(8,128)} %param.18), channel_id=1, source_target_pairs={{0,96},{16,112},{32,128},{48,144},{64,160},{80,176},{96,192},{112,... | collective-permute-start | bytes 786440 | tf_op jit(solution)/shard_map/gather_second/ppermute | solution.py:295
  15.9 8.6 %copy-start.4 = (s32[48,1]{0,1:T(1,128)S(1)}, s32[48,1]{0,1:T(1,128)}, u32[]{:S(2)}) copy-start(s32[48,1]{0,1:T(1,128)} %param.13) | copy-start | bytes 580
  15.9 8.7 %copy-start.8 = (s32[48]{0:T(128)S(1)}, s32[48]{0:T(128)}, u32[]{:S(2)}) copy-start(s32[48]{0:T(128)} %param.14) | copy-start | bytes 580
  15.9 8.7 %copy-start.1 = (f32[256,256]{1,0:T(8,128)S(1)}, f32[256,256]{1,0:T(8,128)}, u32[]{:S(2)}) copy-start(f32[256,256]{1,0:T(8,128)} %param.18) | copy-start | bytes 786436
  16.8 17.1 %all-to-all-start = ((f32[16,32,256]{2,1,0:T(8,128)}), f32[16,32,256]{2,1,0:T(8,128)S(1)}, u32[]{:S(2)}, u32[]{:S(2)}) async-start(f32[16,32,256]{2,1,0:T(8,128)} %pad_maximum_fusion), calls=%async_computation | async-start | bytes 1048576 | tf_op jit(solution)/shard_map/normal/all_to_all | solution.py:339
  24.8 36.0 %collective-permute-start.5 = (f32[256,256]{1,0:T(8,128)S(1)}, f32[256,256]{1,0:T(8,128)S(1)}, u32[]{:S(2)}, u32[]{:S(2)}) collective-permute-start(f32[256,256]{1,0:T(8,128)S(1)} %copy-done.1), channel_id=1, source_target_pairs={{0,160},{16,176},{32,192},{48,208},{64,224},{80,240},{96,0},{112,1... | collective-permute-start | bytes 786440 | tf_op jit(solution)/shard_map/gather_second/ppermute | solution.py:295
  25.9 35.0 %collective-permute-start.6 = (f32[256,256]{1,0:T(8,128)S(1)}, f32[256,256]{1,0:T(8,128)}, u32[]{:S(2)}, u32[]{:S(2)}) collective-permute-start(f32[256,256]{1,0:T(8,128)S(1)} %copy-done.1), channel_id=1, source_target_pairs={{0,128},{16,144},{32,160},{48,176},{64,192},{80,208},{96,224},{112... | collective-permute-start | bytes 786440 | tf_op jit(solution)/shard_map/gather_second/ppermute | solution.py:295
  30.3 31.5 %copy-start.2 = (f32[1280,256]{1,0:T(8,128)}, f32[1280,256]{1,0:T(8,128)S(1)}, u32[]{:S(2)}) copy-start(f32[1280,256]{1,0:T(8,128)S(1)} %constant_dynamic-update-slice_fusion) | copy-start | bytes 3932164
  30.3 40.2 %collective-permute-start.7 = (f32[1280,256]{1,0:T(8,128)S(1)}, f32[1280,256]{1,0:T(8,128)}, u32[]{:S(2)}, u32[]{:S(2)}) collective-permute-start(f32[1280,256]{1,0:T(8,128)S(1)} %constant_dynamic-update-slice_fusion), channel_id=1, source_target_pairs={{0,16},{16,0},{32,48},{48,32},{64,80},{80,64},{96,112},{112,96},{1... | collective-permute-start | bytes 3932168 | tf_op jit(solution)/shard_map/gather_second/ppermute | solution.py:302
  34.0 28.0 %copy-start.5 = (s32[48,1]{0,1:T(1,128)S(1)}, s32[48,1]{0,1:T(1,128)}, u32[]{:S(2)}) copy-start(s32[48,1]{0,1:T(1,128)} %param.15) | copy-start | bytes 580
  34.7 27.5 %all-to-all-start.1 = ((f32[16,16,256]{2,1,0:T(8,128)}), f32[16,16,256]{2,1,0:T(8,128)S(1)}, u32[]{:S(2)}, u32[]{:S(2)}) async-start(f32[16,16,256]{2,1,0:T(8,128)} %broadcast_in_dim.41), calls=%async_computation.1 | async-start | bytes 524288 | tf_op jit(solution)/shard_map/normal/all_to_all | solution.py:341
  49.8 20.1 %copy-start.6 = (s32[48]{0:T(128)S(1)}, s32[48]{0:T(128)}, u32[]{:S(2)}) copy-start(s32[48]{0:T(128)} %param.17) | copy-start | bytes 580
  49.8 20.1 %copy-start.7 = (s32[48]{0:T(128)S(1)}, s32[48]{0:T(128)}, u32[]{:S(2)}) copy-start(s32[48]{0:T(128)} %param.16) | copy-start | bytes 580
  61.9 8.7 %copy-start.3 = (f32[768,256]{1,0:T(8,128)}, f32[768,256]{1,0:T(8,128)S(1)}, u32[]{:S(2)}) copy-start(f32[768,256]{1,0:T(8,128)S(1)} %constant_dynamic-update-slice_fusion.5) | copy-start | bytes 2359300
  61.9 8.7 %collective-permute-start.8 = (f32[768,256]{1,0:T(8,128)S(1)}, f32[768,256]{1,0:T(8,128)}, u32[]{:S(2)}, u32[]{:S(2)}) collective-permute-start(f32[768,256]{1,0:T(8,128)S(1)} %constant_dynamic-update-slice_fusion.5), channel_id=1, source_target_pairs={{0,16},{16,0},{32,48},{48,32},{64,80},{80,64},{96,112},{112,96},{1... | collective-permute-start | bytes 2359304 | tf_op jit(solution)/shard_map/gather_second/ppermute | solution.py:303
  63.0 21.3 %all-to-all-start.2 = ((f32[16,24,256]{2,1,0:T(8,128)}), f32[16,24,256]{2,1,0:T(8,128)S(1)}, u32[]{:S(2)}, u32[]{:S(2)}) async-start(f32[16,24,256]{2,1,0:T(8,128)} %broadcast_in_dim.42), calls=%async_computation.2 | async-start | bytes 786432 | tf_op jit(solution)/shard_map/normal/all_to_all | solution.py:346
  84.3 40.0 %all-to-all-start.3 = ((f32[16,128,256]{2,1,0:T(8,128)}), f32[16,128,256]{2,1,0:T(8,128)S(1)}, u32[]{:S(2)}, u32[]{:S(2)}) async-start(f32[16,128,256]{2,1,0:T(8,128)} %bitcast.52), calls=%async_computation.3 | async-start | bytes 4194304 | tf_op jit(solution)/shard_map/exchange/all_to_all | solution.py:364

commit v5 on v4

--- a/solution.py
+++ b/solution.py
@@ -10,7 +10,8 @@
 IB_DEV = 16
 JB_DEV = 8
 SLOTS = 4
-PAIR = 2
+GROUP = 4
+AHEAD = 2
 
 HIGHEST = lax.Precision.HIGHEST
 
@@ -31,36 +32,18 @@
     return jnp.dot(left, right, preferred_element_type=jnp.float32)
 
 
-def contract_kernel(
-    table_ref,
-    count_ref,
-    tile_hbm,
-    third_ref,
-    source_0,
-    source_1,
-    source_2,
-    source_3,
-    out_hbm,
-    tile_buf,
-    second_buf,
-    result_buf,
-    tile_sem,
-    second_sem,
-    result_sem,
-):
+def contract_kernel(table_ref, count_ref, tile_hbm, third_ref, *rest):
+    sources, rest = rest[:-7], rest[-7:]
+    out_hbm, tile_buf, second_buf, result_buf, tile_sem, second_sem, result_sem = rest
     count = count_ref[0]
-    pairs = (count + PAIR - 1) // PAIR
-    tile_edge = third_ref.shape[1]
-    depth = tile_buf.shape[2]
+    groups = (count + GROUP - 1) // GROUP
+    slot_count, tile_edge, depth = tile_hbm.shape
     chunk = min(256, depth)
     per_chunk = chunk // tile_edge
 
-    def tile_copy(pair):
-        return pltpu.make_async_copy(
-            tile_hbm.at[pl.ds(pair * PAIR, PAIR)], tile_buf.at[pl.ds(pair * PAIR, PAIR)], tile_sem.at[pair]
-        )
-
-    sources = [source_0, source_1, source_2, source_3]
+    def tile_copy(group):
+        span = pl.ds(group * GROUP, GROUP)
+        return pltpu.make_async_copy(tile_hbm.at[span], tile_buf.at[span], tile_sem.at[group])
 
     def second_copy(source, slot):
         return pltpu.make_async_copy(source.at[table_ref[0, slot]], second_buf.at[slot], second_sem.at[slot])
@@ -68,27 +51,36 @@
     def result_copy(slot):
         return pltpu.make_async_copy(result_buf.at[slot], out_hbm.at[table_ref[2, slot]], result_sem.at[slot])
 
-    def start(pair, carry):
-        tile_copy(pair).start()
-        for at in range(PAIR):
-            slot = pair * PAIR + at
-            chosen = table_ref[3, slot]
-            for which, source in enumerate(sources):
-
-                @pl.when(chosen == which)
-                def _():
-                    second_copy(source, slot).start()
-
-        return carry
-
-    lax.fori_loop(0, pairs, start, 0)
-
-    def contract(pair, carry):
-        tile_copy(pair).wait()
-        for at in range(PAIR):
-            second_copy(source_0, pair * PAIR + at).wait()
-        for at in range(PAIR):
-            slot = pair * PAIR + at
+    def start(group):
+        tile_copy(group).start()
+        for at in range(GROUP):
+            slot = group * GROUP + at
+            if len(sources) == 1:
+                second_copy(sources[0], slot).start()
+            else:
+                chosen = table_ref[3, slot]
+                for which, source in enumerate(sources):
+
+                    @pl.when(chosen == which)
+                    def _():
+                        second_copy(source, slot).start()
+
+    for group in range(AHEAD):
+
+        @pl.when(group < groups)
+        def _():
+            start(group)
+
+    def contract(group, carry):
+        @pl.when(group + AHEAD < groups)
+        def _():
+            start(group + AHEAD)
+
+        tile_copy(group).wait()
+        for at in range(GROUP):
+            second_copy(sources[0], group * GROUP + at).wait()
+        for at in range(GROUP):
+            slot = group * GROUP + at
             second = second_buf[slot]
             third = third_ref[table_ref[1, slot]]
             high, low = split(tile_buf[slot])
@@ -102,6 +94,8 @@
                 total = total + dot32(both[:, q * chunk : (q + 1) * chunk], khatri_high)
                 total_low = total_low + dot32(high[:, q * chunk : (q + 1) * chunk], khatri_low)
             result_buf[slot] = total[:tile_edge] + (total[tile_edge:] + total_low)
+        for at in range(GROUP):
+            slot = group * GROUP + at
 
             @pl.when(slot < count)
             def _():
@@ -109,7 +103,7 @@
 
         return carry
 
-    lax.fori_loop(0, pairs, contract, 0)
+    lax.fori_loop(0, groups, contract, 0)
 
     def finish(slot, carry):
         result_copy(slot).wait()
@@ -124,6 +118,7 @@
     smem = pl.BlockSpec(memory_space=pltpu.SMEM)
     vmem = pl.BlockSpec(memory_space=pltpu.VMEM)
     hbm = pl.BlockSpec(memory_space=pltpu.HBM)
+    block = (slot_count, tile_edge, rank_width)
     return pl.pallas_call(
         contract_kernel,
         out_shape=jax.ShapeDtypeStruct((out_slots, tile_edge, rank_width), jnp.float32),
@@ -131,9 +126,9 @@
         out_specs=hbm,
         scratch_shapes=[
             pltpu.VMEM((slot_count, tile_edge, depth), jnp.float32),
-            pltpu.VMEM((slot_count, tile_edge, rank_width), jnp.float32),
-            pltpu.VMEM((slot_count, tile_edge, rank_width), jnp.float32),
-            pltpu.SemaphoreType.DMA((slot_count // PAIR,)),
+            pltpu.VMEM(block, jnp.float32),
+            pltpu.VMEM(block, jnp.float32),
+            pltpu.SemaphoreType.DMA((slot_count // GROUP,)),
             pltpu.SemaphoreType.DMA((slot_count,)),
             pltpu.SemaphoreType.DMA((slot_count,)),
         ],
@@ -146,23 +141,25 @@
 
 
 def combine_kernel(target_ref, received_ref, inverse_ref, out_ref, total_ref):
-    tile_edge = received_ref.shape[1]
+    slot_count, tile_edge, _ = received_ref.shape
     total_ref[...] = jnp.zeros_like(total_ref)
 
-    def add(slot, carry):
-        target = target_ref[slot]
-
-        @pl.when(target >= 0)
-        def _():
-            rows = pl.ds(pl.multiple_of(target * tile_edge, tile_edge), tile_edge)
-            total_ref[rows, :] += received_ref[slot]
+    def add(step, carry):
+        for at in range(8):
+            slot = step * 8 + at
+            target = target_ref[slot]
+            rows = pl.ds(pl.multiple_of(jnp.maximum(target, 0) * tile_edge, tile_edge), tile_edge)
+
+            @pl.when(target >= 0)
+            def _():
+                total_ref[rows, :] += received_ref[slot]
 
         return carry
 
-    lax.fori_loop(0, received_ref.shape[0], add, 0)
-    out_ref[...] = jnp.dot(
-        total_ref[...], inverse_ref[...], precision=HIGHEST, preferred_element_type=jnp.float32
-    )
+    lax.fori_loop(0, slot_count // 8, add, 0)
+    high, low = split(total_ref[...])
+    inverse_high, inverse_low = split(inverse_ref[...])
+    out_ref[...] = dot32(high, inverse_high) + (dot32(low, inverse_high) + dot32(high, inverse_low))
 
 
 def combine(targets, received, inverse):
@@ -290,15 +287,20 @@
     with jax.named_scope("gather_second"):
         n_z = n_row // 2
 
-        def moved(shift):
+        def moved(array, shift):
             pairs = [(i, 2 * ((i // 2 + shift) % n_z) + i % 2) for i in range(n_row)]
-            return lax.ppermute(mode2_factor, "row", pairs)
+            return lax.ppermute(array, "row", pairs)
 
         near = [1, n_z - 1, 2, n_z - 2]
         far = [3, n_z - 3, 4]
         twin = [(i, i ^ 1) for i in range(n_row)]
-        near_own = jnp.concatenate([mode2_factor] + [moved(shift) for shift in near], axis=0)
-        far_own = jnp.concatenate([moved(shift) for shift in far], axis=0)
+        up_1, down_1 = moved(mode2_factor, 1), moved(mode2_factor, -1)
+        up_2, down_2 = moved(up_1, 1), moved(down_1, -1)
+        up_3, down_3 = moved(up_2, 1), moved(down_2, -1)
+        middle = mode2_factor.shape[0] // 2
+        up_4, down_4 = moved(up_3[:middle], 1), moved(down_3[middle:], -1)
+        near_own = jnp.concatenate([mode2_factor, up_1, down_1, up_2, down_2], axis=0)
+        far_own = jnp.concatenate([up_3, down_3, up_4, down_4], axis=0)
         near_other = lax.ppermute(near_own, "row", twin)
         far_other = lax.ppermute(far_own, "row", twin)
 

time: 128 us -> 114 us (0.89)
  waiting for transfers between devices: 40.7 us -> 23.7 us
  local copies, waits for them, and re-layouts: 3.89 us -> 8.46 us
  starting transfers between devices: 44.3 us -> 41.1 us
    ppermute x7 -> x8, waiting for transfers between devices: 22.5 us -> 11.2 us  [moved(): return lax.ppermute(array, 'row', pairs)]
    ppermute x7 -> x8, starting transfers between devices: 17.6 us -> 10.8 us  [moved(): return lax.ppermute(array, 'row', pairs)]
    all_to_all x1, starting transfers between devices: 3.56 us -> 8.74 us  [local(): lax.all_to_all(jnp.broadcast_to(strips[None, :part], (n_row, part, rank_w...]
    unnamed x24 -> x31, local copies, waits for them, and re-layouts: 1.11 us -> 4.76 us
    all_to_all x1, waiting for transfers between devices: 3.46 us -> 0.01 us  [local(): strips = lax.all_to_all(jnp.concatenate(strips, axis=1), 'col', 0, 0)]
    all_to_all x1, waiting for transfers between devices: 14.6 us -> 12.5 us  [local(): lax.all_to_all(partials.reshape(n_col, SLOTS * tile_edge, rank_width), 'c...]
    all_to_all x1, starting transfers between devices: 9.05 us -> 7.19 us  [local(): lax.all_to_all(partials.reshape(n_col, SLOTS * tile_edge, rank_width), 'c...]
  transfers between devices with their start and end apart: 13 -> 14, of which waited for: 4 -> 5; matrix products, arithmetic and copies ran while one was open for 7% -> 11% of each run, Pallas kernels for 23% -> 27%
where the time goes in v5:
time: 114 us; the launch traced here: 113 us
  starting transfers between devices  41.1 us (36%)
  Pallas kernels  32.7 us (29%)
  waiting for transfers between devices  23.7 us (21%)
  local copies, waits for them, and re-layouts  8.46 us (7%)
  matrix products  2.85 us (2%)
  other arithmetic  2.71 us (2%)
    pallas_call x1, Pallas kernels, invert(): pl.pallas_call(functools.partial(invert_kernel, block), out_shape=jax.Sha...  16 us
    pallas_call x1, Pallas kernels, contract_tiles(): pl.pallas_call(contract_kernel, out_shape=jax.ShapeDtypeStruct((out_slots...  14.2 us
    all_to_all x1, waiting for transfers between devices, local(): lax.all_to_all(partials.reshape(n_col, SLOTS * tile_edge, rank_width), 'c...  12.5 us
    ppermute x8, waiting for transfers between devices, moved(): return lax.ppermute(array, 'row', pairs)  11.2 us
    ppermute x8, starting transfers between devices, moved(): return lax.ppermute(array, 'row', pairs)  10.8 us
    all_to_all x1, starting transfers between devices, local(): lax.all_to_all(jnp.broadcast_to(strips[None, :part], (n_row, part, rank_w...  8.74 us
    all_to_all x1, starting transfers between devices, local(): lax.all_to_all(partials.reshape(n_col, SLOTS * tile_edge, rank_width), 'c...  7.19 us
    all_to_all x1, starting transfers between devices, local(): strips = lax.all_to_all(jnp.concatenate(strips, axis=1), 'col', 0, 0)  7.03 us
  transfers between devices with their start and end apart: 14, of which 5 were waited for; matrix products, arithmetic and copies ran while one was open for 11% of the time, Pallas kernels for 27%

profile of v5, /device:TPU:32, one launch (start us, length us, event | category | flops | bytes accessed | tf_op | source)
XLA Modules:
  0.0 112.5 jit_solution(3746586807934388359)
XLA Ops:
  0.0 1.9 %collective-permute-start = (f32[256,256]{1,0:T(8,128)}, f32[256,256]{1,0:T(8,128)S(1)}, u32[]{:S(2)}, u32[]{:S(2)}) collective-permute-start(f32[256,256]{1,0:T(8,128)} %param.18), channel_id=1, source_target_pairs={{0,32},{16,48},{32,64},{48,80},{64,96},{80,112},{96,128},{112,144}... | collective-permute-start | bytes 786440 | tf_op jit(solution)/shard_map/gather_second/ppermute | solution.py:292
  1.9 0.1 collective-permute-start.1
  2.0 1.7 %fusion.17 = f32[256,256]{1,0:T(8,128)S(1)} fusion(f32[256,256]{1,0:T(8,128)} %param.18), kind=kOutput, calls=%fused_computation.66 | convolution fusion | flops 201326592 | bytes 524288 | tf_op jit(solution)/shard_map/normal/dot_general | solution.py:20
  3.7 1.0 fusion.18
  4.8 0.0 copy-start.7
  4.8 0.0 copy-start.11
  4.8 0.0 copy-start.1
  4.8 0.8 pad_maximum_fusion
  5.6 7.0 %all-to-all-start = ((f32[16,32,256]{2,1,0:T(8,128)}), f32[16,32,256]{2,1,0:T(8,128)S(1)}, u32[]{:S(2)}, u32[]{:S(2)}) async-start(f32[16,32,256]{2,1,0:T(8,128)} %pad_maximum_fusion), calls=%async_computation | async-start | bytes 1048576 | tf_op jit(solution)/shard_map/normal/all_to_all | solution.py:341
  13.3 0.1 select_reduce_fusion
  13.5 0.1 multiply_reduce_fusion
  13.6 2.0 %collective-permute-start.2 = (f32[256,256]{1,0:T(8,128)S(1)}, f32[256,256]{1,0:T(8,128)}, u32[]{:S(2)}, u32[]{:S(2)}) collective-permute-start(f32[256,256]{1,0:T(8,128)S(1)} %collective-permute-done), channel_id=1, source_target_pairs={{0,32},{16,48},{32,64},{48,80},{64,96},{80,112},{96,128},{112,144}... | collective-permute-start | bytes 786440 | tf_op jit(solution)/shard_map/gather_second/ppermute | solution.py:292
  15.6 2.2 %collective-permute-start.3 = (f32[256,256]{1,0:T(8,128)S(1)}, f32[256,256]{1,0:T(8,128)S(1)}, u32[]{:S(2)}, u32[]{:S(2)}) collective-permute-start(f32[256,256]{1,0:T(8,128)S(1)} %collective-permute-done.1), channel_id=1, source_target_pairs={{0,224},{16,240},{32,0},{48,16},{64,32},{80,48},{96,64},{112,80},{... | collective-permute-start | bytes 786440 | tf_op jit(solution)/shard_map/gather_second/ppermute | solution.py:292
  17.9 5.7 %collective-permute-done.2 = f32[256,256]{1,0:T(8,128)} collective-permute-done((f32[256,256]{1,0:T(8,128)S(1)}, f32[256,256]{1,0:T(8,128)}, u32[]{:S(2)}, u32[]{:S(2)}) %collective-permute-start.2) | collective-permute-done | bytes 262176 | tf_op jit(solution)/shard_map/gather_second/ppermute | solution.py:292
  23.6 0.1 collective-permute-start.4
  23.6 0.5 collective-permute-done.3
  24.1 2.4 %collective-permute-start.5 = (f32[256,256]{1,0:T(8,128)S(1)}, f32[256,256]{1,0:T(8,128)S(1)}, u32[]{:S(2)}, u32[]{:S(2)}) collective-permute-start(f32[256,256]{1,0:T(8,128)S(1)} %collective-permute-done.3), channel_id=1, source_target_pairs={{0,224},{16,240},{32,0},{48,16},{64,32},{80,48},{96,64},{112,80},{... | collective-permute-start | bytes 786440 | tf_op jit(solution)/shard_map/gather_second/ppermute | solution.py:292
  26.6 0.7 broadcast_in_dim.41
  27.3 8.7 %all-to-all-start.1 = ((f32[16,16,256]{2,1,0:T(8,128)}), f32[16,16,256]{2,1,0:T(8,128)}, u32[]{:S(2)}, u32[]{:S(2)}) async-start(f32[16,16,256]{2,1,0:T(8,128)} %broadcast_in_dim.41), calls=%async_computation.1 | async-start | bytes 524288 | tf_op jit(solution)/shard_map/normal/all_to_all | solution.py:343
  36.1 1.0 constant_dynamic-update-slice_fusion.1
  37.0 0.0 copy-start.8
  37.1 0.2 collective-permute-start.8
  37.3 1.6 %collective-permute-start.6 = (f32[128,256]{1,0:T(8,128)S(1)}, f32[128,256]{1,0:T(8,128)S(1)}, u32[]{:S(2)}, u32[]{:S(2)}) collective-permute-start(f32[128,256]{1,0:T(8,128)S(1)} %slice.43), channel_id=1, source_target_pairs={{0,32},{16,48},{32,64},{48,80},{64,96},{80,112},{96,128},{112,144}... | collective-permute-start | bytes 393224 | tf_op jit(solution)/shard_map/gather_second/ppermute | solution.py:292
  38.9 0.7 copy-done.6
  39.6 0.6 collective-permute-start.7
  40.1 1.0 constant_dynamic-update-slice_fusion.8
  41.1 0.0 copy-start.9
  41.1 0.0 copy-start.10
  41.1 1.0 constant_dynamic-update-slice_fusion.7
  42.1 3.9 %collective-permute-done.6 = f32[128,256]{1,0:T(8,128)S(1)} collective-permute-done((f32[128,256]{1,0:T(8,128)S(1)}, f32[128,256]{1,0:T(8,128)S(1)}, u32[]{:S(2)}, u32[]{:S(2)}) %collective-permute-start.6) | collective-permute-done | bytes 131104 | tf_op jit(solution)/shard_map/gather_second/ppermute | solution.py:292
  46.1 1.1 collective-permute-done.7
  47.2 0.1 collective-permute-start.9
  47.3 0.1 copy.12
  47.4 0.1 sub.36
  47.5 1.0 reduce_sum.37
  48.5 0.8 broadcast_in_dim.42
  49.3 7.0 %all-to-all-start.2 = ((f32[16,24,256]{2,1,0:T(8,128)}), f32[16,24,256]{2,1,0:T(8,128)}, u32[]{:S(2)}, u32[]{:S(2)}) async-start(f32[16,24,256]{2,1,0:T(8,128)} %broadcast_in_dim.42), calls=%async_computation.2 | async-start | bytes 786432 | tf_op jit(solution)/shard_map/normal/all_to_all | solution.py:348
  56.3 0.6 pad_add_fusion.table_ref
  56.9 1.1 copy-done.4
  58.0 14.2 %contract.1 = f32[64,32,256]{2,1,0:T(8,128)} custom-call(s32[4,48]{1,0:T(4,128)} %pad_add_fusion.table_ref, s32[1]{0:T(128)} %copy.20.count_ref, f32[48,32,1024]{2,1,0:T(8,128)} %tile_hbm.1, f32[16,32,256]{2,1,0:T(8,128)} %bitcast.53, f32[40,32,256]{2,1,0:T(8,128)} %bitcast.54, f32[24,32,256]{2,1,0:T(8,128)} %bitcast.55, f32[40,32,256]{2,1,0:T(8,128)} %bitcast.56, ...), custom_call_target="tpu_custom_call" | custom-call | flops 2415919104 | bytes 10000000 | tf_op jit(solution)/shard_map/contract/contract/pallas_call | solution.py:122
  72.2 7.2 %all-to-all-start.3 = ((f32[16,128,256]{2,1,0:T(8,128)}), f32[16,128,256]{2,1,0:T(8,128)S(1)}, u32[]{:S(2)}, u32[]{:S(2)}) async-start(f32[16,128,256]{2,1,0:T(8,128)} %bitcast.52), calls=%async_computation.3 | async-start | bytes 4194304 | tf_op jit(solution)/shard_map/exchange/all_to_all | solution.py:366
  79.4 0.9 slice.42
  80.3 0.1 convert_reduce_fusion
  80.4 0.1 convert_element_type.46.target_ref
  80.5 1.0 slice.45
  81.5 16.0 %invert.1.inverse_ref = f32[256,256]{1,0:T(8,128)S(1)} custom-call(f32[256,256]{1,0:T(8,128)S(1)} %bitcast.51), custom_call_target="tpu_custom_call" | custom-call | flops 201326592 | bytes 524288 | tf_op jit(solution)/shard_map/inverse/invert/pallas_call | solution.py:257
  97.5 12.5 %all-to-all-done.3 = f32[16,128,256]{2,1,0:T(8,128)S(1)} async-done(((f32[16,128,256]{2,1,0:T(8,128)}), f32[16,128,256]{2,1,0:T(8,128)S(1)}, u32[]{:S(2)}, u32[]{:S(2)}) %all-to-all-start.3) | async-done | bytes 2097184 | tf_op jit(solution)/shard_map/exchange/all_to_all | solution.py:366
  110.0 2.5 %combine.1 = f32[512,256]{1,0:T(8,128)} custom-call(s32[64]{0:T(128)S(1)} %convert_element_type.46.target_ref, f32[64,32,256]{2,1,0:T(8,128)S(1)} %bitcast.50, f32[256,256]{1,0:T(8,128)S(1)} %invert.1.inverse_ref), custom_call_target="tpu_custom_call" | custom-call | tf_op jit(solution)/shard_map/combine/combine/pallas_call | solution.py:168
  (43 shorter events, 0.3 us)
Async XLA Ops:
  0.0 3.7 %copy-start = (f32[512,256]{1,0:T(8,128)S(1)}, f32[512,256]{1,0:T(8,128)}, u32[]{:S(2)}) copy-start(f32[512,256]{1,0:T(8,128)} %param.19) | copy-start | bytes 1572868
  0.0 13.6 %collective-permute-start = (f32[256,256]{1,0:T(8,128)}, f32[256,256]{1,0:T(8,128)S(1)}, u32[]{:S(2)}, u32[]{:S(2)}) collective-permute-start(f32[256,256]{1,0:T(8,128)} %param.18), channel_id=1, source_target_pairs={{0,32},{16,48},{32,64},{48,80},{64,96},{80,112},{96,128},{112,144}... | collective-permute-start | bytes 786440 | tf_op jit(solution)/shard_map/gather_second/ppermute | solution.py:292
  1.9 13.7 %collective-permute-start.1 = (f32[256,256]{1,0:T(8,128)}, f32[256,256]{1,0:T(8,128)S(1)}, u32[]{:S(2)}, u32[]{:S(2)}) collective-permute-start(f32[256,256]{1,0:T(8,128)} %param.18), channel_id=1, source_target_pairs={{0,224},{16,240},{32,0},{48,16},{64,32},{80,48},{96,64},{112,80},{... | collective-permute-start | bytes 786440 | tf_op jit(solution)/shard_map/gather_second/ppermute | solution.py:292
  4.8 8.6 %copy-start.7 = (s32[48,1]{0,1:T(1,128)S(1)}, s32[48,1]{0,1:T(1,128)}, u32[]{:S(2)}) copy-start(s32[48,1]{0,1:T(1,128)} %param.13) | copy-start | bytes 580
  4.8 8.7 %copy-start.11 = (s32[48]{0:T(128)S(1)}, s32[48]{0:T(128)}, u32[]{:S(2)}) copy-start(s32[48]{0:T(128)} %param.14) | copy-start | bytes 580
  4.8 13.0 %copy-start.1 = (f32[256,256]{1,0:T(8,128)S(1)}, f32[256,256]{1,0:T(8,128)}, u32[]{:S(2)}) copy-start(f32[256,256]{1,0:T(8,128)} %param.18) | copy-start | bytes 786436
  5.6 20.9 %all-to-all-start = ((f32[16,32,256]{2,1,0:T(8,128)}), f32[16,32,256]{2,1,0:T(8,128)S(1)}, u32[]{:S(2)}, u32[]{:S(2)}) async-start(f32[16,32,256]{2,1,0:T(8,128)} %pad_maximum_fusion), calls=%async_computation | async-start | bytes 1048576 | tf_op jit(solution)/shard_map/normal/all_to_all | solution.py:341
  13.6 9.9 %collective-permute-start.2 = (f32[256,256]{1,0:T(8,128)S(1)}, f32[256,256]{1,0:T(8,128)}, u32[]{:S(2)}, u32[]{:S(2)}) collective-permute-start(f32[256,256]{1,0:T(8,128)S(1)} %collective-permute-done), channel_id=1, source_target_pairs={{0,32},{16,48},{32,64},{48,80},{64,96},{80,112},{96,128},{112,144}... | collective-permute-start | bytes 786440 | tf_op jit(solution)/shard_map/gather_second/ppermute | solution.py:292
  15.6 8.5 %collective-permute-start.3 = (f32[256,256]{1,0:T(8,128)S(1)}, f32[256,256]{1,0:T(8,128)S(1)}, u32[]{:S(2)}, u32[]{:S(2)}) collective-permute-start(f32[256,256]{1,0:T(8,128)S(1)} %collective-permute-done.1), channel_id=1, source_target_pairs={{0,224},{16,240},{32,0},{48,16},{64,32},{80,48},{96,64},{112,80},{... | collective-permute-start | bytes 786440 | tf_op jit(solution)/shard_map/gather_second/ppermute | solution.py:292
  23.6 13.8 %collective-permute-start.4 = (f32[256,256]{1,0:T(8,128)}, f32[256,256]{1,0:T(8,128)S(1)}, u32[]{:S(2)}, u32[]{:S(2)}) collective-permute-start(f32[256,256]{1,0:T(8,128)} %collective-permute-done.2), channel_id=1, source_target_pairs={{0,32},{16,48},{32,64},{48,80},{64,96},{80,112},{96,128},{112,144}... | collective-permute-start | bytes 786440 | tf_op jit(solution)/shard_map/gather_second/ppermute | solution.py:292
  24.1 14.8 %collective-permute-start.5 = (f32[256,256]{1,0:T(8,128)S(1)}, f32[256,256]{1,0:T(8,128)S(1)}, u32[]{:S(2)}, u32[]{:S(2)}) collective-permute-start(f32[256,256]{1,0:T(8,128)S(1)} %collective-permute-done.3), channel_id=1, source_target_pairs={{0,224},{16,240},{32,0},{48,16},{64,32},{80,48},{96,64},{112,80},{... | collective-permute-start | bytes 786440 | tf_op jit(solution)/shard_map/gather_second/ppermute | solution.py:292
  27.3 20.2 %all-to-all-start.1 = ((f32[16,16,256]{2,1,0:T(8,128)}), f32[16,16,256]{2,1,0:T(8,128)}, u32[]{:S(2)}, u32[]{:S(2)}) async-start(f32[16,16,256]{2,1,0:T(8,128)} %broadcast_in_dim.41), calls=%async_computation.1 | async-start | bytes 524288 | tf_op jit(solution)/shard_map/normal/all_to_all | solution.py:343
  37.0 10.2 %copy-start.8 = (s32[48,1]{0,1:T(1,128)S(1)}, s32[48,1]{0,1:T(1,128)}, u32[]{:S(2)}) copy-start(s32[48,1]{0,1:T(1,128)} %param.15) | copy-start | bytes 580
  37.1 12.2 %copy-start.2 = (f32[1280,256]{1,0:T(8,128)}, f32[1280,256]{1,0:T(8,128)S(1)}, u32[]{:S(2)}) copy-start(f32[1280,256]{1,0:T(8,128)S(1)} %constant_dynamic-update-slice_fusion) | copy-start | bytes 3932164
  37.1 19.8 %collective-permute-start.8 = (f32[1280,256]{1,0:T(8,128)S(1)}, f32[1280,256]{1,0:T(8,128)S(1)}, u32[]{:S(2)}, u32[]{:S(2)}) collective-permute-start(f32[1280,256]{1,0:T(8,128)S(1)} %constant_dynamic-update-slice_fusion), channel_id=1, source_target_pairs={{0,16},{16,0},{32,48},{48,32},{64,80},{80,64},{96,112},{112,96},{1... | collective-permute-start | bytes 3932168 | tf_op jit(solution)/shard_map/gather_second/ppermute | solution.py:304
  37.3 1.6 %copy-start.5 = (f32[256,256]{1,0:T(8,128)}, f32[256,256]{1,0:T(8,128)S(1)}, u32[]{:S(2)}) copy-start(f32[256,256]{1,0:T(8,128)S(1)} %collective-permute-done.4) | copy-start | bytes 786436
  37.3 8.7 %collective-permute-start.6 = (f32[128,256]{1,0:T(8,128)S(1)}, f32[128,256]{1,0:T(8,128)S(1)}, u32[]{:S(2)}, u32[]{:S(2)}) collective-permute-start(f32[128,256]{1,0:T(8,128)S(1)} %slice.43), channel_id=1, source_target_pairs={{0,32},{16,48},{32,64},{48,80},{64,96},{80,112},{96,128},{112,144}... | collective-permute-start | bytes 393224 | tf_op jit(solution)/shard_map/gather_second/ppermute | solution.py:292
  38.9 0.7 copy-start.6
  39.6 7.6 %collective-permute-start.7 = (f32[128,256]{1,0:T(8,128)S(1)}, f32[128,256]{1,0:T(8,128)S(1)}, u32[]{:S(2)}, u32[]{:S(2)}) collective-permute-start(f32[128,256]{1,0:T(8,128)S(1)} %slice.44), channel_id=1, source_target_pairs={{0,224},{16,240},{32,0},{48,16},{64,32},{80,48},{96,64},{112,80},{... | collective-permute-start | bytes 393224 | tf_op jit(solution)/shard_map/gather_second/ppermute | solution.py:292
  41.1 15.2 %copy-start.9 = (s32[48]{0:T(128)S(1)}, s32[48]{0:T(128)}, u32[]{:S(2)}) copy-start(s32[48]{0:T(128)} %param.17) | copy-start | bytes 580
  41.1 15.2 %copy-start.10 = (s32[48]{0:T(128)S(1)}, s32[48]{0:T(128)}, u32[]{:S(2)}) copy-start(s32[48]{0:T(128)} %param.16) | copy-start | bytes 580
  47.2 9.8 %copy-start.3 = (f32[768,256]{1,0:T(8,128)}, f32[768,256]{1,0:T(8,128)S(1)}, u32[]{:S(2)}) copy-start(f32[768,256]{1,0:T(8,128)S(1)} %constant_dynamic-update-slice_fusion.5) | copy-start | bytes 2359300
  47.2 9.7 %collective-permute-start.9 = (f32[768,256]{1,0:T(8,128)S(1)}, f32[768,256]{1,0:T(8,128)}, u32[]{:S(2)}, u32[]{:S(2)}) collective-permute-start(f32[768,256]{1,0:T(8,128)S(1)} %constant_dynamic-update-slice_fusion.5), channel_id=1, source_target_pairs={{0,16},{16,0},{32,48},{48,32},{64,80},{80,64},{96,112},{112,96},{1... | collective-permute-start | bytes 2359304 | tf_op jit(solution)/shard_map/gather_second/ppermute | solution.py:305
  49.3 22.9 %all-to-all-start.2 = ((f32[16,24,256]{2,1,0:T(8,128)}), f32[16,24,256]{2,1,0:T(8,128)}, u32[]{:S(2)}, u32[]{:S(2)}) async-start(f32[16,24,256]{2,1,0:T(8,128)} %broadcast_in_dim.42), calls=%async_computation.2 | async-start | bytes 786432 | tf_op jit(solution)/shard_map/normal/all_to_all | solution.py:348
  56.9 1.1 copy-start.4
  72.2 37.8 %all-to-all-start.3 = ((f32[16,128,256]{2,1,0:T(8,128)}), f32[16,128,256]{2,1,0:T(8,128)S(1)}, u32[]{:S(2)}, u32[]{:S(2)}) async-start(f32[16,128,256]{2,1,0:T(8,128)} %bitcast.52), calls=%async_computation.3 | async-start | bytes 4194304 | tf_op jit(solution)/shard_map/exchange/all_to_all | solution.py:366

commit v6 on v5

--- a/solution.py
+++ b/solution.py
@@ -32,57 +32,66 @@
     return jnp.dot(left, right, preferred_element_type=jnp.float32)
 
 
-def contract_kernel(table_ref, count_ref, tile_hbm, third_ref, *rest):
-    sources, rest = rest[:-7], rest[-7:]
-    out_hbm, tile_buf, second_buf, result_buf, tile_sem, second_sem, result_sem = rest
-    count = count_ref[0]
+def contract_kernel(part, table_ref, tile_hbm, third_hbm, own_hbm, other_hbm, *rest):
+    out_hbm, third_buf, tile_buf, second_buf, result_buf, third_sem, tile_sem, second_sem, result_sem = rest[-9:]
+    first = table_ref[5, part]
+    count = table_ref[5, part + 1] - first
     groups = (count + GROUP - 1) // GROUP
     slot_count, tile_edge, depth = tile_hbm.shape
     chunk = min(256, depth)
     per_chunk = chunk // tile_edge
 
-    def tile_copy(group):
-        span = pl.ds(group * GROUP, GROUP)
-        return pltpu.make_async_copy(tile_hbm.at[span], tile_buf.at[span], tile_sem.at[group])
+    def entry(row, slot):
+        return table_ref[row, jnp.minimum(first + slot, slot_count - 1)]
+
+    def third_copy():
+        return pltpu.make_async_copy(third_hbm, third_buf, third_sem)
+
+    def tile_copy(slot):
+        return pltpu.make_async_copy(tile_hbm.at[entry(3, slot)], tile_buf.at[slot], tile_sem.at[slot])
 
     def second_copy(source, slot):
-        return pltpu.make_async_copy(source.at[table_ref[0, slot]], second_buf.at[slot], second_sem.at[slot])
+        block = jnp.minimum(entry(0, slot), source.shape[0] - 1)
+        return pltpu.make_async_copy(source.at[block], second_buf.at[slot], second_sem.at[slot])
 
     def result_copy(slot):
-        return pltpu.make_async_copy(result_buf.at[slot], out_hbm.at[table_ref[2, slot]], result_sem.at[slot])
+        return pltpu.make_async_copy(result_buf.at[slot], out_hbm.at[entry(2, slot)], result_sem.at[slot])
 
     def start(group):
-        tile_copy(group).start()
         for at in range(GROUP):
             slot = group * GROUP + at
-            if len(sources) == 1:
-                second_copy(sources[0], slot).start()
-            else:
-                chosen = table_ref[3, slot]
-                for which, source in enumerate(sources):
-
-                    @pl.when(chosen == which)
-                    def _():
-                        second_copy(source, slot).start()
-
+            tile_copy(slot).start()
+            other = entry(4, slot)
+
+            @pl.when(other == 0)
+            def _():
+                second_copy(own_hbm, slot).start()
+
+            @pl.when(other != 0)
+            def _():
+                second_copy(other_hbm, slot).start()
+
+    third_copy().start()
     for group in range(AHEAD):
 
         @pl.when(group < groups)
         def _():
             start(group)
+
+    third_copy().wait()
 
     def contract(group, carry):
         @pl.when(group + AHEAD < groups)
         def _():
             start(group + AHEAD)
 
-        tile_copy(group).wait()
         for at in range(GROUP):
-            second_copy(sources[0], group * GROUP + at).wait()
+            tile_copy(group * GROUP + at).wait()
+            second_copy(own_hbm, group * GROUP + at).wait()
         for at in range(GROUP):
             slot = group * GROUP + at
             second = second_buf[slot]
-            third = third_ref[table_ref[1, slot]]
+            third = third_buf[entry(1, slot)]
             high, low = split(tile_buf[slot])
             both = jnp.concatenate([high, low], axis=0)
             total = jnp.zeros((2 * tile_edge, third.shape[1]), jnp.float32)
@@ -112,32 +121,33 @@
     lax.fori_loop(0, count, finish, 0)
 
 
-def contract_tiles(table, count, tile_values, third_blocks, sources, out_slots):
+def contract_tiles(part, table, tile_values, third_blocks, sources, out_slots, earlier=()):
     slot_count, tile_edge, depth = tile_values.shape
     rank_width = third_blocks.shape[2]
-    smem = pl.BlockSpec(memory_space=pltpu.SMEM)
-    vmem = pl.BlockSpec(memory_space=pltpu.VMEM)
     hbm = pl.BlockSpec(memory_space=pltpu.HBM)
     block = (slot_count, tile_edge, rank_width)
     return pl.pallas_call(
-        contract_kernel,
+        functools.partial(contract_kernel, part),
         out_shape=jax.ShapeDtypeStruct((out_slots, tile_edge, rank_width), jnp.float32),
-        in_specs=[smem, smem, hbm, vmem] + [hbm] * len(sources),
+        in_specs=[pl.BlockSpec(memory_space=pltpu.SMEM)] + [hbm] * (4 + len(earlier)),
         out_specs=hbm,
         scratch_shapes=[
+            pltpu.VMEM(third_blocks.shape, jnp.float32),
             pltpu.VMEM((slot_count, tile_edge, depth), jnp.float32),
             pltpu.VMEM(block, jnp.float32),
             pltpu.VMEM(block, jnp.float32),
-            pltpu.SemaphoreType.DMA((slot_count // GROUP,)),
+            pltpu.SemaphoreType.DMA,
+            pltpu.SemaphoreType.DMA((slot_count,)),
             pltpu.SemaphoreType.DMA((slot_count,)),
             pltpu.SemaphoreType.DMA((slot_count,)),
         ],
+        input_output_aliases={5: 0} if earlier else {},
         compiler_params=pltpu.CompilerParams(vmem_limit_bytes=60 * 1024 * 1024),
         cost_estimate=pl.CostEstimate(
-            flops=6 * slot_count * tile_edge * depth * rank_width, bytes_accessed=10_000_000, transcendentals=0
+            flops=3 * slot_count * tile_edge * depth * rank_width, bytes_accessed=5_000_000, transcendentals=0
         ),
         name="contract",
-    )(table, count, tile_values, third_blocks, *sources)
+    )(table, tile_values, third_blocks, *sources, *earlier)
 
 
 def combine_kernel(target_ref, received_ref, inverse_ref, out_ref, total_ref):
@@ -300,9 +310,7 @@
         middle = mode2_factor.shape[0] // 2
         up_4, down_4 = moved(up_3[:middle], 1), moved(down_3[middle:], -1)
         near_own = jnp.concatenate([mode2_factor, up_1, down_1, up_2, down_2], axis=0)
-        far_own = jnp.concatenate([up_3, down_3, up_4, down_4], axis=0)
         near_other = lax.ppermute(near_own, "row", twin)
-        far_other = lax.ppermute(far_own, "row", twin)
 
     with jax.named_scope("tables"):
         slot_index = jnp.arange(slot_count, dtype=jnp.int32)
@@ -328,13 +336,36 @@
                 place * JB_DEV + jnp.clip(mode2_offset, 0, JB_DEV - 1),
                 jnp.clip(mode3_offset, 0, mode3_factor.shape[0] // tile_edge - 1),
                 out_slot,
-                is_far + 2 * is_other,
+                slot_index,
+                is_other,
             ]
-        ).astype(jnp.int32)
+        ).astype(jnp.float32)
+        group = jnp.where(is_live, is_far, 2)
+        ahead = (group[:, None] < group[None, :]) | (
+            (group[:, None] == group[None, :]) & (slot_index[:, None] < slot_index[None, :])
+        )
+        position = jnp.sum(ahead.astype(jnp.int32), axis=0)
+        placed = (position[:, None] == slot_index[None, :]).astype(jnp.float32)
+        near_count = jnp.sum((group == 0).astype(jnp.int32))
+        bounds = jnp.where(slot_index == 1, near_count, jnp.where(slot_index == 2, tile_count[0], 0))
+        table = jnp.dot(table, placed, precision=HIGHEST)
+        table = jnp.concatenate([table.astype(jnp.int32), bounds[None, :]], axis=0)
         slots = jnp.arange(SLOTS, dtype=jnp.float32)
         taken = chosen[:, None, :] * (rank[:, None, :] == slots[None, :, None])
         targets = jnp.sum(taken * (mode1_offset + 1).astype(jnp.float32), axis=2) - 1.0
         target_rows = jnp.zeros((8, rank_width), jnp.float32).at[0, : n_col * SLOTS].set(targets.reshape(-1))
+
+    def blocks(array):
+        return array.reshape(-1, tile_edge, rank_width)
+
+    with jax.named_scope("contract"):
+        near_partials = contract_tiles(
+            0, table, tile_values, blocks(mode3_factor), [blocks(near_own), blocks(near_other)], n_col * SLOTS
+        )
+    with jax.named_scope("gather_far"):
+        up_4, down_4, near_partials = lax.optimization_barrier((up_4, down_4, near_partials))
+        far_own = jnp.concatenate([up_3, down_3, up_4, down_4], axis=0)
+        far_other = lax.ppermute(far_own, "row", twin)
 
     with jax.named_scope("normal"):
         strips = [gram_of(each).reshape(n_col, part, rank_width) for each in (mode2_factor, mode3_factor)]
@@ -351,16 +382,14 @@
         received_targets = received_targets.astype(jnp.int32).reshape(-1)
 
     with jax.named_scope("contract"):
-        def blocks(array):
-            return array.reshape(-1, tile_edge, rank_width)
-
         partials = contract_tiles(
+            1,
             table,
-            tile_count,
             tile_values,
             blocks(mode3_factor),
-            [blocks(near_own), blocks(far_own), blocks(near_other), blocks(far_other)],
+            [blocks(far_own), blocks(far_other)],
             n_col * SLOTS,
+            (near_partials,),
         )
     with jax.named_scope("exchange"):
         received = lax.all_to_all(

time: 114 us -> 117 us (1.026)
  Pallas kernels: 32.7 us -> 36.9 us
  waiting for transfers between devices: 23.7 us -> 22 us
  other arithmetic: 2.71 us -> 4.15 us
    ppermute x8, waiting for transfers between devices: 11.2 us -> 6.43 us  [moved(): return lax.ppermute(array, 'row', pairs)]
    pallas_call x1 -> x2, Pallas kernels: 14.2 us -> 18.4 us  [contract_tiles(): pl.pallas_call(functools.partial(contract_kernel, part), out_shape=jax.Sh...]
    all_to_all x1, waiting for transfers between devices: 12.5 us -> 14.6 us  [local(): lax.all_to_all(partials.reshape(n_col, SLOTS * tile_edge, rank_width), 'c...]
    unnamed x31 -> x33, local copies, waits for them, and re-layouts: 4.76 us -> 4 us
  transfers between devices with their start and end apart: 14 -> 14, of which waited for: 5 -> 4; matrix products, arithmetic and copies ran while one was open for 11% -> 11% of each run, Pallas kernels for 27% -> 30%
where the time goes in v6:
time: 117 us; the launch traced here: 116 us
  starting transfers between devices  41.1 us (35%)
  Pallas kernels  36.9 us (32%)
  waiting for transfers between devices  22 us (19%)
  local copies, waits for them, and re-layouts  7.73 us (7%)
  other arithmetic  4.15 us (4%)
  matrix products  3.04 us (3%)
    pallas_call x2, Pallas kernels, contract_tiles(): pl.pallas_call(functools.partial(contract_kernel, part), out_shape=jax.Sh...  18.4 us
    pallas_call x1, Pallas kernels, invert(): pl.pallas_call(functools.partial(invert_kernel, block), out_shape=jax.Sha...  16 us
    all_to_all x1, waiting for transfers between devices, local(): lax.all_to_all(partials.reshape(n_col, SLOTS * tile_edge, rank_width), 'c...  14.6 us
    ppermute x8, starting transfers between devices, moved(): return lax.ppermute(array, 'row', pairs)  11.3 us
    all_to_all x1, starting transfers between devices, local(): lax.all_to_all(jnp.broadcast_to(strips[None, :part], (n_row, part, rank_w...  8.52 us
    all_to_all x1, starting transfers between devices, local(): lax.all_to_all(jnp.broadcast_to(sent[None], (n_col,) + sent.shape), 'col'...  8.03 us
    all_to_all x1, starting transfers between devices, local(): strips = lax.all_to_all(jnp.concatenate(strips, axis=1), 'col', 0, 0)  7.03 us
    ppermute x8, waiting for transfers between devices, moved(): return lax.ppermute(array, 'row', pairs)  6.43 us
  transfers between devices with their start and end apart: 14, of which 4 were waited for; matrix products, arithmetic and copies ran while one was open for 11% of the time, Pallas kernels for 30%

profile of v6, /device:TPU:32, one launch (start us, length us, event | category | flops | bytes accessed | tf_op | source)
XLA Modules:
  0.0 116.1 jit_solution(13384739984786435485)
XLA Ops:
  0.0 1.9 %collective-permute-start = (f32[256,256]{1,0:T(8,128)}, f32[256,256]{1,0:T(8,128)S(1)}, u32[]{:S(2)}, u32[]{:S(2)}) collective-permute-start(f32[256,256]{1,0:T(8,128)} %param.18), channel_id=1, source_target_pairs={{0,32},{16,48},{32,64},{48,80},{64,96},{80,112},{96,128},{112,144}... | collective-permute-start | bytes 786440 | tf_op jit(solution)/shard_map/gather_second/ppermute | solution.py:302
  1.9 0.1 collective-permute-start.3
  2.0 1.7 %fusion.25 = f32[256,256]{1,0:T(8,128)S(1)} fusion(f32[256,256]{1,0:T(8,128)} %param.18), kind=kOutput, calls=%fused_computation.83 | convolution fusion | flops 201326592 | bytes 524288 | tf_op jit(solution)/shard_map/normal/dot_general | solution.py:20
  3.7 1.0 fusion.26
  4.8 0.0 copy-start.10
  4.8 0.0 copy-start.11
  4.8 0.0 copy-start.9
  4.8 0.0 copy-start.1
  4.8 0.8 pad_maximum_fusion
  5.7 7.0 %all-to-all-start = ((f32[16,32,256]{2,1,0:T(8,128)}), f32[16,32,256]{2,1,0:T(8,128)S(1)}, u32[]{:S(2)}, u32[]{:S(2)}) async-start(f32[16,32,256]{2,1,0:T(8,128)} %pad_maximum_fusion), calls=%async_computation | async-start | bytes 1048576 | tf_op jit(solution)/shard_map/normal/all_to_all | solution.py:372
  13.4 0.1 select_reduce_fusion
  13.7 0.7 fusion.18
  14.3 1.9 %collective-permute-start.1 = (f32[256,256]{1,0:T(8,128)S(1)}, f32[256,256]{1,0:T(8,128)S(1)}, u32[]{:S(2)}, u32[]{:S(2)}) collective-permute-start(f32[256,256]{1,0:T(8,128)S(1)} %collective-permute-done), channel_id=1, source_target_pairs={{0,32},{16,48},{32,64},{48,80},{64,96},{80,112},{96,128},{112,144}... | collective-permute-start | bytes 786440 | tf_op jit(solution)/shard_map/gather_second/ppermute | solution.py:302
  16.3 2.2 %collective-permute-start.4 = (f32[256,256]{1,0:T(8,128)S(1)}, f32[256,256]{1,0:T(8,128)}, u32[]{:S(2)}, u32[]{:S(2)}) collective-permute-start(f32[256,256]{1,0:T(8,128)S(1)} %collective-permute-done.3), channel_id=1, source_target_pairs={{0,224},{16,240},{32,0},{48,16},{64,32},{80,48},{96,64},{112,80},{... | collective-permute-start | bytes 786440 | tf_op jit(solution)/shard_map/gather_second/ppermute | solution.py:302
  18.6 5.5 %collective-permute-done.1 = f32[256,256]{1,0:T(8,128)S(1)} collective-permute-done((f32[256,256]{1,0:T(8,128)S(1)}, f32[256,256]{1,0:T(8,128)S(1)}, u32[]{:S(2)}, u32[]{:S(2)}) %collective-permute-start.1) | collective-permute-done | bytes 262176 | tf_op jit(solution)/shard_map/gather_second/ppermute | solution.py:302
  24.1 0.9 collective-permute-done.4
  25.0 1.0 constant_dynamic-update-slice_fusion
  26.0 0.1 collective-permute-start.8
  26.1 0.1 convert_reduce_fusion
  26.2 0.2 convolution_convert_fusion
  26.4 3.0 %collective-permute-start.2 = (f32[256,256]{1,0:T(8,128)}, f32[256,256]{1,0:T(8,128)S(1)}, u32[]{:S(2)}, u32[]{:S(2)}) collective-permute-start(f32[256,256]{1,0:T(8,128)} %copy-done.7), channel_id=1, source_target_pairs={{0,32},{16,48},{32,64},{48,80},{64,96},{80,112},{96,128},{112,144}... | collective-permute-start | bytes 786440 | tf_op jit(solution)/shard_map/gather_second/ppermute | solution.py:302
  29.4 0.6 compare_select_fusion.7
  30.1 0.6 pad_add_fusion.table_ref
  30.7 0.1 multiply_reduce_fusion
  30.8 0.7 broadcast_in_dim.34
  31.6 8.5 %all-to-all-start.1 = ((f32[16,16,256]{2,1,0:T(8,128)}), f32[16,16,256]{2,1,0:T(8,128)}, u32[]{:S(2)}, u32[]{:S(2)}) async-start(f32[16,16,256]{2,1,0:T(8,128)} %broadcast_in_dim.34), calls=%async_computation.1 | async-start | bytes 524288 | tf_op jit(solution)/shard_map/normal/all_to_all | solution.py:374
  40.1 1.5 %collective-permute-start.6 = (f32[128,256]{1,0:T(8,128)S(1)}, f32[128,256]{1,0:T(8,128)S(1)}, u32[]{:S(2)}, u32[]{:S(2)}) collective-permute-start(f32[128,256]{1,0:T(8,128)S(1)} %slice.43), channel_id=1, source_target_pairs={{0,32},{16,48},{32,64},{48,80},{64,96},{80,112},{96,128},{112,144}... | collective-permute-start | bytes 393224 | tf_op jit(solution)/shard_map/gather_second/ppermute | solution.py:302
  41.7 0.9 slice.44
  42.6 0.6 collective-permute-start.7
  43.2 1.0 constant_dynamic-update-slice_fusion.8
  44.2 1.0 constant_dynamic-update-slice_fusion.7
  45.2 1.1 copy-done.4
  46.2 9.7 %contract.2.rest_0_ = f32[64,32,256]{2,1,0:T(8,128)} custom-call(s32[6,48]{1,0:T(8,128)} %pad_add_fusion.table_ref, f32[48,32,1024]{2,1,0:T(8,128)} %tile_hbm.3, f32[16,32,256]{2,1,0:T(8,128)} %bitcast.46, f32[40,32,256]{2,1,0:T(8,128)} %bitcast.48, f32[40,32,256]{2,1,0:T(8,128)} %bitcast.50), custom_call_target="tpu_custom_call" | custom-call | flops 1207959552 | bytes 5000000 | tf_op jit(solution)/shard_map/contract/contract/pallas_call | solution.py:129
  56.0 0.1 collective-permute-start.9
  56.1 0.1 copy.13
  56.2 0.1 sub.34
  56.3 1.0 reduce_sum.55
  57.3 0.8 broadcast_in_dim.35
  58.1 8.0 %all-to-all-start.2 = ((f32[16,24,256]{2,1,0:T(8,128)}), f32[16,24,256]{2,1,0:T(8,128)S(1)}, u32[]{:S(2)}, u32[]{:S(2)}) async-start(f32[16,24,256]{2,1,0:T(8,128)} %broadcast_in_dim.35), calls=%async_computation.2 | async-start | bytes 786432 | tf_op jit(solution)/shard_map/normal/all_to_all | solution.py:379
  66.2 0.9 copy-done.5
  67.0 8.7 %contract.3 = f32[64,32,256]{2,1,0:T(8,128)} custom-call(s32[6,48]{1,0:T(8,128)} %pad_add_fusion.table_ref, f32[48,32,1024]{2,1,0:T(8,128)} %tile_hbm.3, f32[16,32,256]{2,1,0:T(8,128)} %bitcast.47, f32[24,32,256]{2,1,0:T(8,128)} %bitcast.49, f32[24,32,256]{2,1,0:T(8,128)} %bitcast.53, f32[64,32,256]{2,1,0:T(8,128)} %contract.2.rest_0_), custom_call_target="tpu_custom_call", output_to_operand_aliasing={{}: (5, {})} | custom-call | flops 1207959552 | bytes 5000000 | tf_op jit(solution)/shard_map/contract/contract/pallas_call | solution.py:129
  75.7 0.9 all-to-all-done.2
  76.6 6.0 %all-to-all-start.3 = ((f32[16,128,256]{2,1,0:T(8,128)}), f32[16,128,256]{2,1,0:T(8,128)S(1)}, u32[]{:S(2)}, u32[]{:S(2)}) async-start(f32[16,128,256]{2,1,0:T(8,128)} %bitcast.45), calls=%async_computation.3 | async-start | bytes 4194304 | tf_op jit(solution)/shard_map/exchange/all_to_all | solution.py:395
  82.7 0.1 convert_reduce_fusion.1
  82.8 0.1 convert_element_type.68.target_ref
  82.9 16.0 %invert.1.inverse_ref = f32[256,256]{1,0:T(8,128)S(1)} custom-call(f32[256,256]{1,0:T(8,128)S(1)} %bitcast.44), custom_call_target="tpu_custom_call" | custom-call | flops 201326592 | bytes 524288 | tf_op jit(solution)/shard_map/inverse/invert/pallas_call | solution.py:267
  98.9 14.6 %all-to-all-done.3 = f32[16,128,256]{2,1,0:T(8,128)S(1)} async-done(((f32[16,128,256]{2,1,0:T(8,128)}), f32[16,128,256]{2,1,0:T(8,128)S(1)}, u32[]{:S(2)}, u32[]{:S(2)}) %all-to-all-start.3) | async-done | bytes 2097184 | tf_op jit(solution)/shard_map/exchange/all_to_all | solution.py:395
  113.6 2.5 %combine.1 = f32[512,256]{1,0:T(8,128)} custom-call(s32[64]{0:T(128)S(1)} %convert_element_type.68.target_ref, f32[64,32,256]{2,1,0:T(8,128)S(1)} %bitcast.43, f32[256,256]{1,0:T(8,128)S(1)} %invert.1.inverse_ref), custom_call_target="tpu_custom_call" | custom-call | tf_op jit(solution)/shard_map/combine/combine/pallas_call | solution.py:178
  (55 shorter events, 0.4 us)
Async XLA Ops:
  0.0 3.7 %copy-start = (f32[512,256]{1,0:T(8,128)S(1)}, f32[512,256]{1,0:T(8,128)}, u32[]{:S(2)}) copy-start(f32[512,256]{1,0:T(8,128)} %param.19) | copy-start | bytes 1572868
  0.0 14.3 %collective-permute-start = (f32[256,256]{1,0:T(8,128)}, f32[256,256]{1,0:T(8,128)S(1)}, u32[]{:S(2)}, u32[]{:S(2)}) collective-permute-start(f32[256,256]{1,0:T(8,128)} %param.18), channel_id=1, source_target_pairs={{0,32},{16,48},{32,64},{48,80},{64,96},{80,112},{96,128},{112,144}... | collective-permute-start | bytes 786440 | tf_op jit(solution)/shard_map/gather_second/ppermute | solution.py:302
  1.9 14.4 %collective-permute-start.3 = (f32[256,256]{1,0:T(8,128)}, f32[256,256]{1,0:T(8,128)S(1)}, u32[]{:S(2)}, u32[]{:S(2)}) collective-permute-start(f32[256,256]{1,0:T(8,128)} %param.18), channel_id=1, source_target_pairs={{0,224},{16,240},{32,0},{48,16},{64,32},{80,48},{96,64},{112,80},{... | collective-permute-start | bytes 786440 | tf_op jit(solution)/shard_map/gather_second/ppermute | solution.py:302
  4.8 8.6 %copy-start.10 = (s32[48,1]{0,1:T(1,128)S(1)}, s32[48,1]{0,1:T(1,128)}, u32[]{:S(2)}) copy-start(s32[48,1]{0,1:T(1,128)} %param.13) | copy-start | bytes 580
  4.8 8.8 %copy-start.11 = (s32[48]{0:T(128)S(1)}, s32[48]{0:T(128)}, u32[]{:S(2)}) copy-start(s32[48]{0:T(128)} %param.17) | copy-start | bytes 580
  4.8 8.8 %copy-start.8 = (s32[48,1]{0,1:T(1,128)S(1)}, s32[48,1]{0,1:T(1,128)}, u32[]{:S(2)}) copy-start(s32[48,1]{0,1:T(1,128)} %param.15) | copy-start | bytes 580
  4.8 8.8 %copy-start.9 = (s32[48]{0:T(128)S(1)}, s32[48]{0:T(128)}, u32[]{:S(2)}) copy-start(s32[48]{0:T(128)} %param.16) | copy-start | bytes 580
  4.8 11.4 %copy-start.1 = (f32[256,256]{1,0:T(8,128)S(1)}, f32[256,256]{1,0:T(8,128)}, u32[]{:S(2)}) copy-start(f32[256,256]{1,0:T(8,128)} %param.18) | copy-start | bytes 786436
  5.7 25.1 %all-to-all-start = ((f32[16,32,256]{2,1,0:T(8,128)}), f32[16,32,256]{2,1,0:T(8,128)S(1)}, u32[]{:S(2)}, u32[]{:S(2)}) async-start(f32[16,32,256]{2,1,0:T(8,128)} %pad_maximum_fusion), calls=%async_computation | async-start | bytes 1048576 | tf_op jit(solution)/shard_map/normal/all_to_all | solution.py:372
  14.3 12.1 %copy-start.12 = (s32[48]{0:T(128)S(1)}, s32[48]{0:T(128)}, u32[]{:S(2)}) copy-start(s32[48]{0:T(128)} %param.14) | copy-start | bytes 580
  14.3 9.8 %collective-permute-start.1 = (f32[256,256]{1,0:T(8,128)S(1)}, f32[256,256]{1,0:T(8,128)S(1)}, u32[]{:S(2)}, u32[]{:S(2)}) collective-permute-start(f32[256,256]{1,0:T(8,128)S(1)} %collective-permute-done), channel_id=1, source_target_pairs={{0,32},{16,48},{32,64},{48,80},{64,96},{80,112},{96,128},{112,144}... | collective-permute-start | bytes 786440 | tf_op jit(solution)/shard_map/gather_second/ppermute | solution.py:302
  16.3 8.7 %collective-permute-start.4 = (f32[256,256]{1,0:T(8,128)S(1)}, f32[256,256]{1,0:T(8,128)}, u32[]{:S(2)}, u32[]{:S(2)}) collective-permute-start(f32[256,256]{1,0:T(8,128)S(1)} %collective-permute-done.3), channel_id=1, source_target_pairs={{0,224},{16,240},{32,0},{48,16},{64,32},{80,48},{96,64},{112,80},{... | collective-permute-start | bytes 786440 | tf_op jit(solution)/shard_map/gather_second/ppermute | solution.py:302
  24.1 0.9 copy-start.7
  26.0 19.2 %copy-start.2 = (f32[1280,256]{1,0:T(8,128)}, f32[1280,256]{1,0:T(8,128)S(1)}, u32[]{:S(2)}) copy-start(f32[1280,256]{1,0:T(8,128)S(1)} %constant_dynamic-update-slice_fusion) | copy-start | bytes 3932164
  26.0 19.2 %collective-permute-start.8 = (f32[1280,256]{1,0:T(8,128)S(1)}, f32[1280,256]{1,0:T(8,128)S(1)}, u32[]{:S(2)}, u32[]{:S(2)}) collective-permute-start(f32[1280,256]{1,0:T(8,128)S(1)} %constant_dynamic-update-slice_fusion), channel_id=1, source_target_pairs={{0,16},{16,0},{32,48},{48,32},{64,80},{80,64},{96,112},{112,96},{1... | collective-permute-start | bytes 3932168 | tf_op jit(solution)/shard_map/gather_second/ppermute | solution.py:313
  26.4 13.7 %collective-permute-start.2 = (f32[256,256]{1,0:T(8,128)}, f32[256,256]{1,0:T(8,128)S(1)}, u32[]{:S(2)}, u32[]{:S(2)}) collective-permute-start(f32[256,256]{1,0:T(8,128)} %copy-done.7), channel_id=1, source_target_pairs={{0,32},{16,48},{32,64},{48,80},{64,96},{80,112},{96,128},{112,144}... | collective-permute-start | bytes 786440 | tf_op jit(solution)/shard_map/gather_second/ppermute | solution.py:302
  29.4 12.2 %collective-permute-start.5 = (f32[256,256]{1,0:T(8,128)}, f32[256,256]{1,0:T(8,128)}, u32[]{:S(2)}, u32[]{:S(2)}) collective-permute-start(f32[256,256]{1,0:T(8,128)} %collective-permute-done.4), channel_id=1, source_target_pairs={{0,224},{16,240},{32,0},{48,16},{64,32},{80,48},{96,64},{112,80},{... | collective-permute-start | bytes 786440 | tf_op jit(solution)/shard_map/gather_second/ppermute | solution.py:302
  31.6 24.7 %all-to-all-start.1 = ((f32[16,16,256]{2,1,0:T(8,128)}), f32[16,16,256]{2,1,0:T(8,128)}, u32[]{:S(2)}, u32[]{:S(2)}) async-start(f32[16,16,256]{2,1,0:T(8,128)} %broadcast_in_dim.34), calls=%async_computation.1 | async-start | bytes 524288 | tf_op jit(solution)/shard_map/normal/all_to_all | solution.py:374
  40.1 2.5 %copy-start.6 = (f32[256,256]{1,0:T(8,128)}, f32[256,256]{1,0:T(8,128)S(1)}, u32[]{:S(2)}) copy-start(f32[256,256]{1,0:T(8,128)S(1)} %collective-permute-done.2) | copy-start | bytes 786436
  40.1 15.8 %collective-permute-start.6 = (f32[128,256]{1,0:T(8,128)S(1)}, f32[128,256]{1,0:T(8,128)S(1)}, u32[]{:S(2)}, u32[]{:S(2)}) collective-permute-start(f32[128,256]{1,0:T(8,128)S(1)} %slice.43), channel_id=1, source_target_pairs={{0,32},{16,48},{32,64},{48,80},{64,96},{80,112},{96,128},{112,144}... | collective-permute-start | bytes 393224 | tf_op jit(solution)/shard_map/gather_second/ppermute | solution.py:302
  42.6 13.4 %collective-permute-start.7 = (f32[128,256]{1,0:T(8,128)S(1)}, f32[128,256]{1,0:T(8,128)S(1)}, u32[]{:S(2)}, u32[]{:S(2)}) collective-permute-start(f32[128,256]{1,0:T(8,128)S(1)} %slice.44), channel_id=1, source_target_pairs={{0,224},{16,240},{32,0},{48,16},{64,32},{80,48},{96,64},{112,80},{... | collective-permute-start | bytes 393224 | tf_op jit(solution)/shard_map/gather_second/ppermute | solution.py:302
  45.2 1.1 copy-start.4
  56.0 10.1 %copy-start.3 = (f32[768,256]{1,0:T(8,128)}, f32[768,256]{1,0:T(8,128)S(1)}, u32[]{:S(2)}) copy-start(f32[768,256]{1,0:T(8,128)S(1)} %constant_dynamic-update-slice_fusion.5) | copy-start | bytes 2359300
  56.0 10.1 %collective-permute-start.9 = (f32[768,256]{1,0:T(8,128)S(1)}, f32[768,256]{1,0:T(8,128)S(1)}, u32[]{:S(2)}, u32[]{:S(2)}) collective-permute-start(f32[768,256]{1,0:T(8,128)S(1)} %constant_dynamic-update-slice_fusion.5), channel_id=1, source_target_pairs={{0,16},{16,0},{32,48},{48,32},{64,80},{80,64},{96,112},{112,96},{1... | collective-permute-start | bytes 2359304 | tf_op jit(solution)/shard_map/gather_far/ppermute | solution.py:368
  58.1 18.5 %all-to-all-start.2 = ((f32[16,24,256]{2,1,0:T(8,128)}), f32[16,24,256]{2,1,0:T(8,128)S(1)}, u32[]{:S(2)}, u32[]{:S(2)}) async-start(f32[16,24,256]{2,1,0:T(8,128)} %broadcast_in_dim.35), calls=%async_computation.2 | async-start | bytes 786432 | tf_op jit(solution)/shard_map/normal/all_to_all | solution.py:379
  66.1 0.9 copy-start.5
  76.6 37.0 %all-to-all-start.3 = ((f32[16,128,256]{2,1,0:T(8,128)}), f32[16,128,256]{2,1,0:T(8,128)S(1)}, u32[]{:S(2)}, u32[]{:S(2)}) async-start(f32[16,128,256]{2,1,0:T(8,128)} %bitcast.45), calls=%async_computation.3 | async-start | bytes 4194304 | tf_op jit(solution)/shard_map/exchange/all_to_all | solution.py:395

commit v7 on v5

--- a/solution.py
+++ b/solution.py
@@ -284,6 +284,12 @@
     n_col = lax.axis_size("col")
     part = rank_width // n_col
 
+    with jax.named_scope("normal"):
+        strips = [gram_of(each).reshape(n_col, part, rank_width) for each in (mode2_factor, mode3_factor)]
+        strips = jnp.concatenate(strips, axis=1)
+        held_second, strips = lax.optimization_barrier((mode2_factor, strips))
+        strips = lax.all_to_all(strips, "col", 0, 0)
+
     with jax.named_scope("gather_second"):
         n_z = n_row // 2
 
@@ -294,13 +300,12 @@
         near = [1, n_z - 1, 2, n_z - 2]
         far = [3, n_z - 3, 4]
         twin = [(i, i ^ 1) for i in range(n_row)]
-        up_1, down_1 = moved(mode2_factor, 1), moved(mode2_factor, -1)
+        up_1, down_1 = moved(held_second, 1), moved(held_second, -1)
+        across = moved(held_second, n_z // 2)
         up_2, down_2 = moved(up_1, 1), moved(down_1, -1)
         up_3, down_3 = moved(up_2, 1), moved(down_2, -1)
-        middle = mode2_factor.shape[0] // 2
-        up_4, down_4 = moved(up_3[:middle], 1), moved(down_3[middle:], -1)
         near_own = jnp.concatenate([mode2_factor, up_1, down_1, up_2, down_2], axis=0)
-        far_own = jnp.concatenate([up_3, down_3, up_4, down_4], axis=0)
+        far_own = jnp.concatenate([up_3, down_3, across], axis=0)
         near_other = lax.ppermute(near_own, "row", twin)
         far_other = lax.ppermute(far_own, "row", twin)
 
@@ -337,8 +342,6 @@
         target_rows = jnp.zeros((8, rank_width), jnp.float32).at[0, : n_col * SLOTS].set(targets.reshape(-1))
 
     with jax.named_scope("normal"):
-        strips = [gram_of(each).reshape(n_col, part, rank_width) for each in (mode2_factor, mode3_factor)]
-        strips = lax.all_to_all(jnp.concatenate(strips, axis=1), "col", 0, 0)
         strips = jnp.sum(strips, axis=0)
         second_strips = lax.all_to_all(
             jnp.broadcast_to(strips[None, :part], (n_row, part, rank_width)), "row", 0, 0

time: 114 us -> 124 us (1.088)
  waiting for transfers between devices: 23.7 us -> 34.2 us
  local copies, waits for them, and re-layouts: 8.46 us -> 3.89 us
  starting transfers between devices: 41.1 us -> 44.3 us
    all_to_all x1, waiting for transfers between devices: 0.01 us -> 7.16 us  [local(): lax.all_to_all(jnp.broadcast_to(strips[None, :part], (n_row, part, rank_w...]
    unnamed x31 -> x22, local copies, waits for them, and re-layouts: 4.76 us -> 2.06 us
    ppermute x8 -> x7, starting transfers between devices: 10.8 us -> 13.1 us  [moved(): return lax.ppermute(array, 'row', pairs)]
    all_to_all x1, waiting for transfers between devices: 12.5 us -> 14.4 us  [local(): lax.all_to_all(partials.reshape(n_col, SLOTS * tile_edge, rank_width), 'c...]
    ppermute x8 -> x7, waiting for transfers between devices: 11.2 us -> 12.6 us  [moved(): return lax.ppermute(array, 'row', pairs)]
  transfers between devices with their start and end apart: 14 -> 13, of which waited for: 5 -> 4; matrix products, arithmetic and copies ran while one was open for 11% -> 4% of each run, Pallas kernels for 27% -> 26%
where the time goes in v7:
time: 124 us; the launch traced here: 122 us
  starting transfers between devices  44.3 us (36%)
  waiting for transfers between devices  34.2 us (28%)
  Pallas kernels  33.7 us (27%)
  local copies, waits for them, and re-layouts  3.89 us (3%)
  matrix products  2.98 us (2%)
  other arithmetic  1.77 us (1%)
    pallas_call x1, Pallas kernels, invert(): pl.pallas_call(functools.partial(invert_kernel, block), out_shape=jax.Sha...  16 us
    pallas_call x1, Pallas kernels, contract_tiles(): pl.pallas_call(contract_kernel, out_shape=jax.ShapeDtypeStruct((out_slots...  15.2 us
    all_to_all x1, waiting for transfers between devices, local(): lax.all_to_all(partials.reshape(n_col, SLOTS * tile_edge, rank_width), 'c...  14.4 us
    ppermute x7, starting transfers between devices, moved(): return lax.ppermute(array, 'row', pairs)  13.1 us
    ppermute x7, waiting for transfers between devices, moved(): return lax.ppermute(array, 'row', pairs)  12.6 us
    all_to_all x1, starting transfers between devices, local(): lax.all_to_all(jnp.broadcast_to(strips[None, :part], (n_row, part, rank_w...  9.86 us
    all_to_all x1, waiting for transfers between devices, local(): lax.all_to_all(jnp.broadcast_to(strips[None, :part], (n_row, part, rank_w...  7.16 us
    all_to_all x1, starting transfers between devices, local(): lax.all_to_all(jnp.broadcast_to(sent[None], (n_col,) + sent.shape), 'col'...  7.04 us
  transfers between devices with their start and end apart: 13, of which 4 were waited for; matrix products, arithmetic and copies ran while one was open for 4% of the time, Pallas kernels for 26%

profile of v7, /device:TPU:32, one launch (start us, length us, event | category | flops | bytes accessed | tf_op | source)
XLA Modules:
  0.0 121.8 jit_solution(2846251760292117202)
XLA Ops:
  0.0 2.2 %fusion.18 = f32[256,256]{1,0:T(8,128)S(1)} fusion(f32[512,256]{1,0:T(8,128)} %param.19), kind=kOutput, calls=%fused_computation.66 | convolution fusion | flops 402653184 | bytes 786432 | tf_op jit(solution)/shard_map/normal/dot_general | solution.py:20
  2.3 0.0 copy-start.3
  2.3 0.0 copy-start.7
  2.3 0.6 fusion.17
  2.9 0.8 pad_maximum_fusion
  3.7 6.3 %collective-permute-start.6 = (f32[256,256]{1,0:T(8,128)S(1)}, f32[256,256]{1,0:T(8,128)S(1)}, u32[]{:S(2)}, u32[]{:S(2)}) collective-permute-start(f32[256,256]{1,0:T(8,128)S(1)} %copy-done), channel_id=1, source_target_pairs={{0,128},{16,144},{32,160},{48,176},{64,192},{80,208},{96,224},{112... | collective-permute-start | bytes 786440 | tf_op jit(solution)/shard_map/gather_second/ppermute | solution.py:298
  10.0 1.0 collective-permute-start.1
  11.0 1.0 collective-permute-start
  12.0 7.0 %all-to-all-start = ((f32[16,32,256]{2,1,0:T(8,128)}), f32[16,32,256]{2,1,0:T(8,128)S(1)}, u32[]{:S(2)}, u32[]{:S(2)}) async-start(f32[16,32,256]{2,1,0:T(8,128)} %pad_maximum_fusion), calls=%async_computation | async-start | bytes 1048576 | tf_op jit(solution)/shard_map/normal/all_to_all | solution.py:291
  19.8 0.1 select_reduce_fusion
  19.9 7.7 %collective-permute-done = f32[256,256]{1,0:T(8,128)S(1)} collective-permute-done((f32[256,256]{1,0:T(8,128)S(1)}, f32[256,256]{1,0:T(8,128)S(1)}, u32[]{:S(2)}, u32[]{:S(2)}) %collective-permute-start) | collective-permute-done | bytes 262176 | tf_op jit(solution)/shard_map/gather_second/ppermute | solution.py:298
  27.6 1.4 %collective-permute-start.2 = (f32[256,256]{1,0:T(8,128)S(1)}, f32[256,256]{1,0:T(8,128)S(1)}, u32[]{:S(2)}, u32[]{:S(2)}) collective-permute-start(f32[256,256]{1,0:T(8,128)S(1)} %collective-permute-done), channel_id=1, source_target_pairs={{0,32},{16,48},{32,64},{48,80},{64,96},{80,112},{96,128},{112,144}... | collective-permute-start | bytes 786440 | tf_op jit(solution)/shard_map/gather_second/ppermute | solution.py:298
  29.1 0.1 multiply_reduce_fusion
  29.1 0.0 collective-permute-done.1
  29.1 0.7 collective-permute-start.3
  29.9 4.9 %collective-permute-done.2 = f32[256,256]{1,0:T(8,128)S(1)} collective-permute-done((f32[256,256]{1,0:T(8,128)S(1)}, f32[256,256]{1,0:T(8,128)S(1)}, u32[]{:S(2)}, u32[]{:S(2)}) %collective-permute-start.2) | collective-permute-done | bytes 262176 | tf_op jit(solution)/shard_map/gather_second/ppermute | solution.py:298
  34.8 2.5 %collective-permute-start.4 = (f32[256,256]{1,0:T(8,128)S(1)}, f32[256,256]{1,0:T(8,128)}, u32[]{:S(2)}, u32[]{:S(2)}) collective-permute-start(f32[256,256]{1,0:T(8,128)S(1)} %collective-permute-done.2), channel_id=1, source_target_pairs={{0,32},{16,48},{32,64},{48,80},{64,96},{80,112},{96,128},{112,144}... | collective-permute-start | bytes 786440 | tf_op jit(solution)/shard_map/gather_second/ppermute | solution.py:298
  37.3 0.0 collective-permute-done.3
  37.4 0.1 collective-permute-start.7
  37.5 0.2 collective-permute-start.5
  37.7 0.0 all-to-all-done
  37.7 0.0 copy-start.4
  37.7 0.0 copy-start.5
  37.7 0.0 copy-start.6
  37.8 0.7 broadcast_in_dim.41
  38.5 9.9 %all-to-all-start.1 = ((f32[16,16,256]{2,1,0:T(8,128)}), f32[16,16,256]{2,1,0:T(8,128)S(1)}, u32[]{:S(2)}, u32[]{:S(2)}) async-start(f32[16,16,256]{2,1,0:T(8,128)} %broadcast_in_dim.41), calls=%async_computation.1 | async-start | bytes 524288 | tf_op jit(solution)/shard_map/normal/all_to_all | solution.py:346
  48.3 0.0 collective-permute-done.4
  48.4 1.0 constant_dynamic-update-slice_fusion.7
  49.3 0.0 collective-permute-done.5
  49.3 1.0 constant_dynamic-update-slice_fusion.6
  50.3 0.0 collective-permute-done.6
  50.4 0.2 collective-permute-start.8
  50.6 0.1 copy.12
  50.7 0.1 sub.36
  50.8 7.2 %all-to-all-done.1 = f32[16,16,256]{2,1,0:T(8,128)S(1)} async-done(((f32[16,16,256]{2,1,0:T(8,128)}), f32[16,16,256]{2,1,0:T(8,128)S(1)}, u32[]{:S(2)}, u32[]{:S(2)}) %all-to-all-start.1) | async-done | bytes 262176 | tf_op jit(solution)/shard_map/normal/all_to_all | solution.py:346
  58.0 0.8 broadcast_in_dim.42
  58.8 7.0 %all-to-all-start.2 = ((f32[16,24,256]{2,1,0:T(8,128)}), f32[16,24,256]{2,1,0:T(8,128)S(1)}, u32[]{:S(2)}, u32[]{:S(2)}) async-start(f32[16,24,256]{2,1,0:T(8,128)} %broadcast_in_dim.42), calls=%async_computation.2 | async-start | bytes 786432 | tf_op jit(solution)/shard_map/normal/all_to_all | solution.py:351
  65.9 0.6 pad_add_fusion.table_ref
  66.5 0.0 collective-permute-done.8
  66.5 0.0 collective-permute-done.7
  66.5 15.2 %contract.1 = f32[64,32,256]{2,1,0:T(8,128)} custom-call(s32[4,48]{1,0:T(4,128)} %pad_add_fusion.table_ref, s32[1]{0:T(128)} %copy.19.count_ref, f32[48,32,1024]{2,1,0:T(8,128)} %tile_hbm.1, f32[16,32,256]{2,1,0:T(8,128)} %bitcast.53, f32[40,32,256]{2,1,0:T(8,128)} %bitcast.54, f32[24,32,256]{2,1,0:T(8,128)} %bitcast.55, f32[40,32,256]{2,1,0:T(8,128)} %bitcast.13.rest_2_, ...), custom_call_target="tpu_custom_call" | custom-call | flops 2415919104 | bytes 10000000 | tf_op jit(solution)/shard_map/contract/contract/pallas_call | solution.py:122
  81.7 0.0 all-to-all-done.2
  81.7 7.0 %all-to-all-start.3 = ((f32[16,128,256]{2,1,0:T(8,128)}), f32[16,128,256]{2,1,0:T(8,128)S(1)}, u32[]{:S(2)}, u32[]{:S(2)}) async-start(f32[16,128,256]{2,1,0:T(8,128)} %bitcast.52), calls=%async_computation.3 | async-start | bytes 4194304 | tf_op jit(solution)/shard_map/exchange/all_to_all | solution.py:369
  88.7 0.1 convert_reduce_fusion
  88.8 0.1 convert_element_type.46.target_ref
  88.9 16.0 %invert.1.inverse_ref = f32[256,256]{1,0:T(8,128)S(1)} custom-call(f32[256,256]{1,0:T(8,128)S(1)} %bitcast.51), custom_call_target="tpu_custom_call" | custom-call | flops 201326592 | bytes 524288 | tf_op jit(solution)/shard_map/inverse/invert/pallas_call | solution.py:257
  104.9 14.4 %all-to-all-done.3 = f32[16,128,256]{2,1,0:T(8,128)S(1)} async-done(((f32[16,128,256]{2,1,0:T(8,128)}), f32[16,128,256]{2,1,0:T(8,128)S(1)}, u32[]{:S(2)}, u32[]{:S(2)}) %all-to-all-start.3) | async-done | bytes 2097184 | tf_op jit(solution)/shard_map/exchange/all_to_all | solution.py:369
  119.4 2.5 %combine.1 = f32[512,256]{1,0:T(8,128)} custom-call(s32[64]{0:T(128)S(1)} %convert_element_type.46.target_ref, f32[64,32,256]{2,1,0:T(8,128)S(1)} %bitcast.50, f32[256,256]{1,0:T(8,128)S(1)} %invert.1.inverse_ref), custom_call_target="tpu_custom_call" | custom-call | tf_op jit(solution)/shard_map/combine/combine/pallas_call | solution.py:168
  (30 shorter events, 0.3 us)
Async XLA Ops:
  0.0 2.3 %copy-start = (f32[256,256]{1,0:T(8,128)S(1)}, f32[256,256]{1,0:T(8,128)}, u32[]{:S(2)}) copy-start(f32[256,256]{1,0:T(8,128)} %param.18) | copy-start | bytes 786436
  2.3 17.5 %copy-start.3 = (s32[48,1]{0,1:T(1,128)S(1)}, s32[48,1]{0,1:T(1,128)}, u32[]{:S(2)}) copy-start(s32[48,1]{0,1:T(1,128)} %param.13) | copy-start | bytes 580
  2.3 17.6 %copy-start.7 = (s32[48]{0:T(128)S(1)}, s32[48]{0:T(128)}, u32[]{:S(2)}) copy-start(s32[48]{0:T(128)} %param.14) | copy-start | bytes 580
  3.7 46.6 %collective-permute-start.6 = (f32[256,256]{1,0:T(8,128)S(1)}, f32[256,256]{1,0:T(8,128)S(1)}, u32[]{:S(2)}, u32[]{:S(2)}) collective-permute-start(f32[256,256]{1,0:T(8,128)S(1)} %copy-done), channel_id=1, source_target_pairs={{0,128},{16,144},{32,160},{48,176},{64,192},{80,208},{96,224},{112... | collective-permute-start | bytes 786440 | tf_op jit(solution)/shard_map/gather_second/ppermute | solution.py:298
  10.0 19.1 %collective-permute-start.1 = (f32[256,256]{1,0:T(8,128)S(1)}, f32[256,256]{1,0:T(8,128)S(1)}, u32[]{:S(2)}, u32[]{:S(2)}) collective-permute-start(f32[256,256]{1,0:T(8,128)S(1)} %copy-done), channel_id=1, source_target_pairs={{0,224},{16,240},{32,0},{48,16},{64,32},{80,48},{96,64},{112,80},{... | collective-permute-start | bytes 786440 | tf_op jit(solution)/shard_map/gather_second/ppermute | solution.py:298
  11.0 16.6 %collective-permute-start = (f32[256,256]{1,0:T(8,128)S(1)}, f32[256,256]{1,0:T(8,128)S(1)}, u32[]{:S(2)}, u32[]{:S(2)}) collective-permute-start(f32[256,256]{1,0:T(8,128)S(1)} %copy-done), channel_id=1, source_target_pairs={{0,32},{16,48},{32,64},{48,80},{64,96},{80,112},{96,128},{112,144}... | collective-permute-start | bytes 786440 | tf_op jit(solution)/shard_map/gather_second/ppermute | solution.py:298
  12.0 25.6 %all-to-all-start = ((f32[16,32,256]{2,1,0:T(8,128)}), f32[16,32,256]{2,1,0:T(8,128)S(1)}, u32[]{:S(2)}, u32[]{:S(2)}) async-start(f32[16,32,256]{2,1,0:T(8,128)} %pad_maximum_fusion), calls=%async_computation | async-start | bytes 1048576 | tf_op jit(solution)/shard_map/normal/all_to_all | solution.py:291
  27.6 7.2 %collective-permute-start.2 = (f32[256,256]{1,0:T(8,128)S(1)}, f32[256,256]{1,0:T(8,128)S(1)}, u32[]{:S(2)}, u32[]{:S(2)}) collective-permute-start(f32[256,256]{1,0:T(8,128)S(1)} %collective-permute-done), channel_id=1, source_target_pairs={{0,32},{16,48},{32,64},{48,80},{64,96},{80,112},{96,128},{112,144}... | collective-permute-start | bytes 786440 | tf_op jit(solution)/shard_map/gather_second/ppermute | solution.py:298
  29.1 8.2 %collective-permute-start.3 = (f32[256,256]{1,0:T(8,128)S(1)}, f32[256,256]{1,0:T(8,128)S(1)}, u32[]{:S(2)}, u32[]{:S(2)}) collective-permute-start(f32[256,256]{1,0:T(8,128)S(1)} %collective-permute-done.1), channel_id=1, source_target_pairs={{0,224},{16,240},{32,0},{48,16},{64,32},{80,48},{96,64},{112,80},{... | collective-permute-start | bytes 786440 | tf_op jit(solution)/shard_map/gather_second/ppermute | solution.py:298
  34.8 13.5 %collective-permute-start.4 = (f32[256,256]{1,0:T(8,128)S(1)}, f32[256,256]{1,0:T(8,128)}, u32[]{:S(2)}, u32[]{:S(2)}) collective-permute-start(f32[256,256]{1,0:T(8,128)S(1)} %collective-permute-done.2), channel_id=1, source_target_pairs={{0,32},{16,48},{32,64},{48,80},{64,96},{80,112},{96,128},{112,144}... | collective-permute-start | bytes 786440 | tf_op jit(solution)/shard_map/gather_second/ppermute | solution.py:298
  37.3 13.0 %copy-start.1 = (f32[1280,256]{1,0:T(8,128)}, f32[1280,256]{1,0:T(8,128)S(1)}, u32[]{:S(2)}) copy-start(f32[1280,256]{1,0:T(8,128)S(1)} %constant_dynamic-update-slice_fusion) | copy-start | bytes 3932164
  37.4 29.1 %collective-permute-start.7 = (f32[1280,256]{1,0:T(8,128)S(1)}, f32[1280,256]{1,0:T(8,128)}, u32[]{:S(2)}, u32[]{:S(2)}) collective-permute-start(f32[1280,256]{1,0:T(8,128)S(1)} %constant_dynamic-update-slice_fusion), channel_id=1, source_target_pairs={{0,16},{16,0},{32,48},{48,32},{64,80},{80,64},{96,112},{112,96},{1... | collective-permute-start | bytes 3932168 | tf_op jit(solution)/shard_map/gather_second/ppermute | solution.py:309
  37.5 11.9 %collective-permute-start.5 = (f32[256,256]{1,0:T(8,128)S(1)}, f32[256,256]{1,0:T(8,128)}, u32[]{:S(2)}, u32[]{:S(2)}) collective-permute-start(f32[256,256]{1,0:T(8,128)S(1)} %collective-permute-done.3), channel_id=1, source_target_pairs={{0,224},{16,240},{32,0},{48,16},{64,32},{80,48},{96,64},{112,80},{... | collective-permute-start | bytes 786440 | tf_op jit(solution)/shard_map/gather_second/ppermute | solution.py:298
  37.7 12.9 %copy-start.4 = (s32[48,1]{0,1:T(1,128)S(1)}, s32[48,1]{0,1:T(1,128)}, u32[]{:S(2)}) copy-start(s32[48,1]{0,1:T(1,128)} %param.15) | copy-start | bytes 580
  37.7 12.9 %copy-start.5 = (s32[48]{0:T(128)S(1)}, s32[48]{0:T(128)}, u32[]{:S(2)}) copy-start(s32[48]{0:T(128)} %param.17) | copy-start | bytes 580
  37.7 12.9 %copy-start.6 = (s32[48]{0:T(128)S(1)}, s32[48]{0:T(128)}, u32[]{:S(2)}) copy-start(s32[48]{0:T(128)} %param.16) | copy-start | bytes 580
  38.5 19.5 %all-to-all-start.1 = ((f32[16,16,256]{2,1,0:T(8,128)}), f32[16,16,256]{2,1,0:T(8,128)S(1)}, u32[]{:S(2)}, u32[]{:S(2)}) async-start(f32[16,16,256]{2,1,0:T(8,128)} %broadcast_in_dim.41), calls=%async_computation.1 | async-start | bytes 524288 | tf_op jit(solution)/shard_map/normal/all_to_all | solution.py:346
  50.4 16.1 %copy-start.2 = (f32[768,256]{1,0:T(8,128)}, f32[768,256]{1,0:T(8,128)S(1)}, u32[]{:S(2)}) copy-start(f32[768,256]{1,0:T(8,128)S(1)} %constant_dynamic-update-slice_fusion.5) | copy-start | bytes 2359300
  50.4 16.1 %collective-permute-start.8 = (f32[768,256]{1,0:T(8,128)S(1)}, f32[768,256]{1,0:T(8,128)}, u32[]{:S(2)}, u32[]{:S(2)}) collective-permute-start(f32[768,256]{1,0:T(8,128)S(1)} %constant_dynamic-update-slice_fusion.5), channel_id=1, source_target_pairs={{0,16},{16,0},{32,48},{48,32},{64,80},{80,64},{96,112},{112,96},{1... | collective-permute-start | bytes 2359304 | tf_op jit(solution)/shard_map/gather_second/ppermute | solution.py:310
  58.8 22.8 %all-to-all-start.2 = ((f32[16,24,256]{2,1,0:T(8,128)}), f32[16,24,256]{2,1,0:T(8,128)S(1)}, u32[]{:S(2)}, u32[]{:S(2)}) async-start(f32[16,24,256]{2,1,0:T(8,128)} %broadcast_in_dim.42), calls=%async_computation.2 | async-start | bytes 786432 | tf_op jit(solution)/shard_map/normal/all_to_all | solution.py:351
  81.7 37.7 %all-to-all-start.3 = ((f32[16,128,256]{2,1,0:T(8,128)}), f32[16,128,256]{2,1,0:T(8,128)S(1)}, u32[]{:S(2)}, u32[]{:S(2)}) async-start(f32[16,128,256]{2,1,0:T(8,128)} %bitcast.52), calls=%async_computation.3 | async-start | bytes 4194304 | tf_op jit(solution)/shard_map/exchange/all_to_all | solution.py:369

commit v8 on v5

--- a/solution.py
+++ b/solution.py
@@ -227,9 +227,12 @@
         groups = out
     return groups
 
-def invert_kernel(block, normal_ref, out_ref, work_ref):
-    n = normal_ref.shape[0]
-    normal = normal_ref[...]
+def invert_kernel(block, order_ref, strips_ref, out_ref, work_ref):
+    n = out_ref.shape[0]
+    strip = n // strips_ref.shape[0]
+    for at in range(strips_ref.shape[0]):
+        work_ref[at * strip : (at + 1) * strip, :] = strips_ref[order_ref[at], 0:strip, :]
+    normal = work_ref[...]
     on_diagonal = lax.broadcasted_iota(jnp.int32, (n, n), 0) == lax.broadcasted_iota(jnp.int32, (n, n), 1)
     diagonal = jnp.where(on_diagonal, normal, 0.0)
     scale_row = lax.rsqrt(jnp.sum(diagonal, axis=0, keepdims=True))
@@ -251,18 +254,19 @@
         work_ref[first:last, :] = rows
     out_ref[...] = work_ref[...] * scale_col * scale_row
 
-def invert(normal, block=64):
-    n = normal.shape[0]
+def invert(order, strips, block=64):
+    n = strips.shape[2]
     vmem = pl.BlockSpec(memory_space=pltpu.VMEM)
     return pl.pallas_call(
         functools.partial(invert_kernel, block),
         out_shape=jax.ShapeDtypeStruct((n, n), jnp.float32),
-        in_specs=[vmem], out_specs=vmem,
+        in_specs=[pl.BlockSpec(memory_space=pltpu.SMEM), vmem],
+        out_specs=vmem,
         scratch_shapes=[pltpu.VMEM((n, n), jnp.float32)],
         compiler_params=pltpu.CompilerParams(vmem_limit_bytes=16 * 1024 * 1024),
         cost_estimate=pl.CostEstimate(flops=12 * n * n * n, bytes_accessed=8 * n * n, transcendentals=0),
         name="invert",
-    )(normal)
+    )(order, strips)
 
 
 def local(
@@ -345,9 +349,26 @@
         )
         normal_part = jnp.sum(second_strips, axis=0) * strips[part:]
         sent = jnp.concatenate([normal_part, target_rows], axis=0)
-        spread = lax.all_to_all(jnp.broadcast_to(sent[None], (n_col,) + sent.shape), "col", 0, 0)
-        normal_matrix = spread[:, :part].reshape(rank_width, rank_width)
+        side = 4
+
+        def turned(array, along_x, along_y):
+            pairs = [
+                (i, (i // side + along_x) % side * side + (i % side + along_y) % side) for i in range(n_col)
+            ]
+            return lax.ppermute(array, "col", pairs)
+
+        line = jnp.stack([sent] + [turned(sent, 0, shift) for shift in range(1, side)])
+        spread = jnp.stack([line] + [turned(line, shift, 0) for shift in range(1, side)])
+        spread = spread.reshape((n_col,) + sent.shape)
+        each_col = jnp.arange(n_col, dtype=jnp.int32)
+        order = (col_index // side - each_col // side + side) % side * side + (
+            col_index % side - each_col % side + side
+        ) % side
+        order = order.astype(jnp.int32)
         received_targets = lax.dynamic_slice_in_dim(spread[:, part], col_index * SLOTS, SLOTS, 1)
+        received_targets = jnp.sum(
+            jnp.where(order[:, None, None] == each_col[None, :, None], received_targets[None, :, :], 0.0), axis=1
+        )
         received_targets = received_targets.astype(jnp.int32).reshape(-1)
 
     with jax.named_scope("contract"):
@@ -368,7 +389,7 @@
         ).reshape(n_col * SLOTS, tile_edge, rank_width)
 
     with jax.named_scope("inverse"):
-        inverse = invert(normal_matrix)
+        inverse = invert(order, spread)
 
     with jax.named_scope("combine"):
         return combine(received_targets, received, inverse)

time: 114 us -> 128 us (1.12)
  starting transfers between devices: 41.1 us -> 51.7 us
  waiting for transfers between devices: 23.7 us -> 33.8 us
  local copies, waits for them, and re-layouts: 8.46 us -> 1.49 us
    ppermute x0 -> x6, waiting for transfers between devices: none -> 20.3 us  [turned(): return lax.ppermute(array, 'col', pairs)]
    ppermute x0 -> x6, starting transfers between devices: none -> 16.2 us  [turned(): return lax.ppermute(array, 'col', pairs)]
    all_to_all x1, waiting for transfers between devices: 12.5 us -> 0.01 us  [local(): lax.all_to_all(partials.reshape(n_col, SLOTS * tile_edge, rank_width), 'c...]
    all_to_all x1 -> x0, starting transfers between devices: 6.99 us -> none  [local(): lax.all_to_all(jnp.broadcast_to(sent[None], (n_col,) + sent.shape), 'col'...]
    unnamed x31 -> x23, local copies, waits for them, and re-layouts: 4.76 us -> 0.17 us
    ppermute x8, waiting for transfers between devices: 11.2 us -> 13.5 us  [moved(): return lax.ppermute(array, 'row', pairs)]
  transfers between devices with their start and end apart: 14 -> 19, of which waited for: 5 -> 11; matrix products, arithmetic and copies ran while one was open for 11% -> 5% of each run, Pallas kernels for 27% -> 24%
where the time goes in v8:
time: 128 us; the launch traced here: 126 us
  starting transfers between devices  51.7 us (40%)
  waiting for transfers between devices  33.8 us (26%)
  Pallas kernels  33.3 us (26%)
  matrix products  2.97 us (2%)
  other arithmetic  1.89 us (1%)
  local copies, waits for them, and re-layouts  1.49 us (1%)
    ppermute x6, waiting for transfers between devices, turned(): return lax.ppermute(array, 'col', pairs)  20.3 us
    pallas_call x1, Pallas kernels, invert(): pl.pallas_call(functools.partial(invert_kernel, block), out_shape=jax.Sha...  16.6 us
    ppermute x6, starting transfers between devices, turned(): return lax.ppermute(array, 'col', pairs)  16.2 us
    pallas_call x1, Pallas kernels, contract_tiles(): pl.pallas_call(contract_kernel, out_shape=jax.ShapeDtypeStruct((out_slots...  14.2 us
    ppermute x8, waiting for transfers between devices, moved(): return lax.ppermute(array, 'row', pairs)  13.5 us
    ppermute x8, starting transfers between devices, moved(): return lax.ppermute(array, 'row', pairs)  11.6 us
    all_to_all x1, starting transfers between devices, local(): lax.all_to_all(jnp.broadcast_to(strips[None, :part], (n_row, part, rank_w...  8.81 us
    all_to_all x1, starting transfers between devices, local(): lax.all_to_all(partials.reshape(n_col, SLOTS * tile_edge, rank_width), 'c...  7.88 us
  transfers between devices with their start and end apart: 19, of which 11 were waited for; matrix products, arithmetic and copies ran while one was open for 5% of the time, Pallas kernels for 24%

profile of v8, /device:TPU:32, one launch (start us, length us, event | category | flops | bytes accessed | tf_op | source)
XLA Modules:
  0.0 126.3 jit_solution(10392299063386581206)
XLA Ops:
  0.0 1.9 %collective-permute-start.6 = (f32[256,256]{1,0:T(8,128)}, f32[256,256]{1,0:T(8,128)S(1)}, u32[]{:S(2)}, u32[]{:S(2)}) collective-permute-start(f32[256,256]{1,0:T(8,128)} %param.18), channel_id=1, source_target_pairs={{0,32},{16,48},{32,64},{48,80},{64,96},{80,112},{96,128},{112,144}... | collective-permute-start | bytes 786440 | tf_op jit(solution)/shard_map/gather_second/ppermute | solution.py:296
  1.9 0.1 collective-permute-start.7
  2.0 2.2 %fusion.28 = f32[256,256]{1,0:T(8,128)S(1)} fusion(f32[512,256]{1,0:T(8,128)} %param.19), kind=kOutput, calls=%fused_computation.92 | convolution fusion | flops 402653184 | bytes 786432 | tf_op jit(solution)/shard_map/normal/dot_general | solution.py:20
  4.3 0.6 fusion.27
  4.9 0.8 pad_maximum_fusion
  5.7 7.0 %all-to-all-start = ((f32[16,32,256]{2,1,0:T(8,128)}), f32[16,32,256]{2,1,0:T(8,128)S(1)}, u32[]{:S(2)}, u32[]{:S(2)}) async-start(f32[16,32,256]{2,1,0:T(8,128)} %pad_maximum_fusion), calls=%async_computation | async-start | bytes 1048576 | tf_op jit(solution)/shard_map/normal/all_to_all | solution.py:345
  12.8 2.0 %collective-permute-start.8 = (f32[256,256]{1,0:T(8,128)S(1)}, f32[256,256]{1,0:T(8,128)S(1)}, u32[]{:S(2)}, u32[]{:S(2)}) collective-permute-start(f32[256,256]{1,0:T(8,128)S(1)} %collective-permute-done.6), channel_id=1, source_target_pairs={{0,32},{16,48},{32,64},{48,80},{64,96},{80,112},{96,128},{112,144}... | collective-permute-start | bytes 786440 | tf_op jit(solution)/shard_map/gather_second/ppermute | solution.py:296
  14.8 2.2 %collective-permute-start.9 = (f32[256,256]{1,0:T(8,128)S(1)}, f32[256,256]{1,0:T(8,128)S(1)}, u32[]{:S(2)}, u32[]{:S(2)}) collective-permute-start(f32[256,256]{1,0:T(8,128)S(1)} %collective-permute-done.7), channel_id=1, source_target_pairs={{0,224},{16,240},{32,0},{48,16},{64,32},{80,48},{96,64},{112,80},{... | collective-permute-start | bytes 786440 | tf_op jit(solution)/shard_map/gather_second/ppermute | solution.py:296
  17.7 4.9 %collective-permute-done.8 = f32[256,256]{1,0:T(8,128)S(1)} collective-permute-done((f32[256,256]{1,0:T(8,128)S(1)}, f32[256,256]{1,0:T(8,128)S(1)}, u32[]{:S(2)}, u32[]{:S(2)}) %collective-permute-start.8) | collective-permute-done | bytes 262176 | tf_op jit(solution)/shard_map/gather_second/ppermute | solution.py:296
  22.6 0.2 collective-permute-start.10
  22.8 0.5 collective-permute-done.9
  23.3 2.3 %collective-permute-start.11 = (f32[256,256]{1,0:T(8,128)S(1)}, f32[256,256]{1,0:T(8,128)S(1)}, u32[]{:S(2)}, u32[]{:S(2)}) collective-permute-start(f32[256,256]{1,0:T(8,128)S(1)} %collective-permute-done.9), channel_id=1, source_target_pairs={{0,224},{16,240},{32,0},{48,16},{64,32},{80,48},{96,64},{112,80},{... | collective-permute-start | bytes 786440 | tf_op jit(solution)/shard_map/gather_second/ppermute | solution.py:296
  25.6 0.1 collective-permute-start.14
  25.8 4.6 %collective-permute-done.10 = f32[256,256]{1,0:T(8,128)S(1)} collective-permute-done((f32[256,256]{1,0:T(8,128)S(1)}, f32[256,256]{1,0:T(8,128)S(1)}, u32[]{:S(2)}, u32[]{:S(2)}) %collective-permute-start.10) | collective-permute-done | bytes 262176 | tf_op jit(solution)/shard_map/gather_second/ppermute | solution.py:296
  30.4 0.1 collective-permute-start.12
  30.5 0.3 collective-permute-done.11
  30.8 2.8 %collective-permute-start.13 = (f32[128,256]{1,0:T(8,128)S(1)}, f32[128,256]{1,0:T(8,128)S(1)}, u32[]{:S(2)}, u32[]{:S(2)}) collective-permute-start(f32[128,256]{1,0:T(8,128)S(1)} %slice.40), channel_id=1, source_target_pairs={{0,224},{16,240},{32,0},{48,16},{64,32},{80,48},{96,64},{112,80},{... | collective-permute-start | bytes 393224 | tf_op jit(solution)/shard_map/gather_second/ppermute | solution.py:296
  33.6 2.8 %collective-permute-done.12 = f32[128,256]{1,0:T(8,128)S(1)} collective-permute-done((f32[128,256]{1,0:T(8,128)S(1)}, f32[128,256]{1,0:T(8,128)S(1)}, u32[]{:S(2)}, u32[]{:S(2)}) %collective-permute-start.12) | collective-permute-done | bytes 131104 | tf_op jit(solution)/shard_map/gather_second/ppermute | solution.py:296
  36.4 0.4 collective-permute-done.13
  36.9 0.1 collective-permute-start.15
  37.0 0.1 select_reduce_fusion.1
  37.2 0.7 broadcast_in_dim.61
  38.0 8.8 %all-to-all-start.1 = ((f32[16,16,256]{2,1,0:T(8,128)}), f32[16,16,256]{2,1,0:T(8,128)S(1)}, u32[]{:S(2)}, u32[]{:S(2)}) async-start(f32[16,16,256]{2,1,0:T(8,128)} %broadcast_in_dim.61), calls=%async_computation.1 | async-start | bytes 524288 | tf_op jit(solution)/shard_map/normal/all_to_all | solution.py:347
  46.8 0.6 pad_add_fusion.table_ref
  47.4 14.2 %contract.1 = f32[64,32,256]{2,1,0:T(8,128)} custom-call(s32[4,48]{1,0:T(4,128)} %pad_add_fusion.table_ref, s32[1]{0:T(128)} %copy.24.count_ref, f32[48,32,1024]{2,1,0:T(8,128)} %tile_hbm.1, f32[16,32,256]{2,1,0:T(8,128)} %bitcast.65, f32[40,32,256]{2,1,0:T(8,128)} %bitcast.66, f32[24,32,256]{2,1,0:T(8,128)} %bitcast.67, f32[40,32,256]{2,1,0:T(8,128)} %bitcast.23.rest_2_, ...), custom_call_target="tpu_custom_call" | custom-call | flops 2415919104 | bytes 10000000 | tf_op jit(solution)/shard_map/contract/contract/pallas_call | solution.py:122
  61.6 7.9 %all-to-all-start.2 = ((f32[16,128,256]{2,1,0:T(8,128)}), f32[16,128,256]{2,1,0:T(8,128)S(1)}, u32[]{:S(2)}, u32[]{:S(2)}) async-start(f32[16,128,256]{2,1,0:T(8,128)} %bitcast.64), calls=%async_computation.2 | async-start | bytes 4194304 | tf_op jit(solution)/shard_map/exchange/all_to_all | solution.py:387
  69.6 0.1 multiply_reduce_fusion
  69.7 0.1 copy.14
  69.8 0.1 sub.69
  70.0 2.2 %collective-permute-start = (f32[24,256]{1,0:T(8,128)S(1)}, f32[24,256]{1,0:T(8,128)S(1)}, u32[]{:S(2)}, u32[]{:S(2)}) collective-permute-start(f32[24,256]{1,0:T(8,128)S(1)} %get-tuple-element.20), channel_id=1, source_target_pairs={{0,1},{1,2},{2,3},{3,0},{4,5},{5,6},{6,7},{7,4},{8,9},{9,10},{10,1... | collective-permute-start | bytes 73736 | tf_op jit(solution)/shard_map/normal/ppermute | solution.py:358
  72.1 2.7 %collective-permute-start.1 = (f32[24,256]{1,0:T(8,128)S(1)}, f32[24,256]{1,0:T(8,128)S(1)}, u32[]{:S(2)}, u32[]{:S(2)}) collective-permute-start(f32[24,256]{1,0:T(8,128)S(1)} %get-tuple-element.20), channel_id=1, source_target_pairs={{0,2},{1,3},{2,0},{3,1},{4,6},{5,7},{6,4},{7,5},{8,10},{9,11},{10,... | collective-permute-start | bytes 73736 | tf_op jit(solution)/shard_map/normal/ppermute | solution.py:358
  74.8 1.5 %collective-permute-start.2 = (f32[24,256]{1,0:T(8,128)S(1)}, f32[24,256]{1,0:T(8,128)S(1)}, u32[]{:S(2)}, u32[]{:S(2)}) collective-permute-start(f32[24,256]{1,0:T(8,128)S(1)} %get-tuple-element.20), channel_id=1, source_target_pairs={{0,3},{1,0},{2,1},{3,2},{4,7},{5,4},{6,5},{7,6},{8,11},{9,8},{10,9... | collective-permute-start | bytes 73736 | tf_op jit(solution)/shard_map/normal/ppermute | solution.py:358
  76.3 12.2 %collective-permute-done = f32[24,256]{1,0:T(8,128)S(1)} collective-permute-done((f32[24,256]{1,0:T(8,128)S(1)}, f32[24,256]{1,0:T(8,128)S(1)}, u32[]{:S(2)}, u32[]{:S(2)}) %collective-permute-start) | collective-permute-done | bytes 24608 | tf_op jit(solution)/shard_map/normal/ppermute | solution.py:358
  88.5 2.4 %collective-permute-done.2 = f32[24,256]{1,0:T(8,128)S(1)} collective-permute-done((f32[24,256]{1,0:T(8,128)S(1)}, f32[24,256]{1,0:T(8,128)S(1)}, u32[]{:S(2)}, u32[]{:S(2)}) %collective-permute-start.2) | collective-permute-done | bytes 24608 | tf_op jit(solution)/shard_map/normal/ppermute | solution.py:358
  90.9 7.8 %collective-permute-start.4 = (f32[4,24,256]{2,1,0:T(8,128)S(1)}, f32[4,24,256]{2,1,0:T(8,128)S(1)}, u32[]{:S(2)}, u32[]{:S(2)}) collective-permute-start(f32[4,24,256]{2,1,0:T(8,128)S(1)} %get-tuple-element.18), channel_id=1, source_target_pairs={{0,8},{1,9},{2,10},{3,11},{4,12},{5,13},{6,14},{7,15},{8,0},{9,1},... | collective-permute-start | bytes 294920 | tf_op jit(solution)/shard_map/normal/ppermute | solution.py:358
  98.8 2.0 %collective-permute-start.5 = (f32[4,24,256]{2,1,0:T(8,128)S(1)}, f32[4,24,256]{2,1,0:T(8,128)S(1)}, u32[]{:S(2)}, u32[]{:S(2)}) collective-permute-start(f32[4,24,256]{2,1,0:T(8,128)S(1)} %get-tuple-element.18), channel_id=1, source_target_pairs={{0,12},{1,13},{2,14},{3,15},{4,0},{5,1},{6,2},{7,3},{8,4},{9,5},{1... | collective-permute-start | bytes 294920 | tf_op jit(solution)/shard_map/normal/ppermute | solution.py:358
  100.8 0.0 collective-permute-start.3
  100.8 0.1 iota_compare_fusion.5
  100.9 1.0 collective-permute-done.4
  101.8 2.6 %collective-permute-done.5 = f32[4,24,256]{2,1,0:T(8,128)S(1)} collective-permute-done((f32[4,24,256]{2,1,0:T(8,128)S(1)}, f32[4,24,256]{2,1,0:T(8,128)S(1)}, u32[]{:S(2)}, u32[]{:S(2)}) %collective-permute-start.5) | collective-permute-done | bytes 98336 | tf_op jit(solution)/shard_map/normal/ppermute | solution.py:358
  104.4 2.2 %collective-permute-done.3 = f32[4,24,256]{2,1,0:T(8,128)S(1)} collective-permute-done((f32[4,24,256]{2,1,0:T(8,128)S(1)}, f32[4,24,256]{2,1,0:T(8,128)S(1)}, u32[]{:S(2)}, u32[]{:S(2)}) %collective-permute-start.3) | collective-permute-done | bytes 98336 | tf_op jit(solution)/shard_map/normal/ppermute | solution.py:358
  106.6 0.1 constant_dynamic-slice_fusion
  106.7 0.1 copy.15
  106.8 0.1 select_reduce_fusion
  106.9 0.1 copy.16
  107.0 0.1 convert_element_type.46.target_ref
  107.1 16.6 %invert.1.inverse_ref = f32[256,256]{1,0:T(8,128)S(1)} custom-call(s32[16]{0:T(128)S(1)} %fusion.8.order_ref, f32[16,24,256]{2,1,0:T(8,128)S(1)} %bitcast.63), custom_call_target="tpu_custom_call" | custom-call | flops 201326592 | bytes 524288 | tf_op jit(solution)/shard_map/inverse/invert/pallas_call | solution.py:260
  123.7 2.6 %combine.1 = f32[512,256]{1,0:T(8,128)} custom-call(s32[64]{0:T(128)S(1)} %convert_element_type.46.target_ref, f32[64,32,256]{2,1,0:T(8,128)S(1)} %bitcast.61, f32[256,256]{1,0:T(8,128)S(1)} %invert.1.inverse_ref), custom_call_target="tpu_custom_call" | custom-call | tf_op jit(solution)/shard_map/combine/combine/pallas_call | solution.py:168
  (51 shorter events, 0.5 us)
Async XLA Ops:
  0.0 4.3 %copy-start = (f32[256,256]{1,0:T(8,128)S(1)}, f32[256,256]{1,0:T(8,128)}, u32[]{:S(2)}) copy-start(f32[256,256]{1,0:T(8,128)} %param.18) | copy-start | bytes 786436
  0.0 12.8 %collective-permute-start.6 = (f32[256,256]{1,0:T(8,128)}, f32[256,256]{1,0:T(8,128)S(1)}, u32[]{:S(2)}, u32[]{:S(2)}) collective-permute-start(f32[256,256]{1,0:T(8,128)} %param.18), channel_id=1, source_target_pairs={{0,32},{16,48},{32,64},{48,80},{64,96},{80,112},{96,128},{112,144}... | collective-permute-start | bytes 786440 | tf_op jit(solution)/shard_map/gather_second/ppermute | solution.py:296
  1.9 12.8 %collective-permute-start.7 = (f32[256,256]{1,0:T(8,128)}, f32[256,256]{1,0:T(8,128)S(1)}, u32[]{:S(2)}, u32[]{:S(2)}) collective-permute-start(f32[256,256]{1,0:T(8,128)} %param.18), channel_id=1, source_target_pairs={{0,224},{16,240},{32,0},{48,16},{64,32},{80,48},{96,64},{112,80},{... | collective-permute-start | bytes 786440 | tf_op jit(solution)/shard_map/gather_second/ppermute | solution.py:296
  5.7 31.4 %all-to-all-start = ((f32[16,32,256]{2,1,0:T(8,128)}), f32[16,32,256]{2,1,0:T(8,128)S(1)}, u32[]{:S(2)}, u32[]{:S(2)}) async-start(f32[16,32,256]{2,1,0:T(8,128)} %pad_maximum_fusion), calls=%async_computation | async-start | bytes 1048576 | tf_op jit(solution)/shard_map/normal/all_to_all | solution.py:345
  12.8 9.8 %collective-permute-start.8 = (f32[256,256]{1,0:T(8,128)S(1)}, f32[256,256]{1,0:T(8,128)S(1)}, u32[]{:S(2)}, u32[]{:S(2)}) collective-permute-start(f32[256,256]{1,0:T(8,128)S(1)} %collective-permute-done.6), channel_id=1, source_target_pairs={{0,32},{16,48},{32,64},{48,80},{64,96},{80,112},{96,128},{112,144}... | collective-permute-start | bytes 786440 | tf_op jit(solution)/shard_map/gather_second/ppermute | solution.py:296
  14.8 8.5 %collective-permute-start.9 = (f32[256,256]{1,0:T(8,128)S(1)}, f32[256,256]{1,0:T(8,128)S(1)}, u32[]{:S(2)}, u32[]{:S(2)}) collective-permute-start(f32[256,256]{1,0:T(8,128)S(1)} %collective-permute-done.7), channel_id=1, source_target_pairs={{0,224},{16,240},{32,0},{48,16},{64,32},{80,48},{96,64},{112,80},{... | collective-permute-start | bytes 786440 | tf_op jit(solution)/shard_map/gather_second/ppermute | solution.py:296
  22.6 7.8 %collective-permute-start.10 = (f32[256,256]{1,0:T(8,128)S(1)}, f32[256,256]{1,0:T(8,128)S(1)}, u32[]{:S(2)}, u32[]{:S(2)}) collective-permute-start(f32[256,256]{1,0:T(8,128)S(1)} %collective-permute-done.8), channel_id=1, source_target_pairs={{0,32},{16,48},{32,64},{48,80},{64,96},{80,112},{96,128},{112,144}... | collective-permute-start | bytes 786440 | tf_op jit(solution)/shard_map/gather_second/ppermute | solution.py:296
  23.3 7.5 %collective-permute-start.11 = (f32[256,256]{1,0:T(8,128)S(1)}, f32[256,256]{1,0:T(8,128)S(1)}, u32[]{:S(2)}, u32[]{:S(2)}) collective-permute-start(f32[256,256]{1,0:T(8,128)S(1)} %collective-permute-done.9), channel_id=1, source_target_pairs={{0,224},{16,240},{32,0},{48,16},{64,32},{80,48},{96,64},{112,80},{... | collective-permute-start | bytes 786440 | tf_op jit(solution)/shard_map/gather_second/ppermute | solution.py:296
  25.6 11.4 %copy-start.3 = (s32[48,1]{0,1:T(1,128)S(1)}, s32[48,1]{0,1:T(1,128)}, u32[]{:S(2)}) copy-start(s32[48,1]{0,1:T(1,128)} %param.13) | copy-start | bytes 580
  25.6 11.5 %copy-start.4 = (s32[48,1]{0,1:T(1,128)S(1)}, s32[48,1]{0,1:T(1,128)}, u32[]{:S(2)}) copy-start(s32[48,1]{0,1:T(1,128)} %param.15) | copy-start | bytes 580
  25.6 11.6 %copy-start.1 = (f32[1280,256]{1,0:T(8,128)}, f32[1280,256]{1,0:T(8,128)S(1)}, u32[]{:S(2)}) copy-start(f32[1280,256]{1,0:T(8,128)S(1)} %constant_dynamic-update-slice_fusion) | copy-start | bytes 3932164
  25.6 21.8 %collective-permute-start.14 = (f32[1280,256]{1,0:T(8,128)S(1)}, f32[1280,256]{1,0:T(8,128)}, u32[]{:S(2)}, u32[]{:S(2)}) collective-permute-start(f32[1280,256]{1,0:T(8,128)S(1)} %constant_dynamic-update-slice_fusion), channel_id=1, source_target_pairs={{0,16},{16,0},{32,48},{48,32},{64,80},{80,64},{96,112},{112,96},{1... | collective-permute-start | bytes 3932168 | tf_op jit(solution)/shard_map/gather_second/ppermute | solution.py:308
  30.4 6.0 %collective-permute-start.12 = (f32[128,256]{1,0:T(8,128)S(1)}, f32[128,256]{1,0:T(8,128)S(1)}, u32[]{:S(2)}, u32[]{:S(2)}) collective-permute-start(f32[128,256]{1,0:T(8,128)S(1)} %slice.39), channel_id=1, source_target_pairs={{0,32},{16,48},{32,64},{48,80},{64,96},{80,112},{96,128},{112,144}... | collective-permute-start | bytes 393224 | tf_op jit(solution)/shard_map/gather_second/ppermute | solution.py:296
  30.8 6.1 %collective-permute-start.13 = (f32[128,256]{1,0:T(8,128)S(1)}, f32[128,256]{1,0:T(8,128)S(1)}, u32[]{:S(2)}, u32[]{:S(2)}) collective-permute-start(f32[128,256]{1,0:T(8,128)S(1)} %slice.40), channel_id=1, source_target_pairs={{0,224},{16,240},{32,0},{48,16},{64,32},{80,48},{96,64},{112,80},{... | collective-permute-start | bytes 393224 | tf_op jit(solution)/shard_map/gather_second/ppermute | solution.py:296
  33.6 13.2 %copy-start.5 = (s32[48]{0:T(128)S(1)}, s32[48]{0:T(128)}, u32[]{:S(2)}) copy-start(s32[48]{0:T(128)} %param.17) | copy-start | bytes 580
  33.6 13.2 %copy-start.6 = (s32[48]{0:T(128)S(1)}, s32[48]{0:T(128)}, u32[]{:S(2)}) copy-start(s32[48]{0:T(128)} %param.16) | copy-start | bytes 580
  36.8 10.6 %copy-start.2 = (f32[768,256]{1,0:T(8,128)}, f32[768,256]{1,0:T(8,128)S(1)}, u32[]{:S(2)}) copy-start(f32[768,256]{1,0:T(8,128)S(1)} %constant_dynamic-update-slice_fusion.5) | copy-start | bytes 2359300
  36.9 10.6 %collective-permute-start.15 = (f32[768,256]{1,0:T(8,128)S(1)}, f32[768,256]{1,0:T(8,128)}, u32[]{:S(2)}, u32[]{:S(2)}) collective-permute-start(f32[768,256]{1,0:T(8,128)S(1)} %constant_dynamic-update-slice_fusion.5), channel_id=1, source_target_pairs={{0,16},{16,0},{32,48},{48,32},{64,80},{80,64},{96,112},{112,96},{1... | collective-permute-start | bytes 2359304 | tf_op jit(solution)/shard_map/gather_second/ppermute | solution.py:309
  38.0 23.7 %all-to-all-start.1 = ((f32[16,16,256]{2,1,0:T(8,128)}), f32[16,16,256]{2,1,0:T(8,128)S(1)}, u32[]{:S(2)}, u32[]{:S(2)}) async-start(f32[16,16,256]{2,1,0:T(8,128)} %broadcast_in_dim.61), calls=%async_computation.1 | async-start | bytes 524288 | tf_op jit(solution)/shard_map/normal/all_to_all | solution.py:347
  61.6 7.9 %copy-start.7 = (s32[48]{0:T(128)S(1)}, s32[48]{0:T(128)}, u32[]{:S(2)}) copy-start(s32[48]{0:T(128)} %param.14) | copy-start | bytes 580
  61.6 62.0 %all-to-all-start.2 = ((f32[16,128,256]{2,1,0:T(8,128)}), f32[16,128,256]{2,1,0:T(8,128)S(1)}, u32[]{:S(2)}, u32[]{:S(2)}) async-start(f32[16,128,256]{2,1,0:T(8,128)} %bitcast.64), calls=%async_computation.2 | async-start | bytes 4194304 | tf_op jit(solution)/shard_map/exchange/all_to_all | solution.py:387
  70.0 18.5 %collective-permute-start = (f32[24,256]{1,0:T(8,128)S(1)}, f32[24,256]{1,0:T(8,128)S(1)}, u32[]{:S(2)}, u32[]{:S(2)}) collective-permute-start(f32[24,256]{1,0:T(8,128)S(1)} %get-tuple-element.20), channel_id=1, source_target_pairs={{0,1},{1,2},{2,3},{3,0},{4,5},{5,6},{6,7},{7,4},{8,9},{9,10},{10,1... | collective-permute-start | bytes 73736 | tf_op jit(solution)/shard_map/normal/ppermute | solution.py:358
  72.1 16.3 %collective-permute-start.1 = (f32[24,256]{1,0:T(8,128)S(1)}, f32[24,256]{1,0:T(8,128)S(1)}, u32[]{:S(2)}, u32[]{:S(2)}) collective-permute-start(f32[24,256]{1,0:T(8,128)S(1)} %get-tuple-element.20), channel_id=1, source_target_pairs={{0,2},{1,3},{2,0},{3,1},{4,6},{5,7},{6,4},{7,5},{8,10},{9,11},{10,... | collective-permute-start | bytes 73736 | tf_op jit(solution)/shard_map/normal/ppermute | solution.py:358
  74.8 16.1 %collective-permute-start.2 = (f32[24,256]{1,0:T(8,128)S(1)}, f32[24,256]{1,0:T(8,128)S(1)}, u32[]{:S(2)}, u32[]{:S(2)}) collective-permute-start(f32[24,256]{1,0:T(8,128)S(1)} %get-tuple-element.20), channel_id=1, source_target_pairs={{0,3},{1,0},{2,1},{3,2},{4,7},{5,4},{6,5},{7,6},{8,11},{9,8},{10,9... | collective-permute-start | bytes 73736 | tf_op jit(solution)/shard_map/normal/ppermute | solution.py:358
  90.9 10.9 %collective-permute-start.4 = (f32[4,24,256]{2,1,0:T(8,128)S(1)}, f32[4,24,256]{2,1,0:T(8,128)S(1)}, u32[]{:S(2)}, u32[]{:S(2)}) collective-permute-start(f32[4,24,256]{2,1,0:T(8,128)S(1)} %get-tuple-element.18), channel_id=1, source_target_pairs={{0,8},{1,9},{2,10},{3,11},{4,12},{5,13},{6,14},{7,15},{8,0},{9,1},... | collective-permute-start | bytes 294920 | tf_op jit(solution)/shard_map/normal/ppermute | solution.py:358
  98.8 5.7 %collective-permute-start.5 = (f32[4,24,256]{2,1,0:T(8,128)S(1)}, f32[4,24,256]{2,1,0:T(8,128)S(1)}, u32[]{:S(2)}, u32[]{:S(2)}) collective-permute-start(f32[4,24,256]{2,1,0:T(8,128)S(1)} %get-tuple-element.18), channel_id=1, source_target_pairs={{0,12},{1,13},{2,14},{3,15},{4,0},{5,1},{6,2},{7,3},{8,4},{9,5},{1... | collective-permute-start | bytes 294920 | tf_op jit(solution)/shard_map/normal/ppermute | solution.py:358
  100.8 5.8 %collective-permute-start.3 = (f32[4,24,256]{2,1,0:T(8,128)S(1)}, f32[4,24,256]{2,1,0:T(8,128)S(1)}, u32[]{:S(2)}, u32[]{:S(2)}) collective-permute-start(f32[4,24,256]{2,1,0:T(8,128)S(1)} %get-tuple-element.18), channel_id=1, source_target_pairs={{0,4},{1,5},{2,6},{3,7},{4,8},{5,9},{6,10},{7,11},{8,12},{9,13},{1... | collective-permute-start | bytes 294920 | tf_op jit(solution)/shard_map/normal/ppermute | solution.py:358

commit v9 on v5

--- a/solution.py
+++ b/solution.py
@@ -300,9 +300,7 @@
         middle = mode2_factor.shape[0] // 2
         up_4, down_4 = moved(up_3[:middle], 1), moved(down_3[middle:], -1)
         near_own = jnp.concatenate([mode2_factor, up_1, down_1, up_2, down_2], axis=0)
-        far_own = jnp.concatenate([up_3, down_3, up_4, down_4], axis=0)
         near_other = lax.ppermute(near_own, "row", twin)
-        far_other = lax.ppermute(far_own, "row", twin)
 
     with jax.named_scope("tables"):
         slot_index = jnp.arange(slot_count, dtype=jnp.int32)
@@ -331,6 +329,9 @@
                 is_far + 2 * is_other,
             ]
         ).astype(jnp.int32)
+        held_up_3, near_other, table = lax.optimization_barrier((up_3, near_other, table))
+        far_own = jnp.concatenate([held_up_3, down_3, up_4, down_4], axis=0)
+        far_other = lax.ppermute(far_own, "row", twin)
         slots = jnp.arange(SLOTS, dtype=jnp.float32)
         taken = chosen[:, None, :] * (rank[:, None, :] == slots[None, :, None])
         targets = jnp.sum(taken * (mode1_offset + 1).astype(jnp.float32), axis=2) - 1.0

time: 114 us -> 116 us (1.018)
  the two profiles are of different devices: /device:TPU:32 before, /device:TPU:1 now
where the time goes in v9:
time: 116 us
  starting transfers between devices  45 us (39%)
  Pallas kernels  32.8 us (28%)
  waiting for transfers between devices  21.8 us (19%)
  local copies, waits for them, and re-layouts  9.36 us (8%)
  matrix products  2.97 us (3%)
  other arithmetic  2.71 us (2%)
    pallas_call x1, Pallas kernels, invert(): pl.pallas_call(functools.partial(invert_kernel, block), out_shape=jax.Sha...  16 us
    ppermute x8, starting transfers between devices, moved(): return lax.ppermute(array, 'row', pairs)  15.1 us
    pallas_call x1, Pallas kernels, contract_tiles(): pl.pallas_call(contract_kernel, out_shape=jax.ShapeDtypeStruct((out_slots...  14.2 us
    all_to_all x1, waiting for transfers between devices, local(): lax.all_to_all(partials.reshape(n_col, SLOTS * tile_edge, rank_width), 'c...  11.4 us
    ppermute x8, waiting for transfers between devices, moved(): return lax.ppermute(array, 'row', pairs)  10.3 us
    all_to_all x1, starting transfers between devices, local(): lax.all_to_all(partials.reshape(n_col, SLOTS * tile_edge, rank_width), 'c...  7.33 us
    all_to_all x1, starting transfers between devices, local(): strips = lax.all_to_all(jnp.concatenate(strips, axis=1), 'col', 0, 0)  6.76 us
    all_to_all x1, starting transfers between devices, local(): lax.all_to_all(jnp.broadcast_to(sent[None], (n_col,) + sent.shape), 'col'...  6.7 us
  transfers between devices with their start and end apart: 14, of which 3 were waited for; matrix products, arithmetic and copies ran while one was open for 12% of the time, Pallas kernels for 26%

profile of v9, /device:TPU:1, one launch (start us, length us, event | category | flops | bytes accessed | tf_op | source)
XLA Modules:
  0.0 115.6 jit_solution(1736067788501420431)
XLA Ops:
  0.0 2.5 %collective-permute-start = (f32[256,256]{1,0:T(8,128)}, f32[256,256]{1,0:T(8,128)S(1)}, u32[]{:S(2)}, u32[]{:S(2)}) collective-permute-start(f32[256,256]{1,0:T(8,128)} %param.18), channel_id=1, source_target_pairs={{0,32},{16,48},{32,64},{48,80},{64,96},{80,112},{96,128},{112,144}... | collective-permute-start | bytes 786440 | tf_op jit(solution)/shard_map/gather_second/ppermute | solution.py:292
  2.5 4.0 %collective-permute-start.3 = (f32[256,256]{1,0:T(8,128)}, f32[256,256]{1,0:T(8,128)S(1)}, u32[]{:S(2)}, u32[]{:S(2)}) collective-permute-start(f32[256,256]{1,0:T(8,128)} %param.18), channel_id=1, source_target_pairs={{0,224},{16,240},{32,0},{48,16},{64,32},{80,48},{96,64},{112,80},{... | collective-permute-start | bytes 786440 | tf_op jit(solution)/shard_map/gather_second/ppermute | solution.py:292
  6.5 2.2 %fusion.18 = f32[256,256]{1,0:T(8,128)S(1)} fusion(f32[512,256]{1,0:T(8,128)} %param.19), kind=kOutput, calls=%fused_computation.67 | convolution fusion | flops 402653184 | bytes 786432 | tf_op jit(solution)/shard_map/normal/dot_general | solution.py:20
  8.7 0.6 fusion.17
  9.3 0.8 pad_maximum_fusion
  10.2 6.8 %all-to-all-start = ((f32[16,32,256]{2,1,0:T(8,128)}), f32[16,32,256]{2,1,0:T(8,128)S(1)}, u32[]{:S(2)}, u32[]{:S(2)}) async-start(f32[16,32,256]{2,1,0:T(8,128)} %pad_maximum_fusion), calls=%async_computation | async-start | bytes 1048576 | tf_op jit(solution)/shard_map/normal/all_to_all | solution.py:342
  16.9 0.0 copy-start.7
  16.9 0.0 copy-start.8
  17.0 0.0 copy-start.9
  17.0 0.0 copy-start.10
  17.0 0.0 copy-start.11
  17.0 0.0 collective-permute-done
  17.0 0.1 collective-permute-start.1
  17.8 0.0 collective-permute-done.3
  17.8 2.7 %collective-permute-start.4 = (f32[256,256]{1,0:T(8,128)S(1)}, f32[256,256]{1,0:T(8,128)}, u32[]{:S(2)}, u32[]{:S(2)}) collective-permute-start(f32[256,256]{1,0:T(8,128)S(1)} %collective-permute-done.3), channel_id=1, source_target_pairs={{0,224},{16,240},{32,0},{48,16},{64,32},{80,48},{96,64},{112,80},{... | collective-permute-start | bytes 786440 | tf_op jit(solution)/shard_map/gather_second/ppermute | solution.py:292
  20.6 4.3 %collective-permute-done.1 = f32[256,256]{1,0:T(8,128)S(1)} collective-permute-done((f32[256,256]{1,0:T(8,128)S(1)}, f32[256,256]{1,0:T(8,128)S(1)}, u32[]{:S(2)}, u32[]{:S(2)}) %collective-permute-start.1) | collective-permute-done | bytes 262176 | tf_op jit(solution)/shard_map/gather_second/ppermute | solution.py:292
  24.9 0.7 copy-done.6
  25.6 1.0 constant_dynamic-update-slice_fusion
  26.5 2.2 %collective-permute-start.5 = (f32[1280,256]{1,0:T(8,128)S(1)}, f32[1280,256]{1,0:T(8,128)S(1)}, u32[]{:S(2)}, u32[]{:S(2)}) collective-permute-start(f32[1280,256]{1,0:T(8,128)S(1)} %constant_dynamic-update-slice_fusion), channel_id=1, source_target_pairs={{0,16},{16,0},{32,48},{48,32},{64,80},{80,64},{96,112},{112,96},{1... | collective-permute-start | bytes 3932168 | tf_op jit(solution)/shard_map/gather_second/ppermute | solution.py:303
  28.8 0.1 select_reduce_fusion
  29.0 0.1 collective-permute-start.2
  29.1 2.9 %collective-permute-start.6 = (f32[256,256]{1,0:T(8,128)}, f32[256,256]{1,0:T(8,128)}, u32[]{:S(2)}, u32[]{:S(2)}) collective-permute-start(f32[256,256]{1,0:T(8,128)} %collective-permute-done.4), channel_id=1, source_target_pairs={{0,224},{16,240},{32,0},{48,16},{64,32},{80,48},{96,64},{112,80},{... | collective-permute-start | bytes 786440 | tf_op jit(solution)/shard_map/gather_second/ppermute | solution.py:292
  32.1 0.6 pad_add_fusion.table_ref
  32.7 0.7 broadcast_in_dim.41
  33.4 5.8 %all-to-all-start.1 = ((f32[16,16,256]{2,1,0:T(8,128)}), f32[16,16,256]{2,1,0:T(8,128)}, u32[]{:S(2)}, u32[]{:S(2)}) async-start(f32[16,16,256]{2,1,0:T(8,128)} %broadcast_in_dim.41), calls=%async_computation.1 | async-start | bytes 524288 | tf_op jit(solution)/shard_map/normal/all_to_all | solution.py:344
  39.3 1.5 %collective-permute-start.7 = (f32[128,256]{1,0:T(8,128)S(1)}, f32[128,256]{1,0:T(8,128)S(1)}, u32[]{:S(2)}, u32[]{:S(2)}) collective-permute-start(f32[128,256]{1,0:T(8,128)S(1)} %slice.43), channel_id=1, source_target_pairs={{0,32},{16,48},{32,64},{48,80},{64,96},{80,112},{96,128},{112,144}... | collective-permute-start | bytes 393224 | tf_op jit(solution)/shard_map/gather_second/ppermute | solution.py:292
  40.8 0.9 slice.44
  41.7 1.4 %collective-permute-start.8 = (f32[128,256]{1,0:T(8,128)S(1)}, f32[128,256]{1,0:T(8,128)S(1)}, u32[]{:S(2)}, u32[]{:S(2)}) collective-permute-start(f32[128,256]{1,0:T(8,128)S(1)} %slice.44), channel_id=1, source_target_pairs={{0,224},{16,240},{32,0},{48,16},{64,32},{80,48},{96,64},{112,80},{... | collective-permute-start | bytes 393224 | tf_op jit(solution)/shard_map/gather_second/ppermute | solution.py:292
  43.1 1.1 constant_dynamic-update-slice_fusion.8
  44.2 1.0 constant_dynamic-update-slice_fusion.7
  45.2 6.0 %collective-permute-done.7 = f32[128,256]{1,0:T(8,128)S(1)} collective-permute-done((f32[128,256]{1,0:T(8,128)S(1)}, f32[128,256]{1,0:T(8,128)S(1)}, u32[]{:S(2)}, u32[]{:S(2)}) %collective-permute-start.7) | collective-permute-done | bytes 131104 | tf_op jit(solution)/shard_map/gather_second/ppermute | solution.py:292
  51.3 1.0 collective-permute-start.9
  52.3 0.1 multiply_reduce_fusion
  52.4 0.1 copy.12
  52.5 0.1 sub.36
  52.6 1.0 reduce_sum.37
  53.6 0.8 broadcast_in_dim.42
  54.3 6.7 %all-to-all-start.2 = ((f32[16,24,256]{2,1,0:T(8,128)}), f32[16,24,256]{2,1,0:T(8,128)}, u32[]{:S(2)}, u32[]{:S(2)}) async-start(f32[16,24,256]{2,1,0:T(8,128)} %broadcast_in_dim.42), calls=%async_computation.2 | async-start | bytes 786432 | tf_op jit(solution)/shard_map/normal/all_to_all | solution.py:349
  61.1 0.9 copy-done.4
  62.0 14.2 %contract.1 = f32[64,32,256]{2,1,0:T(8,128)} custom-call(s32[4,48]{1,0:T(4,128)} %pad_add_fusion.table_ref, s32[1]{0:T(128)} %copy.20.count_ref, f32[48,32,1024]{2,1,0:T(8,128)} %tile_hbm.1, f32[16,32,256]{2,1,0:T(8,128)} %bitcast.53, f32[40,32,256]{2,1,0:T(8,128)} %bitcast.54, f32[24,32,256]{2,1,0:T(8,128)} %bitcast.55, f32[40,32,256]{2,1,0:T(8,128)} %bitcast.56, ...), custom_call_target="tpu_custom_call" | custom-call | flops 2415919104 | bytes 10000000 | tf_op jit(solution)/shard_map/contract/contract/pallas_call | solution.py:122
  76.2 7.3 %all-to-all-start.3 = ((f32[16,128,256]{2,1,0:T(8,128)}), f32[16,128,256]{2,1,0:T(8,128)S(1)}, u32[]{:S(2)}, u32[]{:S(2)}) async-start(f32[16,128,256]{2,1,0:T(8,128)} %bitcast.52), calls=%async_computation.3 | async-start | bytes 4194304 | tf_op jit(solution)/shard_map/exchange/all_to_all | solution.py:367
  83.5 0.9 slice.42
  84.4 0.1 convert_reduce_fusion
  84.5 0.1 convert_element_type.46.target_ref
  84.6 1.0 slice.45
  85.6 16.0 %invert.1.inverse_ref = f32[256,256]{1,0:T(8,128)S(1)} custom-call(f32[256,256]{1,0:T(8,128)S(1)} %bitcast.51), custom_call_target="tpu_custom_call" | custom-call | flops 201326592 | bytes 524288 | tf_op jit(solution)/shard_map/inverse/invert/pallas_call | solution.py:257
  101.6 11.4 %all-to-all-done.3 = f32[16,128,256]{2,1,0:T(8,128)S(1)} async-done(((f32[16,128,256]{2,1,0:T(8,128)}), f32[16,128,256]{2,1,0:T(8,128)S(1)}, u32[]{:S(2)}, u32[]{:S(2)}) %all-to-all-start.3) | async-done | bytes 2097184 | tf_op jit(solution)/shard_map/exchange/all_to_all | solution.py:367
  113.1 2.5 %combine.1 = f32[512,256]{1,0:T(8,128)} custom-call(s32[64]{0:T(128)S(1)} %convert_element_type.46.target_ref, f32[64,32,256]{2,1,0:T(8,128)S(1)} %bitcast.50, f32[256,256]{1,0:T(8,128)S(1)} %invert.1.inverse_ref), custom_call_target="tpu_custom_call" | custom-call | tf_op jit(solution)/shard_map/combine/combine/pallas_call | solution.py:168
  (43 shorter events, 0.3 us)
Async XLA Ops:
  0.0 8.7 %copy-start = (f32[256,256]{1,0:T(8,128)S(1)}, f32[256,256]{1,0:T(8,128)}, u32[]{:S(2)}) copy-start(f32[256,256]{1,0:T(8,128)} %param.18) | copy-start | bytes 786436
  0.0 17.0 %collective-permute-start = (f32[256,256]{1,0:T(8,128)}, f32[256,256]{1,0:T(8,128)S(1)}, u32[]{:S(2)}, u32[]{:S(2)}) collective-permute-start(f32[256,256]{1,0:T(8,128)} %param.18), channel_id=1, source_target_pairs={{0,32},{16,48},{32,64},{48,80},{64,96},{80,112},{96,128},{112,144}... | collective-permute-start | bytes 786440 | tf_op jit(solution)/shard_map/gather_second/ppermute | solution.py:292
  2.5 15.3 %collective-permute-start.3 = (f32[256,256]{1,0:T(8,128)}, f32[256,256]{1,0:T(8,128)S(1)}, u32[]{:S(2)}, u32[]{:S(2)}) collective-permute-start(f32[256,256]{1,0:T(8,128)} %param.18), channel_id=1, source_target_pairs={{0,224},{16,240},{32,0},{48,16},{64,32},{80,48},{96,64},{112,80},{... | collective-permute-start | bytes 786440 | tf_op jit(solution)/shard_map/gather_second/ppermute | solution.py:292
  10.2 22.5 %all-to-all-start = ((f32[16,32,256]{2,1,0:T(8,128)}), f32[16,32,256]{2,1,0:T(8,128)S(1)}, u32[]{:S(2)}, u32[]{:S(2)}) async-start(f32[16,32,256]{2,1,0:T(8,128)} %pad_maximum_fusion), calls=%async_computation | async-start | bytes 1048576 | tf_op jit(solution)/shard_map/normal/all_to_all | solution.py:342
  16.9 11.9 %copy-start.7 = (s32[48,1]{0,1:T(1,128)S(1)}, s32[48,1]{0,1:T(1,128)}, u32[]{:S(2)}) copy-start(s32[48,1]{0,1:T(1,128)} %param.13) | copy-start | bytes 580
  16.9 12.0 %copy-start.8 = (s32[48,1]{0,1:T(1,128)S(1)}, s32[48,1]{0,1:T(1,128)}, u32[]{:S(2)}) copy-start(s32[48,1]{0,1:T(1,128)} %param.15) | copy-start | bytes 580
  17.0 12.0 %copy-start.9 = (s32[48]{0:T(128)S(1)}, s32[48]{0:T(128)}, u32[]{:S(2)}) copy-start(s32[48]{0:T(128)} %param.17) | copy-start | bytes 580
  17.0 12.0 %copy-start.10 = (s32[48]{0:T(128)S(1)}, s32[48]{0:T(128)}, u32[]{:S(2)}) copy-start(s32[48]{0:T(128)} %param.16) | copy-start | bytes 580
  17.0 12.0 %copy-start.11 = (s32[48]{0:T(128)S(1)}, s32[48]{0:T(128)}, u32[]{:S(2)}) copy-start(s32[48]{0:T(128)} %param.14) | copy-start | bytes 580
  17.0 7.8 %collective-permute-start.1 = (f32[256,256]{1,0:T(8,128)S(1)}, f32[256,256]{1,0:T(8,128)S(1)}, u32[]{:S(2)}, u32[]{:S(2)}) collective-permute-start(f32[256,256]{1,0:T(8,128)S(1)} %collective-permute-done), channel_id=1, source_target_pairs={{0,32},{16,48},{32,64},{48,80},{64,96},{80,112},{96,128},{112,144}... | collective-permute-start | bytes 786440 | tf_op jit(solution)/shard_map/gather_second/ppermute | solution.py:292
  17.8 7.1 %collective-permute-start.4 = (f32[256,256]{1,0:T(8,128)S(1)}, f32[256,256]{1,0:T(8,128)}, u32[]{:S(2)}, u32[]{:S(2)}) collective-permute-start(f32[256,256]{1,0:T(8,128)S(1)} %collective-permute-done.3), channel_id=1, source_target_pairs={{0,224},{16,240},{32,0},{48,16},{64,32},{80,48},{96,64},{112,80},{... | collective-permute-start | bytes 786440 | tf_op jit(solution)/shard_map/gather_second/ppermute | solution.py:292
  24.9 0.7 copy-start.6
  26.5 18.6 %copy-start.1 = (f32[1280,256]{1,0:T(8,128)}, f32[1280,256]{1,0:T(8,128)S(1)}, u32[]{:S(2)}) copy-start(f32[1280,256]{1,0:T(8,128)S(1)} %constant_dynamic-update-slice_fusion) | copy-start | bytes 3932164
  26.5 16.5 %collective-permute-start.5 = (f32[1280,256]{1,0:T(8,128)S(1)}, f32[1280,256]{1,0:T(8,128)S(1)}, u32[]{:S(2)}, u32[]{:S(2)}) collective-permute-start(f32[1280,256]{1,0:T(8,128)S(1)} %constant_dynamic-update-slice_fusion), channel_id=1, source_target_pairs={{0,16},{16,0},{32,48},{48,32},{64,80},{80,64},{96,112},{112,96},{1... | collective-permute-start | bytes 3932168 | tf_op jit(solution)/shard_map/gather_second/ppermute | solution.py:303
  29.0 10.2 %collective-permute-start.2 = (f32[256,256]{1,0:T(8,128)}, f32[256,256]{1,0:T(8,128)S(1)}, u32[]{:S(2)}, u32[]{:S(2)}) collective-permute-start(f32[256,256]{1,0:T(8,128)} %copy-done.6), channel_id=1, source_target_pairs={{0,32},{16,48},{32,64},{48,80},{64,96},{80,112},{96,128},{112,144}... | collective-permute-start | bytes 786440 | tf_op jit(solution)/shard_map/gather_second/ppermute | solution.py:292
  29.1 11.6 %collective-permute-start.6 = (f32[256,256]{1,0:T(8,128)}, f32[256,256]{1,0:T(8,128)}, u32[]{:S(2)}, u32[]{:S(2)}) collective-permute-start(f32[256,256]{1,0:T(8,128)} %collective-permute-done.4), channel_id=1, source_target_pairs={{0,224},{16,240},{32,0},{48,16},{64,32},{80,48},{96,64},{112,80},{... | collective-permute-start | bytes 786440 | tf_op jit(solution)/shard_map/gather_second/ppermute | solution.py:292
  33.4 19.1 %all-to-all-start.1 = ((f32[16,16,256]{2,1,0:T(8,128)}), f32[16,16,256]{2,1,0:T(8,128)}, u32[]{:S(2)}, u32[]{:S(2)}) async-start(f32[16,16,256]{2,1,0:T(8,128)} %broadcast_in_dim.41), calls=%async_computation.1 | async-start | bytes 524288 | tf_op jit(solution)/shard_map/normal/all_to_all | solution.py:344
  39.3 3.8 %copy-start.5 = (f32[256,256]{1,0:T(8,128)}, f32[256,256]{1,0:T(8,128)S(1)}, u32[]{:S(2)}) copy-start(f32[256,256]{1,0:T(8,128)S(1)} %collective-permute-done.2) | copy-start | bytes 786436
  39.3 11.9 %collective-permute-start.7 = (f32[128,256]{1,0:T(8,128)S(1)}, f32[128,256]{1,0:T(8,128)S(1)}, u32[]{:S(2)}, u32[]{:S(2)}) collective-permute-start(f32[128,256]{1,0:T(8,128)S(1)} %slice.43), channel_id=1, source_target_pairs={{0,32},{16,48},{32,64},{48,80},{64,96},{80,112},{96,128},{112,144}... | collective-permute-start | bytes 393224 | tf_op jit(solution)/shard_map/gather_second/ppermute | solution.py:292
  41.7 9.5 %collective-permute-start.8 = (f32[128,256]{1,0:T(8,128)S(1)}, f32[128,256]{1,0:T(8,128)S(1)}, u32[]{:S(2)}, u32[]{:S(2)}) collective-permute-start(f32[128,256]{1,0:T(8,128)S(1)} %slice.44), channel_id=1, source_target_pairs={{0,224},{16,240},{32,0},{48,16},{64,32},{80,48},{96,64},{112,80},{... | collective-permute-start | bytes 393224 | tf_op jit(solution)/shard_map/gather_second/ppermute | solution.py:292
  43.1 11.3 %copy-start.3 = (f32[1280,256]{1,0:T(8,128)}, f32[1280,256]{1,0:T(8,128)S(1)}, u32[]{:S(2)}) copy-start(f32[1280,256]{1,0:T(8,128)S(1)} %collective-permute-done.5) | copy-start | bytes 3932164
  51.3 9.8 %copy-start.2 = (f32[768,256]{1,0:T(8,128)}, f32[768,256]{1,0:T(8,128)S(1)}, u32[]{:S(2)}) copy-start(f32[768,256]{1,0:T(8,128)S(1)} %constant_dynamic-update-slice_fusion.5) | copy-start | bytes 2359300
  51.3 9.8 %collective-permute-start.9 = (f32[768,256]{1,0:T(8,128)S(1)}, f32[768,256]{1,0:T(8,128)S(1)}, u32[]{:S(2)}, u32[]{:S(2)}) collective-permute-start(f32[768,256]{1,0:T(8,128)S(1)} %constant_dynamic-update-slice_fusion.5), channel_id=1, source_target_pairs={{0,16},{16,0},{32,48},{48,32},{64,80},{80,64},{96,112},{112,96},{1... | collective-permute-start | bytes 2359304 | tf_op jit(solution)/shard_map/tables/ppermute | solution.py:334
  54.3 21.8 %all-to-all-start.2 = ((f32[16,24,256]{2,1,0:T(8,128)}), f32[16,24,256]{2,1,0:T(8,128)}, u32[]{:S(2)}, u32[]{:S(2)}) async-start(f32[16,24,256]{2,1,0:T(8,128)} %broadcast_in_dim.42), calls=%async_computation.2 | async-start | bytes 786432 | tf_op jit(solution)/shard_map/normal/all_to_all | solution.py:349
  61.1 0.9 copy-start.4
  76.2 36.9 %all-to-all-start.3 = ((f32[16,128,256]{2,1,0:T(8,128)}), f32[16,128,256]{2,1,0:T(8,128)S(1)}, u32[]{:S(2)}, u32[]{:S(2)}) async-start(f32[16,128,256]{2,1,0:T(8,128)} %bitcast.52), calls=%async_computation.3 | async-start | bytes 4194304 | tf_op jit(solution)/shard_map/exchange/all_to_all | solution.py:367
